TPU v7x, 512 devices: a whole 4x8x8 slice. The times are simulated.
512 devices in a mesh: particle: 16 (over y_lo, z), space: 32 (over x, y_hi, core).
Axes of the slice: x: 4, y: 8 (y_hi: 4, y_lo: 2; y = y_hi * 2 + y_lo), z: 8, core: 2. Of those that a mesh axis runs over, the one named last changes fastest.
Arguments:
- stream: float32 [16, 2048, 2048], P('particle', 'space'), may hold values from -6 to 6
- depth_field: float32 [2048, 2048], P('space'), may hold values from 0.5 to 4
- obs_col: int32 [2048, 16], P('space'), may hold values from 0 to 2047
- obs_val: float32 [2048, 16], P('space'), may hold values from -6 to 6
- obs_weight: float32 [2048, 16], P('space'), may hold values from 0.1 to 1
- log_weight: float32 [16], P('particle'), may hold values from -24576 to 24576
- target: float32 [1], replicated, may hold values from 0 to 8192
- spectrum: float32 [512, 512], P('space'), may hold values from 1 to 10
- noise_coef: bfloat16 [16, 512, 512], P('particle', 'space'), may hold values from -6 to 6
- selection: int32 [2, 16], replicated, may hold values from 0 to 1
Outputs:
- analysis: float32 [16, 2048, 2048], P('particle', 'space')
- misfit_out: float32 [16], P('particle')
All inputs are finite; a program needn't handle non-finite values.
Results may differ from a plain program's by a relative error of at most 0.0003.
The roundings to bfloat16 on the way count: a program that leaves them out, or rounds other values in their place, can miss the bound.
Values may be sent and summed in bfloat16 or wider, within the bound.
No kernel may reach another device: no remote copies, remote signals or barrier semaphores. Data moves between devices by JAX's collectives and lax.ppermute only.
A program may use at most 64 MiB of HBM per device.

v0:
```python
import math

import jax
import jax.numpy as jnp
from jax import lax
from jax.sharding import PartitionSpec as P

ITERS = 2


STRETCH = 0.05
RELAX_RATE = 0.8
NOISE_AMP = 0.3


def extended(cells, sides, width):
    for axis, dim in sides:
        count = lax.axis_size(axis)
        ends = count - 1
        head = lax.slice_in_dim(cells, 0, width, axis=dim)
        tail = lax.slice_in_dim(cells, cells.shape[dim] - width, cells.shape[dim], axis=dim)
        cells = jnp.concatenate(
            [
                lax.ppermute(tail, axis, [(i, (i + 1) % count) for i in range(ends)]),
                cells,
                lax.ppermute(head, axis, [((i + 1) % count, i) for i in range(ends)]),
            ],
            axis=dim,
        )
    return cells


def swapped(value, axis, bit):
    mask = 2**bit
    pairs = [(source, source ^ mask) for source in range(lax.axis_size(axis))]
    return lax.ppermute(value, axis, pairs)


def tables(extent, half_modes):
    cell_index = jnp.arange(extent, dtype=jnp.int32)[:, None]
    frequency = jnp.arange(half_modes + 1, dtype=jnp.int32)[None, :]
    angles = (cell_index * frequency % extent).astype(jnp.float32) * (2.0 * math.pi / extent)
    cosines = jnp.cos(angles).astype(jnp.bfloat16)
    sines = jnp.sin(angles[:, 1:half_modes]).astype(jnp.bfloat16)
    return jnp.concatenate([cosines, sines], axis=1)


def compare_obs(grid_field, obs_col, obs_val, obs_weight):
    index_grid = jnp.broadcast_to(obs_col, grid_field.shape[:-1] + obs_col.shape[-1:])
    seen_vals = jnp.take_along_axis(grid_field, index_grid, axis=-1)
    mismatch_vals = obs_val - seen_vals
    return (mismatch_vals, 0.5 * jnp.sum(obs_weight * mismatch_vals * mismatch_vals, axis=(-2, -1)))


def spread_obs(weighted_miss, obs_col, columns):
    row_index = jnp.broadcast_to(
        jnp.arange(obs_col.shape[0], dtype=jnp.int32)[:, None], obs_col.shape
    )
    return (
        jnp.zeros((obs_col.shape[0], columns), jnp.float32)
        .at[row_index, obs_col]
        .add(weighted_miss)
    )


def operate_band(grid_field, screening):
    padded = extended(grid_field, (("space", 1),), 1)
    return (
        padded[:, 2:]
        + padded[:, :-2]
        + jnp.roll(grid_field, 1, axis=2)
        + jnp.roll(grid_field, -1, axis=2)
        - (4.0 + screening) * grid_field
    )


def relax_all(base, increment, depth_field):
    screening = STRETCH / depth_field
    pv_target = operate_band(base, screening) + increment
    relaxed = base + increment
    for sweep_index in range(ITERS):
        relaxed = relaxed + RELAX_RATE * (operate_band(relaxed, screening) - pv_target) / (
            4.0 + screening
        )
    return relaxed


def per_device(
    stream,
    depth_field,
    obs_col,
    obs_val,
    obs_weight,
    log_weight,
    target,
    spectrum,
    noise_coef,
    selection,
):
    members = stream.shape[0]
    band_rows = stream.shape[1]
    columns = stream.shape[2]
    n_modes = spectrum.shape[1]
    total_rows = band_rows * lax.axis_size("space")
    x_table = tables(columns, n_modes // 2)
    y_table = tables(total_rows, n_modes // 2)
    norm_factor = 4.0 / (columns * total_rows)
    mismatch_vals, misfit_part = compare_obs(stream, obs_col, obs_val, obs_weight)
    misfit = lax.psum(misfit_part, "space")
    gradient = jax.vmap(lambda weighted_miss: spread_obs(weighted_miss, obs_col, columns))(
        obs_weight * mismatch_vals
    ).astype(jnp.bfloat16)
    row_modes = jnp.einsum(
        "prx,xk->pkr", gradient, x_table, preferred_element_type=jnp.float32
    ).astype(jnp.bfloat16)
    col_modes = lax.all_to_all(row_modes, "space", split_axis=1, concat_axis=2, tiled=True)
    coefficients = jnp.einsum("pky,ym->pkm", col_modes, y_table, preferred_element_type=jnp.float32)
    weighted = coefficients * (norm_factor * spectrum)
    energy_part = jnp.sum(coefficients * weighted, axis=(1, 2))
    energy = lax.psum(energy_part, "space")
    shaped = (jnp.sqrt(norm_factor * spectrum) * noise_coef.astype(jnp.float32)).astype(
        jnp.bfloat16
    )
    stacked = jnp.concatenate([weighted.astype(jnp.bfloat16), shaped], axis=0)
    inverted = jnp.einsum(
        "qkm,ym->qky", stacked, y_table, preferred_element_type=jnp.float32
    ).astype(jnp.bfloat16)
    band_modes = lax.all_to_all(inverted, "space", split_axis=2, concat_axis=1, tiled=True)
    pulled = jnp.einsum("qkr,xk->qrx", band_modes, x_table, preferred_element_type=jnp.float32)
    step_size = (misfit + log_weight - target[0]) / (energy + 1.0)
    increment = step_size[:, None, None] * pulled[:members] + NOISE_AMP * pulled[members:]
    island = lax.axis_index("particle")
    fields = relax_all(stream, increment, depth_field)
    for section_bit in range(selection.shape[0]):
        chosen = lax.dynamic_slice_in_dim(selection[section_bit], island * members, members)
        partner = swapped(fields, "particle", section_bit)
        fields = jnp.take(jnp.concatenate([fields, partner], axis=0), chosen, axis=0)
    final_miss, final_part = compare_obs(fields, obs_col, obs_val, obs_weight)
    misfit_out = lax.psum(final_part, "space")
    return (fields, misfit_out)


def solution(mesh):
    return jax.shard_map(
        per_device,
        mesh=mesh,
        in_specs=(
            P("particle", "space", None),
            P("space", None),
            P("space", None),
            P("space", None),
            P("space", None),
            P("particle"),
            P(),
            P("space", None),
            P("particle", "space", None),
            P(),
        ),
        out_specs=(P("particle", "space", None), P("particle")),
        check_vma=False,
    )
```

profile of v0, /device:TPU:1, one launch (start us, length us, event | category | flops | bytes accessed | tf_op | source)
XLA Modules:
  0.0 302.5 jit_solution(11489714073195342933)
XLA Ops:
  0.6 0.8 copy.22
  1.5 0.7 fusion.46
  2.2 3.2 %fusion.2 = f32[2048,257]{1,0:T(8,128)} fusion(), kind=kLoop, calls=%fused_computation.8 | loop fusion | flops 7368704 | bytes 2105344 | tf_op jit(solution)/shard_map/mul | solution.py:42
  5.3 11.8 %cosine_convert_fusion = bf16[2048,257]{1,0:T(8,128)(2,1)S(1)} fusion(), kind=kLoop, calls=%fused_computation.9 | loop fusion | flops 7895040 | bytes 1052672 | tf_op jit(solution)/shard_map/convert_element_type | solution.py:43
  17.1 0.1 reshape.159
  17.2 0.0 copy-start.8
  17.3 8.6 %gather_fusion = f32[1024]{0:T(1024)S(1)} fusion(f32[64,2048]{1,0:T(8,128)S(1)} %bitcast.84, s32[1024]{0:T(1024)S(1)} %reshape.159), kind=kCustom, calls=%fused_computation.clone | custom fusion | bytes 16384 | tf_op jit(solution)/shard_map/jit(take_along_axis)/gather | solution.py:50
  25.9 0.1 reshape.162
  25.9 0.1 copy.20
  26.0 0.1 copy.21
  26.1 0.6 multiply_reduce_fusion.1
  26.7 0.1 reshape.138
  26.8 0.1 multiply_reduce_fusion.2
  26.9 0.1 and_reduce_fusion
  27.0 0.1 copy.23
  27.1 0.1 reshape.136
  27.2 6.1 %scatter_custom_fusion = f32[131072]{0:T(1024)S(1)} fusion(s32[1024]{0:T(1024)S(1)} %reshape.136, f32[1024]{0:T(1024)S(1)} %reshape.138, f32[]{:T(128)} %constant.36.clone.1), kind=kCustom, calls=%fused_computation.64 | custom fusion | flops 1024 | bytes 524292
  33.3 0.1 reshape.70
  33.4 8.4 %fusion.6 = bf16[2048,255]{1,0:T(8,128)(2,1)S(1)} fusion(f32[2048,257]{1,0:T(8,128)} %fusion.2), kind=kLoop, calls=%fused_computation.15 | loop fusion | flops 522240 | bytes 3133440 | tf_op jit(solution)/shard_map/convert_element_type | solution.py:44
  41.8 0.6 fusion.10
  42.4 0.2 copy.24
  42.6 0.5 broadcast.181
  43.1 2.1 reduce.8
  45.2 1.7 reshape.174
  46.9 11.2 %all-to-all-start = ((bf16[32,2,512]{2,1,0:T(2,128)(2,1)}), bf16[32,2,512]{2,1,0:T(2,128)(2,1)S(1)}, u32[]{:S(2)}, u32[]{:S(2)}) async-start(bf16[32,2,512]{2,1,0:T(2,128)(2,1)} %reshape.174), calls=%async_computation | async-start | bytes 131072 | tf_op jit(solution)/shard_map/all_to_all | solution.py:116
  58.1 1.4 fusion.44
  59.5 8.3 %all-to-all-done = bf16[32,2,512]{2,1,0:T(2,128)(2,1)S(1)} async-done(((bf16[32,2,512]{2,1,0:T(2,128)(2,1)}), bf16[32,2,512]{2,1,0:T(2,128)(2,1)S(1)}, u32[]{:S(2)}, u32[]{:S(2)}) %all-to-all-start) | async-done | bytes 65568 | tf_op jit(solution)/shard_map/all_to_all | solution.py:116
  67.8 0.1 reshape.175
  68.1 0.2 reshape.71
  68.3 1.9 multiply_reduce_fusion
  70.2 0.7 convolution_convert_fusion
  70.9 0.7 copy.26
  71.7 1.8 reshape.176
  73.5 3.9 %all-to-all-start.1 = ((bf16[32,2,1024]{2,1,0:T(2,128)(2,1)}), bf16[32,2,1024]{2,1,0:T(2,128)(2,1)S(1)}, u32[]{:S(2)}, u32[]{:S(2)}) async-start(bf16[32,2,1024]{2,1,0:T(2,128)(2,1)} %reshape.176), calls=%async_computation.1 | async-start | bytes 262144 | tf_op jit(solution)/shard_map/all_to_all | solution.py:128
  77.4 2.3 collective-permute-start.2
  79.7 4.2 %collective-permute-start.3 = (f32[1,1,2048]{2,1,0:T(1,128)S(1)}, f32[1,1,2048]{2,1,0:T(1,128)S(1)}, u32[]{:S(2)}, u32[]{:S(2)}) collective-permute-start(f32[1,1,2048]{2,1,0:T(1,128)S(1)} %get-tuple-element.28), channel_id=1, source_target_pairs={{0,1},{1,2},{2,3},{3,4},{4,5},{5,6},{6,7},{7,8},{8,9},{9,10},{10,1... | collective-permute-start | bytes 24584 | tf_op jit(solution)/shard_map/ppermute | solution.py:24
  85.8 70.6 %all-reduce = (f32[1]{0:T(128)}, f32[1]{0:T(128)}) all-reduce(f32[1]{0:T(128)} %bitcast.9, f32[1]{0:T(128)} %bitcast.13), channel_id=1, replica_groups=mesh['particle'=16,'space'=32] {'space'}, use_global_device_ids=true, to_apply=%region_1.3 | all-reduce | flops 2 | bytes 16 | tf_op jit(solution)/shard_map/psum | solution.py:109
  157.8 0.7 reshape.177
  158.5 1.2 copy.27
  159.7 2.3 fusion.7
  162.1 0.1 fusion.39
  162.2 0.4 fusion.55
  162.6 5.8 %collective-permute-start = (f32[1,1,2048]{2,1,0:T(1,128)S(1)}, f32[1,1,2048]{2,1,0:T(1,128)S(1)}, u32[]{:S(2)}, u32[]{:S(2)}) collective-permute-start(f32[1,1,2048]{2,1,0:T(1,128)S(1)} %get-tuple-element.37), channel_id=1, source_target_pairs={{1,0},{2,1},{3,2},{4,3},{5,4},{6,5},{7,6},{8,7},{9,8},{10,9},{11,1... | collective-permute-start | bytes 24584 | tf_op jit(solution)/shard_map/ppermute | solution.py:26
  168.4 1.9 collective-permute-start.1
  170.3 0.1 fusion.54
  170.4 1.0 collective-permute-done.1
  171.4 0.7 fusion.35
  172.1 0.2 fusion.50
  172.3 2.1 collective-permute-start.4
  174.4 4.6 %collective-permute-start.5 = (f32[1,1,2048]{2,1,0:T(1,128)S(1)}, f32[1,1,2048]{2,1,0:T(1,128)S(1)}, u32[]{:S(2)}, u32[]{:S(2)}) collective-permute-start(f32[1,1,2048]{2,1,0:T(1,128)S(1)} %get-tuple-element.26), channel_id=1, source_target_pairs={{0,1},{1,2},{2,3},{3,4},{4,5},{5,6},{6,7},{7,8},{8,9},{9,10},{10,1... | collective-permute-start | bytes 24584 | tf_op jit(solution)/shard_map/ppermute | solution.py:24
  179.0 0.1 fusion.51
  179.1 0.7 collective-permute-done.5
  179.8 0.4 fusion.22
  180.2 4.0 %collective-permute-start.6 = (f32[1,64,2048]{2,1,0:T(8,128)S(1)}, f32[1,64,2048]{2,1,0:T(8,128)S(1)}, u32[]{:S(2)}, u32[]{:S(2)}) collective-permute-start(f32[1,64,2048]{2,1,0:T(8,128)S(1)} %fusion.22), channel_id=1, source_target_pairs={{0,32},{32,0},{64,96},{96,64},{128,160},{160,128},{192,224},{224,1... | collective-permute-start | bytes 1572872 | tf_op jit(solution)/shard_map/ppermute | solution.py:36
  184.2 0.6 constant_dynamic-slice_fusion
  186.7 7.7 %collective-permute-done.6 = f32[1,64,2048]{2,1,0:T(8,128)S(1)} collective-permute-done((f32[1,64,2048]{2,1,0:T(8,128)S(1)}, f32[1,64,2048]{2,1,0:T(8,128)S(1)}, u32[]{:S(2)}, u32[]{:S(2)}) %collective-permute-start.6) | collective-permute-done | bytes 524320 | tf_op jit(solution)/shard_map/ppermute | solution.py:36
  194.4 0.1 fusion.14
  194.5 5.8 %collective-permute-start.7 = (f32[1,64,2048]{2,1,0:T(8,128)S(1)}, f32[1,64,2048]{2,1,0:T(8,128)S(1)}, u32[]{:S(2)}, u32[]{:S(2)}) collective-permute-start(f32[1,64,2048]{2,1,0:T(8,128)S(1)} %fusion.14), channel_id=1, source_target_pairs={{0,64},{32,96},{64,0},{96,32},{128,192},{160,224},{192,128},{224,1... | collective-permute-start | bytes 1572872 | tf_op jit(solution)/shard_map/ppermute | solution.py:36
  202.3 20.3 %collective-permute-done.7 = f32[1,64,2048]{2,1,0:T(8,128)S(1)} collective-permute-done((f32[1,64,2048]{2,1,0:T(8,128)S(1)}, f32[1,64,2048]{2,1,0:T(8,128)S(1)}, u32[]{:S(2)}, u32[]{:S(2)}) %collective-permute-start.7) | collective-permute-done | bytes 524320 | tf_op jit(solution)/shard_map/ppermute | solution.py:36
  222.6 0.1 fusion.12
  222.7 8.6 %gather_fusion.1 = f32[1024]{0:T(1024)S(1)} fusion(f32[64,2048]{1,0:T(8,128)S(1)} %bitcast.85, s32[1024]{0:T(1024)S(1)} %reshape.159), kind=kCustom, calls=%fused_computation.1.clone | custom fusion | bytes 16384 | tf_op jit(solution)/shard_map/jit(take_along_axis)/gather | solution.py:50
  231.3 0.1 reshape.170
  231.4 0.6 fusion.40
  232.7 69.9 %psum.23 = f32[1]{0:T(128)} all-reduce(f32[1]{0:T(128)} %bitcast.26), channel_id=1, replica_groups=mesh['particle'=16,'space'=32] {'space'}, use_global_device_ids=true, to_apply=%region_6.9 | all-reduce | flops 1 | bytes 8 | tf_op jit(solution)/shard_map/psum | solution.py:139
  (35 shorter events, 0.2 us)
Async XLA Ops:
  0.6 16.6 %copy-start = (f32[1,64,2048]{2,1,0:T(8,128)S(1)}, f32[1,64,2048]{2,1,0:T(8,128)}, u32[]{:S(2)}) copy-start(f32[1,64,2048]{2,1,0:T(8,128)} %param.14) | copy-start | bytes 1572868
  17.2 8.7 %copy-start.5 = (f32[64,16]{0,1:T(8,128)S(1)}, f32[64,16]{0,1:T(8,128)}, u32[]{:S(2)}) copy-start(f32[64,16]{0,1:T(8,128)} %param.18) | copy-start | bytes 12292
  17.2 8.8 %copy-start.6 = (f32[64,16]{0,1:T(8,128)S(1)}, f32[64,16]{0,1:T(8,128)}, u32[]{:S(2)}) copy-start(f32[64,16]{0,1:T(8,128)} %param.17) | copy-start | bytes 12292
  17.2 9.6 %copy-start.8 = (s32[2]{0:T(128)S(1)}, s32[2]{0:T(128)}, u32[]{:S(2)}) copy-start(s32[2]{0:T(128)} %constant.79) | copy-start | bytes 28
  17.3 9.7 %copy-start.9 = (s32[2]{0:T(128)S(1)}, s32[2]{0:T(128)}, u32[]{:S(2)}) copy-start(s32[2]{0:T(128)} %constant.82) | copy-start | bytes 28
  41.8 28.4 %copy-start.2 = (bf16[2048,255]{1,0:T(8,128)(2,1)}, bf16[2048,255]{1,0:T(8,128)(2,1)S(1)}, u32[]{:S(2)}) copy-start(bf16[2048,255]{1,0:T(8,128)(2,1)S(1)} %fusion.6) | copy-start | bytes 3133444
  46.9 21.0 %all-to-all-start = ((bf16[32,2,512]{2,1,0:T(2,128)(2,1)}), bf16[32,2,512]{2,1,0:T(2,128)(2,1)S(1)}, u32[]{:S(2)}, u32[]{:S(2)}) async-start(bf16[32,2,512]{2,1,0:T(2,128)(2,1)} %reshape.174), calls=%async_computation | async-start | bytes 131072 | tf_op jit(solution)/shard_map/all_to_all | solution.py:116
  68.0 2.2 copy-start.4
  73.5 84.3 %all-to-all-start.1 = ((bf16[32,2,1024]{2,1,0:T(2,128)(2,1)}), bf16[32,2,1024]{2,1,0:T(2,128)(2,1)S(1)}, u32[]{:S(2)}, u32[]{:S(2)}) async-start(bf16[32,2,1024]{2,1,0:T(2,128)(2,1)} %reshape.176), calls=%async_computation.1 | async-start | bytes 262144 | tf_op jit(solution)/shard_map/all_to_all | solution.py:128
  77.4 92.9 %collective-permute-start.2 = (f32[1,1,2048]{2,1,0:T(1,128)S(1)}, f32[1,1,2048]{2,1,0:T(1,128)S(1)}, u32[]{:S(2)}, u32[]{:S(2)}) collective-permute-start(f32[1,1,2048]{2,1,0:T(1,128)S(1)} %get-tuple-element.27), channel_id=1, source_target_pairs={{1,0},{2,1},{3,2},{4,3},{5,4},{6,5},{7,6},{8,7},{9,8},{10,9},{11,1... | collective-permute-start | bytes 24584 | tf_op jit(solution)/shard_map/ppermute | solution.py:26
  79.7 90.7 %collective-permute-start.3 = (f32[1,1,2048]{2,1,0:T(1,128)S(1)}, f32[1,1,2048]{2,1,0:T(1,128)S(1)}, u32[]{:S(2)}, u32[]{:S(2)}) collective-permute-start(f32[1,1,2048]{2,1,0:T(1,128)S(1)} %get-tuple-element.28), channel_id=1, source_target_pairs={{0,1},{1,2},{2,3},{3,4},{4,5},{5,6},{6,7},{7,8},{8,9},{9,10},{10,1... | collective-permute-start | bytes 24584 | tf_op jit(solution)/shard_map/ppermute | solution.py:24
  162.1 9.3 %copy-start.3 = (f32[64,2048]{1,0:T(8,128)S(1)}, f32[64,2048]{1,0:T(8,128)}, u32[]{:S(2)}) copy-start(f32[64,2048]{1,0:T(8,128)} %param.15) | copy-start | bytes 1572868
  162.6 7.8 %collective-permute-start = (f32[1,1,2048]{2,1,0:T(1,128)S(1)}, f32[1,1,2048]{2,1,0:T(1,128)S(1)}, u32[]{:S(2)}, u32[]{:S(2)}) collective-permute-start(f32[1,1,2048]{2,1,0:T(1,128)S(1)} %get-tuple-element.37), channel_id=1, source_target_pairs={{1,0},{2,1},{3,2},{4,3},{5,4},{6,5},{7,6},{8,7},{9,8},{10,9},{11,1... | collective-permute-start | bytes 24584 | tf_op jit(solution)/shard_map/ppermute | solution.py:26
  168.4 3.1 %collective-permute-start.1 = (f32[1,1,2048]{2,1,0:T(1,128)S(1)}, f32[1,1,2048]{2,1,0:T(1,128)S(1)}, u32[]{:S(2)}, u32[]{:S(2)}) collective-permute-start(f32[1,1,2048]{2,1,0:T(1,128)S(1)} %get-tuple-element.38), channel_id=1, source_target_pairs={{0,1},{1,2},{2,3},{3,4},{4,5},{5,6},{6,7},{7,8},{8,9},{9,10},{10,1... | collective-permute-start | bytes 24584 | tf_op jit(solution)/shard_map/ppermute | solution.py:24
  172.1 12.1 %copy-start.7 = (s32[2,16]{1,0:T(2,128)S(1)}, s32[2,16]{1,0:T(2,128)}, u32[]{:S(2)}) copy-start(s32[2,16]{1,0:T(2,128)} %param.23) | copy-start | bytes 388
  172.3 6.7 %collective-permute-start.4 = (f32[1,1,2048]{2,1,0:T(1,128)S(1)}, f32[1,1,2048]{2,1,0:T(1,128)S(1)}, u32[]{:S(2)}, u32[]{:S(2)}) collective-permute-start(f32[1,1,2048]{2,1,0:T(1,128)S(1)} %get-tuple-element.25), channel_id=1, source_target_pairs={{1,0},{2,1},{3,2},{4,3},{5,4},{6,5},{7,6},{8,7},{9,8},{10,9},{11,1... | collective-permute-start | bytes 24584 | tf_op jit(solution)/shard_map/ppermute | solution.py:26
  174.4 5.3 %collective-permute-start.5 = (f32[1,1,2048]{2,1,0:T(1,128)S(1)}, f32[1,1,2048]{2,1,0:T(1,128)S(1)}, u32[]{:S(2)}, u32[]{:S(2)}) collective-permute-start(f32[1,1,2048]{2,1,0:T(1,128)S(1)} %get-tuple-element.26), channel_id=1, source_target_pairs={{0,1},{1,2},{2,3},{3,4},{4,5},{5,6},{6,7},{7,8},{8,9},{9,10},{10,1... | collective-permute-start | bytes 24584 | tf_op jit(solution)/shard_map/ppermute | solution.py:24
  180.2 14.2 %collective-permute-start.6 = (f32[1,64,2048]{2,1,0:T(8,128)S(1)}, f32[1,64,2048]{2,1,0:T(8,128)S(1)}, u32[]{:S(2)}, u32[]{:S(2)}) collective-permute-start(f32[1,64,2048]{2,1,0:T(8,128)S(1)} %fusion.22), channel_id=1, source_target_pairs={{0,32},{32,0},{64,96},{96,64},{128,160},{160,128},{192,224},{224,1... | collective-permute-start | bytes 1572872 | tf_op jit(solution)/shard_map/ppermute | solution.py:36
  194.5 28.1 %collective-permute-start.7 = (f32[1,64,2048]{2,1,0:T(8,128)S(1)}, f32[1,64,2048]{2,1,0:T(8,128)S(1)}, u32[]{:S(2)}, u32[]{:S(2)}) collective-permute-start(f32[1,64,2048]{2,1,0:T(8,128)S(1)} %fusion.14), channel_id=1, source_target_pairs={{0,64},{32,96},{64,0},{96,32},{128,192},{160,224},{192,128},{224,1... | collective-permute-start | bytes 1572872 | tf_op jit(solution)/shard_map/ppermute | solution.py:36
  222.7 8.6 %copy-start.1 = (f32[1,64,2048]{2,1,0:T(8,128)}, f32[1,64,2048]{2,1,0:T(8,128)S(1)}, u32[]{:S(2)}) copy-start(f32[1,64,2048]{2,1,0:T(8,128)S(1)} %fusion.12) | copy-start | bytes 1572868
where the time goes:
time: 303 us
  blocking collectives  141 us (47%)
  starting transfers between devices  45.7 us (15%)
  waiting for transfers between devices  38.1 us (13%)
  other arithmetic  36.4 us (12%)
  local copies, waits for them, and re-layouts  27.4 us (9%)
  between operations  8.84 us (3%)
  matrix products  5.59 us (2%)
    psum x1, blocking collectives, per_device(): misfit = lax.psum(misfit_part, 'space')  70.6 us
    psum x1, blocking collectives, per_device(): misfit_out = lax.psum(final_part, 'space')  69.9 us
    ppermute x2, waiting for transfers between devices, swapped(): return lax.ppermute(value, axis, pairs)  28 us
    gather x5, local copies, waits for them, and re-layouts, compare_obs(): seen_vals = jnp.take_along_axis(grid_field, index_grid, axis=-1)  17.4 us
    convert_element_type x1, other arithmetic, tables(): cosines = jnp.cos(angles).astype(jnp.bfloat16)  11.8 us
    all_to_all x1, starting transfers between devices, per_device(): lax.all_to_all(row_modes, 'space', split_axis=1, concat_axis=2, tiled=True)  11.2 us
    ppermute x3, starting transfers between devices, extended(): lax.ppermute(tail, axis, [(i, (i + 1) % count) for i in range(ends)])  10.7 us
    ppermute x3, starting transfers between devices, extended(): lax.ppermute(head, axis, [((i + 1) % count, i) for i in range(ends)])  10.1 us
  transfers between devices with their start and end apart: 10, of which 5 were waited for; matrix products, arithmetic and copies ran while one was open for 2% of the time, Pallas kernels for 0%

commit v1 on v0

v1 whole, which is shorter than its diff:
```python
import math

import jax
import jax.numpy as jnp
import ml_dtypes
import numpy as np
from jax import lax
from jax.experimental import pallas as pl
from jax.experimental.pallas import tpu as pltpu
from jax.sharding import PartitionSpec as P

STRETCH = 0.05
RELAX_RATE = 0.8
NOISE_AMP = 0.3
LANES = 128
GROUP = 4
VMEM_LIMIT = 48 * 1024 * 1024


def table(extent, half_modes):
    cell = np.arange(extent, dtype=np.int64)[:, None]
    freq = np.arange(half_modes + 1, dtype=np.int64)[None, :]
    angles = (cell * freq % extent).astype(np.float64) * (2.0 * math.pi / extent)
    return np.concatenate([np.cos(angles), np.sin(angles[:, 1:half_modes])], axis=1).astype(
        ml_dtypes.bfloat16
    )


def halo_table(y_table, bands):
    rows = y_table.shape[0]
    width = rows // bands
    out = np.zeros((bands, 2, 4, y_table.shape[1]), dtype=y_table.dtype)
    for band in range(bands):
        for at, row in enumerate((-2, -1, width, width + 1)):
            source = band * width + row
            if 0 <= source < rows:
                out[band, :, at] = y_table[source]
    return out.reshape(bands * 8, y_table.shape[1])


def pack(values):
    rows, per_row = values.shape
    return values.reshape(rows // 8, 8, per_row).transpose(1, 0, 2).reshape(8, rows // 8 * per_row)


def lane_iota():
    return lax.broadcasted_iota(jnp.int32, (8, LANES), 1)


def split3(value):
    high = value.astype(jnp.bfloat16).astype(jnp.float32)
    rest = value - high
    mid = rest.astype(jnp.bfloat16).astype(jnp.float32)
    return high, mid, rest - mid


def source_slot(sel_ref, meta_ref):
    slot = meta_ref[0]
    one = jnp.where(sel_ref[1, slot] < 1, slot, slot ^ 2)
    return jnp.where(sel_ref[0, one] < 1, one, one ^ 1)


def fill_cols(col_ref, col_scr):
    per_row, rows = col_ref.shape
    col_scr[:, 0:per_row] = col_ref[...].T


def gather_rows(field_ref, col_scr, seen_scr, per_row):
    rows, columns = field_ref.shape
    lane = lane_iota()

    def one_group(group, carry):
        at = pl.multiple_of(group * 8, 8)
        cols = col_scr[pl.ds(at, 8), :]
        high, low = cols >> 7, cols & 127
        seen = jnp.zeros((8, LANES), jnp.float32)
        for j in range(per_row):
            high_j = jnp.broadcast_to(high[:, j : j + 1], (8, LANES))
            low_j = jnp.broadcast_to(low[:, j : j + 1], (8, LANES))
            picked = field_ref[pl.ds(at, 8), 0:LANES]
            for chunk in range(1, columns // LANES):
                picked = jnp.where(
                    high_j == chunk,
                    field_ref[pl.ds(at, 8), chunk * LANES : (chunk + 1) * LANES],
                    picked,
                )
            value = jnp.sum(jnp.where(lane == low_j, picked, 0.0), axis=1, keepdims=True)
            seen = jnp.where(lane == j, value, seen)
        seen_scr[pl.ds(at, 8), :] = seen
        return carry

    lax.fori_loop(0, rows // 8, one_group, 0)


def packed(scr, per_row):
    groups = scr.shape[0] // 8
    lane = lane_iota()
    out = scr[0:8, :]
    for group in range(1, groups):
        rolled = pltpu.roll(scr[group * 8 : group * 8 + 8, :], group * per_row, axis=1)
        out = jnp.where(lane // per_row == group, rolled, out)
    return out


def observe_kernel(lw_ref, col_ref, stream_ref, out_ref, col_scr, seen_scr):
    per_row = col_ref.shape[0]
    fill_cols(col_ref, col_scr)
    gather_rows(stream_ref, col_scr, seen_scr, per_row)
    seen = packed(seen_scr, per_row)
    weight = jnp.full((8, LANES), lw_ref[0], jnp.float32)
    for peer in range(GROUP):
        out_ref[peer, 0:8, :] = seen
        out_ref[peer, 8:16, :] = weight


def gradient_kernel(
    meta_ref, sel_ref, col_ref, val_ref, wgt_ref, seen_ref, tt_ref, send_ref, miss_ref, part_ref,
    col_scr, wm_scr, grad_scr,
):
    per_row, rows = col_ref.shape
    columns = tt_ref.shape[1]
    position = source_slot(sel_ref, meta_ref) % GROUP
    fill_cols(col_ref, col_scr)
    both = seen_ref[position]
    mismatch = val_ref[...] - both[0:8]
    weighted = wgt_ref[...] * mismatch
    miss_ref[0:8, :] = mismatch
    miss_ref[8:16, :] = both[8:16]
    part_ref[...] = jnp.full((8, LANES), 0.5 * jnp.sum(weighted * mismatch), jnp.float32)
    for group in range(rows // 8):
        shift = (LANES - group * per_row) % LANES
        wm_scr[group * 8 : group * 8 + 8, :] = (
            pltpu.roll(weighted, shift, axis=1) if shift else weighted
        )
    lane = lane_iota()

    def one_group(group, carry):
        at = pl.multiple_of(group * 8, 8)
        cols = col_scr[pl.ds(at, 8), :]
        wms = wm_scr[pl.ds(at, 8), :]
        col_j = [jnp.broadcast_to(cols[:, j : j + 1], (8, LANES)) for j in range(per_row)]
        wm_j = [jnp.broadcast_to(wms[:, j : j + 1], (8, LANES)) for j in range(per_row)]
        for chunk in range(columns // LANES):
            here = lane + chunk * LANES
            total = jnp.where(col_j[0] == here, wm_j[0], 0.0)
            for j in range(1, per_row):
                total = total + jnp.where(col_j[j] == here, wm_j[j], 0.0)
            grad_scr[pl.ds(at, 8), chunk * LANES : (chunk + 1) * LANES] = total
        return carry

    lax.fori_loop(0, rows // 8, one_group, 0)
    gradient = grad_scr[...].astype(jnp.bfloat16)
    modes = lax.dot_general(
        tt_ref[...], gradient, (((1,), (1,)), ((), ())), preferred_element_type=jnp.float32
    )
    bands = send_ref.shape[0]
    split = modes.reshape(bands, 2, 8, rows)
    send_ref[...] = jnp.concatenate([split[:, 0], split[:, 1]], axis=2).astype(jnp.bfloat16)


def spectral_kernel(
    meta_ref, sel_ref, modes_ref, noise_ref, spec_ref, part_ref, tt_ref, ht_ref, send_ref,
):
    bands = modes_ref.shape[0]
    half = LANES // 2
    modes_here, n_modes = spec_ref.shape
    rows = tt_ref.shape[1]
    norm_factor = 4.0 / (rows * rows)
    position = source_slot(sel_ref, meta_ref) % GROUP
    me = meta_ref[1] % 8
    lane = lane_iota()
    low = lane < half
    tops, bottoms = [], []
    for pair in range(bands // 2):
        even = modes_ref[2 * pair].astype(jnp.float32)
        odd = modes_ref[2 * pair + 1].astype(jnp.float32)
        tops.append(jnp.where(low, even, pltpu.roll(odd, half, axis=1)))
        bottoms.append(jnp.where(low, pltpu.roll(even, half, axis=1), odd))
    columns = jnp.concatenate(
        [jnp.concatenate(tops, axis=1), jnp.concatenate(bottoms, axis=1)], axis=0
    ).astype(jnp.bfloat16)
    coefficients = lax.dot_general(
        columns, tt_ref[...], (((1,), (1,)), ((), ())), preferred_element_type=jnp.float32
    )
    scaled = norm_factor * spec_ref[...]
    weighted = coefficients * scaled
    energy = jnp.sum(coefficients * weighted)
    shaped = (jnp.sqrt(scaled) * noise_ref[position].astype(jnp.float32)).astype(jnp.bfloat16)
    weighted = weighted.astype(jnp.bfloat16)
    stacked = jnp.concatenate([weighted, shaped], axis=0)
    inverted = jnp.dot(stacked, tt_ref[...], preferred_element_type=jnp.float32)
    low16 = lax.broadcasted_iota(jnp.int32, (modes_here, LANES), 1) < half
    for pair in range(bands // 2):
        first = inverted[0:modes_here, pair * LANES : (pair + 1) * LANES]
        second = inverted[modes_here:, pair * LANES : (pair + 1) * LANES]
        send_ref[2 * pair, 0:modes_here, :] = jnp.where(
            low16, first, pltpu.roll(second, half, axis=1)
        ).astype(jnp.bfloat16)
        send_ref[2 * pair + 1, 0:modes_here, :] = jnp.where(
            low16, pltpu.roll(first, half, axis=1), second
        ).astype(jnp.bfloat16)
    halo = lax.dot_general(
        ht_ref[...], stacked, (((1,), (1,)), ((), ())), preferred_element_type=jnp.float32
    )
    halo = halo.reshape(bands, 8, 2 * modes_here)
    row8 = lax.broadcasted_iota(jnp.int32, (bands, 8, LANES), 1)
    lane8 = lax.broadcasted_iota(jnp.int32, (bands, 8, LANES), 2)
    wide = jnp.concatenate([halo, jnp.zeros((bands, 8, LANES - 2 * modes_here), jnp.float32)], axis=2)
    wide = wide.reshape(bands * 8, LANES)
    at = me * modes_here
    as_first = pltpu.roll(wide, at, axis=1).reshape(bands, 8, LANES)
    as_second = pltpu.roll(wide, (at + LANES - modes_here) % LANES, axis=1).reshape(bands, 8, LANES)
    placed = jnp.where(row8 < 4, as_first, as_second)
    pieces = jnp.zeros((8, LANES), jnp.float32)
    row = lax.broadcasted_iota(jnp.int32, (8, LANES), 0)
    energy = jnp.full((8, LANES), energy, jnp.float32)
    for at_row, piece in enumerate(split3(part_ref[...]) + split3(energy)):
        pieces = jnp.where(row == at_row, piece, pieces)
    pieces = jnp.broadcast_to(pieces[None], (bands, 8, LANES))
    mine = lane8 // modes_here == me
    scalar_at = lane8 == ((me + 1) % 8) * modes_here
    tail = jnp.where(mine, placed, jnp.where(scalar_at, pieces, 0.0))
    send_ref[:, modes_here:, :] = tail.astype(jnp.bfloat16)


def relax_kernel(
    target_ref, col_ref, wgt_ref, miss_ref, rate_ref, modes_ref, tt_ref, field_ref, part_ref,
    col_scr, seen_scr, inc_scr, one_scr,
):
    per_row, rows = col_ref.shape
    bands, _, _ = modes_ref.shape
    n_modes, columns = tt_ref.shape
    modes_here = n_modes // bands
    fill_cols(col_ref, col_scr)
    lane = lane_iota()
    quads, scalars = [], jnp.zeros((8, LANES), jnp.float32)
    for quad in range(bands // 8):
        total = jnp.zeros((8, LANES), jnp.float32)
        for at in range(8):
            tail = modes_ref[quad * 8 + at, modes_here:, :].astype(jnp.float32)
            window = lane // modes_here
            total = jnp.where(window == at, tail, total)
            scalars = scalars + jnp.where(window == (at + 1) % 8, tail, 0.0)
        quads.append(total)
    halo = jnp.concatenate(quads, axis=1)
    row = lax.broadcasted_iota(jnp.int32, (8, LANES), 0)
    misfit = jnp.sum(jnp.where(row < 3, scalars, 0.0))
    energy = jnp.sum(jnp.where((row >= 3) & (row < 6), scalars, 0.0))
    weight = jnp.max(miss_ref[8:16, :])
    misfit_v = jnp.full((8, LANES), misfit + weight - target_ref[0], jnp.float32)
    step = (misfit_v / jnp.full((8, LANES), energy + 1.0, jnp.float32))[0:1, 0:1]
    main = modes_ref[:, 0:modes_here, :].reshape(n_modes, LANES)
    left = jnp.concatenate([main.astype(jnp.float32).T, halo], axis=0).astype(jnp.bfloat16)
    pulled = jnp.dot(left, tt_ref[...], preferred_element_type=jnp.float32)
    inc_scr[8 : 8 + rows, :] = step * pulled[0:rows] + NOISE_AMP * pulled[rows : 2 * rows]
    edge = step * pulled[2 * rows : 2 * rows + 4] + NOISE_AMP * pulled[2 * rows + 4 : 2 * rows + 8]
    inc_scr[6:8, :] = edge[0:2]
    inc_scr[8 + rows : 10 + rows, :] = edge[2:4]

    def beside(values):
        return pltpu.roll(values, 1, axis=1) + pltpu.roll(values, columns - 1, axis=1)

    here = inc_scr[7 : 9 + rows, :]
    around = inc_scr[6 : 8 + rows, :] + inc_scr[8 : 10 + rows, :] + beside(here)
    one_scr[7 : 9 + rows, :] = (1.0 - RELAX_RATE) * here + rate_ref[7 : 9 + rows, :] * (around - here)
    here = one_scr[8 : 8 + rows, :]
    around = one_scr[7 : 7 + rows, :] + one_scr[9 : 9 + rows, :] + beside(here)
    field_ref[...] = (1.0 - RELAX_RATE) * here + rate_ref[8 : 8 + rows, :] * (
        around - inc_scr[8 : 8 + rows, :]
    )
    gather_rows(field_ref, col_scr, seen_scr, per_row)
    left_over = miss_ref[0:8, :] - packed(seen_scr, per_row)
    part = 0.5 * jnp.sum(wgt_ref[...] * left_over * left_over)
    part_ref[...] = jnp.full(part_ref.shape, part, jnp.float32)


SMEM = pl.BlockSpec(memory_space=pltpu.SMEM)
VMEM = pl.BlockSpec(memory_space=pltpu.VMEM)


def call(kernel, in_specs, out_shape, scratch, name):
    return pl.pallas_call(
        kernel,
        in_specs=in_specs,
        out_specs=jax.tree.map(lambda _: VMEM, out_shape),
        out_shape=out_shape,
        scratch_shapes=scratch,
        name=name,
        compiler_params=pltpu.CompilerParams(vmem_limit_bytes=VMEM_LIMIT),
    )


def swapped(value, axis, bit):
    mask = 2**bit
    pairs = [(source, source ^ mask) for source in range(lax.axis_size(axis))]
    return lax.ppermute(value, axis, pairs)


def per_device(
    stream, depth_field, obs_col, obs_val, obs_weight, log_weight, target, spectrum, noise_coef,
    selection,
):
    _, rows, columns = stream.shape
    per_row = obs_col.shape[1]
    modes_here, n_modes = spectrum.shape
    bands = lax.axis_size("space")
    particles = lax.axis_size("particle")
    y_table = table(rows * bands, n_modes // 2)
    tt_all = jnp.asarray(np.ascontiguousarray(y_table.T))
    ht_all = jnp.asarray(halo_table(y_table, bands))
    f32, bf16 = jnp.float32, jnp.bfloat16
    shape = jax.ShapeDtypeStruct
    groups = [[g * GROUP + i for i in range(GROUP)] for g in range(particles // GROUP)]
    slot = lax.axis_index("particle")
    meta = jnp.stack([slot, lax.axis_index("space")]).astype(jnp.int32)
    own = stream[0]
    col_t = obs_col.T
    tile = pltpu.VMEM((rows, LANES), f32)
    col_tile = pltpu.VMEM((rows, LANES), jnp.int32)

    seen = call(
        observe_kernel, [SMEM, VMEM, VMEM], shape((GROUP, 16, LANES), f32), [col_tile, tile], "observe"
    )(log_weight, col_t, own)
    seen = lax.all_to_all(seen, "particle", 0, 0, axis_index_groups=groups, tiled=True)
    noise = jnp.broadcast_to(noise_coef, (GROUP,) + noise_coef.shape[1:])
    noise = lax.all_to_all(noise, "particle", 0, 0, axis_index_groups=groups, tiled=True)

    weight_p = pack(obs_weight)
    send, miss, part = call(
        gradient_kernel,
        [SMEM, SMEM, VMEM, VMEM, VMEM, VMEM, VMEM],
        (shape((bands, 8, LANES), bf16), shape((16, LANES), f32), shape((8, LANES), f32)),
        [col_tile, tile, pltpu.VMEM((rows, columns), f32)],
        "gradient",
    )(meta, selection, col_t, pack(obs_val), weight_p, seen, tt_all)
    col_modes = lax.all_to_all(send, "space", 0, 0, tiled=True)

    send = call(
        spectral_kernel,
        [SMEM, SMEM, VMEM, VMEM, VMEM, VMEM, VMEM, VMEM],
        shape((bands, modes_here + 8, LANES), bf16),
        [],
        "spectral",
    )(meta, selection, col_modes, noise, spectrum, part, tt_all, ht_all)
    band_modes = lax.all_to_all(send, "space", 0, 0, tiled=True)

    above = lax.ppermute(depth_field[-1:], "space", [(i, i + 1) for i in range(bands - 1)])
    below = lax.ppermute(depth_field[:1], "space", [(i + 1, i) for i in range(bands - 1)])
    blank = jnp.zeros((7, columns), f32)
    depth = jnp.concatenate([blank, above, depth_field, below, blank], axis=0)
    rate = RELAX_RATE * depth / (4.0 * depth + STRETCH)

    fields = own
    for section in range(2):
        chosen = selection[section, slot]
        fields = jnp.where(chosen < 1, fields, swapped(fields, "particle", section))

    field, part = call(
        relax_kernel,
        [SMEM, VMEM, VMEM, VMEM, VMEM, VMEM, VMEM],
        (shape((rows, columns), f32), shape((bands, 1, LANES), f32)),
        [col_tile, tile, pltpu.VMEM((rows + 16, columns), f32), pltpu.VMEM((rows + 16, columns), f32)],
        "relax",
    )(target, col_t, weight_p, miss, rate, band_modes, tt_all)
    parts = lax.all_to_all(part, "space", 0, 0, tiled=True)
    misfit_out = jnp.sum(parts[:, 0, 0:1], axis=0)
    return (fields + field)[None], misfit_out


def solution(mesh):
    return jax.shard_map(
        per_device,
        mesh=mesh,
        in_specs=(
            P("particle", "space", None),
            P("space", None),
            P("space", None),
            P("space", None),
            P("space", None),
            P("particle"),
            P(),
            P("space", None),
            P("particle", "space", None),
            P(),
        ),
        out_specs=(P("particle", "space", None), P("particle")),
        check_vma=False,
    )
```

time: 303 us -> 110 us (0.36)
  blocking collectives: 141 us -> 0 us
  other arithmetic: 36.4 us -> 4.69 us
  waiting for transfers between devices: 38.1 us -> 15.4 us
  Pallas kernels: 0 us -> 20.3 us
  local copies, waits for them, and re-layouts: 27.4 us -> 12.5 us
  starting transfers between devices: 45.7 us -> 52.6 us
  matrix products: 5.59 us -> 0 us
  between operations: 8.84 us -> 3.39 us
    psum x2 -> x0, blocking collectives: 141 us -> none  [the longest x1 70.6 us: per_device(): misfit = lax.psum(misfit_part, 'space')]
    ppermute x2, waiting for transfers between devices: 28 us -> 0.01 us  [swapped(): return lax.ppermute(value, axis, pairs)]
    all_to_all x2 -> x5, starting transfers between devices: 15.1 us -> 37.9 us  [the longest x1 12.1 us: per_device(): col_modes = lax.all_to_all(send, 'space', 0, 0, tiled=True)]
    convert_element_type x4 -> x0, other arithmetic: 21.6 us -> none  [the longest x1 11.8 us: tables(): cosines = jnp.cos(angles).astype(jnp.bfloat16)]
    pallas_call x0 -> x4, Pallas kernels: none -> 20.3 us  [the longest x1 7.49 us: per_device(): call(relax_kernel, [SMEM, VMEM, VMEM, VMEM, VMEM, VMEM, VMEM], (shape((ro...]
    gather x5 -> x0, local copies, waits for them, and re-layouts: 17.4 us -> none  [compare_obs(): seen_vals = jnp.take_along_axis(grid_field, index_grid, axis=-1)]
    ppermute x6 -> x2, starting transfers between devices: 20.8 us -> 6.36 us  [the longest x1 4.44 us: per_device(): lax.ppermute(depth_field[-1:], 'space', [(i, i + 1) for i in range(bands...]
    unnamed x5 -> x0, other arithmetic: 8.36 us -> none
  transfers between devices with their start and end apart: 10 -> 9, of which waited for: 5 -> 3; matrix products, arithmetic and copies ran while one was open for 2% -> 10% of each run, Pallas kernels for 0% -> 13%
where the time goes in v1:
time: 110 us; the launch traced here: 109 us
  starting transfers between devices  52.6 us (48%)
  Pallas kernels  20.3 us (18%)
  waiting for transfers between devices  15.4 us (14%)
  local copies, waits for them, and re-layouts  12.5 us (11%)
  other arithmetic  4.69 us (4%)
  between operations  3.39 us (3%)
    all_to_all x1, starting transfers between devices, per_device(): col_modes = lax.all_to_all(send, 'space', 0, 0, tiled=True)  12.1 us
    all_to_all x1, starting transfers between devices, per_device(): band_modes = lax.all_to_all(send, 'space', 0, 0, tiled=True)  9.28 us
    all_to_all x1, waiting for transfers between devices, per_device(): parts = lax.all_to_all(part, 'space', 0, 0, tiled=True)  8.7 us
    ppermute x2, starting transfers between devices, swapped(): return lax.ppermute(value, axis, pairs)  8.32 us
    all_to_all x1, starting transfers between devices, per_device(): lax.all_to_all(seen, 'particle', 0, 0, axis_index_groups=groups, tiled=True)  7.81 us
    pallas_call x1, Pallas kernels, per_device(): call(relax_kernel, [SMEM, VMEM, VMEM, VMEM, VMEM, VMEM, VMEM], (shape((ro...  7.49 us
    unnamed x24, local copies, waits for them, and re-layouts  6.29 us
    pallas_call x1, Pallas kernels, per_device(): call(observe_kernel, [SMEM, VMEM, VMEM], shape((GROUP, 16, LANES), f32),...  6.28 us
  transfers between devices with their start and end apart: 9, of which 3 were waited for; matrix products, arithmetic and copies ran while one was open for 10% of the time, Pallas kernels for 13%

profile of v1, /device:TPU:1, one launch (start us, length us, event | category | flops | bytes accessed | tf_op | source)
XLA Modules:
  0.0 108.8 jit_solution(1154494341855353253)
XLA Ops:
  0.6 0.0 copy-start.10
  1.3 0.0 copy-start.2
  1.3 1.0 copy-done.2
  2.3 0.0 copy-start.5
  2.3 0.7 copy-done.5
  3.0 6.3 %observe.1 = f32[4,16,128]{2,1,0:T(8,128)} custom-call(f32[1]{0:T(128)S(6)} %copy.20.lw_ref, s32[16,64]{1,0:T(8,128)S(1)} %bitcast.19, f32[64,2048]{1,0:T(8,128)S(1)} %bitcast.18), custom_call_target="tpu_custom_call" | custom-call | tf_op jit(solution)/shard_map/observe/pallas_call | solution.py:321
  9.3 7.8 %all-to-all-start = ((f32[4,16,128]{2,1,0:T(8,128)}), f32[4,16,128]{2,1,0:T(8,128)S(1)}, u32[]{:S(2)}, u32[]{:S(2)}) async-start(f32[4,16,128]{2,1,0:T(8,128)} %observe.1), calls=%async_computation | async-start | bytes 65536 | tf_op jit(solution)/shard_map/all_to_all | solution.py:324
  17.1 3.4 %collective-permute-start = (f32[64,2048]{1,0:T(8,128)}, f32[64,2048]{1,0:T(8,128)}, u32[]{:S(2)}, u32[]{:S(2)}) collective-permute-start(f32[64,2048]{1,0:T(8,128)} %bitcast.17), channel_id=1, source_target_pairs={{0,32},{32,0},{64,96},{96,64},{128,160},{160,128},{192,224},{224,1... | collective-permute-start | bytes 1572872 | tf_op jit(solution)/shard_map/ppermute | solution.py:296
  20.5 0.8 copy.16
  21.3 0.0 copy-start.4
  21.3 0.0 copy-start.8
  21.3 0.1 reshape.22.wgt_ref
  21.4 0.8 copy.18
  22.2 0.1 reshape.24.val_ref
  22.3 0.0 all-to-all-done.seen_ref
  22.3 1.4 %broadcast_in_dim.15 = bf16[4,16,512]{2,1,0:T(8,128)(2,1)} broadcast(bf16[16,512]{1,0:T(8,128)(2,1)} %bitcast.24), dimensions={1,2} | broadcast | bytes 81920 | tf_op jit(solution)/shard_map/broadcast_in_dim | solution.py:325
  23.6 3.4 %all-to-all-start.2 = ((bf16[4,16,512]{2,1,0:T(8,128)(2,1)}), bf16[4,16,512]{2,1,0:T(8,128)(2,1)S(1)}, u32[]{:S(2)}, u32[]{:S(2)}) async-start(bf16[4,16,512]{2,1,0:T(8,128)(2,1)} %broadcast_in_dim.15), calls=%async_computation.2 | async-start | bytes 131072 | tf_op jit(solution)/shard_map/all_to_all | solution.py:326
  27.0 0.1 pad_add_fusion.meta_ref
  27.1 0.0 copy-start
  27.1 1.6 %copy-done = bf16[512,2048]{1,0:T(8,128)(2,1)S(1)} copy-done((bf16[512,2048]{1,0:T(8,128)(2,1)S(1)}, bf16[512,2048]{1,0:T(8,128)(2,1)}, u32[]{:S(2)}) %copy-start) | copy-done | bytes 2097176
  28.6 0.0 copy-start.6
  28.6 0.7 copy-done.6
  29.3 0.0 copy-start.9
  29.3 0.7 copy-done.9
  30.0 0.0 copy-start.1
  30.0 3.9 %gradient.1 = (bf16[32,8,128]{2,1,0:T(8,128)(2,1)}, f32[16,128]{1,0:T(8,128)S(1)}, f32[8,128]{1,0:T(8,128)S(1)}) custom-call(s32[2]{0:T(128)S(1)} %pad_add_fusion.meta_ref, s32[2,16]{1,0:T(2,128)S(1)} %copy-done.9, s32[16,64]{1,0:T(8,128)S(1)} %bitcast.20, f32[8,128]{1,0:T(8,128)S(1)} %reshape.24.val_ref, f32[8,128]{1,0:T(8,128)S(1)} %reshape.22.wgt_ref, ...), custom_call_target="tpu_custom_call" | custom-call | tf_op jit(solution)/shard_map/gradient/pallas_call | solution.py:329
  33.9 0.0 all-to-all-done.2.noise_ref
  33.9 12.1 %all-to-all-start.1 = ((bf16[32,8,128]{2,1,0:T(8,128)(2,1)}), bf16[32,8,128]{2,1,0:T(8,128)(2,1)S(1)}, u32[]{:S(2)}, u32[]{:S(2)}) async-start(bf16[32,8,128]{2,1,0:T(8,128)(2,1)} %get-tuple-element.8), calls=%async_computation.1 | async-start | bytes 131072 | tf_op jit(solution)/shard_map/all_to_all | solution.py:336
  46.1 0.9 fusion
  47.0 4.4 %collective-permute-start.2 = (f32[1,2048]{1,0:T(1,128)S(1)}, f32[1,2048]{1,0:T(1,128)S(1)}, u32[]{:S(2)}, u32[]{:S(2)}) collective-permute-start(f32[1,2048]{1,0:T(1,128)S(1)} %get-tuple-element.13), channel_id=1, source_target_pairs={{0,1},{1,2},{2,3},{3,4},{4,5},{5,6},{6,7},{7,8},{8,9},{9,10},{10,1... | collective-permute-start | bytes 24584 | tf_op jit(solution)/shard_map/ppermute | solution.py:347
  51.4 1.9 %collective-permute-start.3 = (f32[1,2048]{1,0:T(1,128)S(1)}, f32[1,2048]{1,0:T(1,128)S(1)}, u32[]{:S(2)}, u32[]{:S(2)}) collective-permute-start(f32[1,2048]{1,0:T(1,128)S(1)} %get-tuple-element.12), channel_id=1, source_target_pairs={{1,0},{2,1},{3,2},{4,3},{5,4},{6,5},{7,6},{8,7},{9,8},{10,9},{11,1... | collective-permute-start | bytes 24584 | tf_op jit(solution)/shard_map/ppermute | solution.py:348
  54.0 0.0 copy-done.10
  54.0 0.7 constant_dynamic-slice_fusion
  55.3 0.0 collective-permute-done.2
  55.3 2.0 %collective-permute-done.3 = f32[1,2048]{1,0:T(1,128)S(1)} collective-permute-done((f32[1,2048]{1,0:T(1,128)S(1)}, f32[1,2048]{1,0:T(1,128)S(1)}, u32[]{:S(2)}, u32[]{:S(2)}) %collective-permute-start.3) | collective-permute-done | bytes 8224 | tf_op jit(solution)/shard_map/ppermute | solution.py:348
  57.3 0.0 copy-start.3
  57.3 3.1 %concatenate.3 = f32[80,2048]{1,0:T(8,128)} concatenate(f32[7,2048]{1,0:T(8,128)S(1)} %broadcast_in_dim.13, f32[1,2048]{1,0:T(1,128)S(1)} %collective-permute-done.2, f32[64,2048]{1,0:T(8,128)} %param.13, f32[1,2048]{1,0:T(1,128)S(1)} %collective-permute-done.3, f32[7,2048]{1,0:T(8,128)S(1)} %broadcast_in_dim.13), dimensions={0} | concatenate | bytes 1310720 | tf_op jit(solution)/shard_map/concatenate | solution.py:350
  60.4 0.0 all-to-all-done.1.modes_ref
  60.4 0.0 copy-done.4
  60.4 0.0 copy-done.8
  60.4 0.0 copy-done.1
  60.4 2.6 %spectral.1 = bf16[32,24,128]{2,1,0:T(8,128)(2,1)} custom-call(s32[2]{0:T(128)S(1)} %pad_add_fusion.meta_ref, s32[2,16]{1,0:T(2,128)S(1)} %copy-done.10, bf16[32,8,128]{2,1,0:T(8,128)(2,1)S(1)} %all-to-all-done.1.modes_ref, bf16[4,16,512]{2,1,0:T(8,128)(2,1)S(1)} %all-to-all-done.2.noise_ref, f32[16,512]{1,0:T(8,128)S(1)} %copy-done.8, ...), custom_call_target="tpu_custom_call" | custom-call | tf_op jit(solution)/shard_map/spectral/pallas_call | solution.py:338
  63.0 0.0 copy-start.7
  63.0 9.3 %all-to-all-start.3 = ((bf16[32,24,128]{2,1,0:T(8,128)(2,1)}), bf16[32,24,128]{2,1,0:T(8,128)(2,1)S(1)}, u32[]{:S(2)}, u32[]{:S(2)}) async-start(bf16[32,24,128]{2,1,0:T(8,128)(2,1)} %spectral.1), calls=%async_computation.3 | async-start | bytes 393216 | tf_op jit(solution)/shard_map/all_to_all | solution.py:345
  72.3 0.0 collective-permute-done
  72.3 0.0 copy-done.3
  72.3 0.9 broadcast_select_fusion
  73.2 5.0 %collective-permute-start.1 = (f32[64,2048]{1,0:T(8,128)}, f32[64,2048]{1,0:T(8,128)}, u32[]{:S(2)}, u32[]{:S(2)}) collective-permute-start(f32[64,2048]{1,0:T(8,128)} %broadcast_select_fusion), channel_id=1, source_target_pairs={{0,64},{32,96},{64,0},{96,32},{128,192},{160,224},{192,128},{224,1... | collective-permute-start | bytes 1572872 | tf_op jit(solution)/shard_map/ppermute | solution.py:296
  78.1 1.2 %add_divide_fusion.rate_ref = f32[80,2048]{1,0:T(8,128)S(1)} fusion(f32[80,2048]{1,0:T(8,128)} %concatenate.3), kind=kLoop, calls=%fused_computation | loop fusion | flops 655360 | bytes 1310720 | tf_op jit(solution)/shard_map/div | solution.py:351
  79.3 4.7 %all-to-all-done.3.modes_ref = bf16[32,24,128]{2,1,0:T(8,128)(2,1)S(1)} async-done(((bf16[32,24,128]{2,1,0:T(8,128)(2,1)}), bf16[32,24,128]{2,1,0:T(8,128)(2,1)S(1)}, u32[]{:S(2)}, u32[]{:S(2)}) %all-to-all-start.3) | async-done | bytes 196640 | tf_op jit(solution)/shard_map/all_to_all | solution.py:345
  84.1 0.0 copy-done.7
  84.1 7.5 %relax.1 = (f32[64,2048]{1,0:T(8,128)S(1)}, f32[32,1,128]{2,1,0:T(1,128)}) custom-call(f32[1]{0:T(128)S(6)} %copy.21.target_ref, s32[16,64]{1,0:T(8,128)S(1)} %bitcast.21, f32[8,128]{1,0:T(8,128)S(1)} %reshape.22.wgt_ref, f32[16,128]{1,0:T(8,128)S(1)} %get-tuple-element.7.miss_ref, f32[80,2048]{1,0:T(8,128)S(1)} %add_divide_fusion.rate_ref, ...), custom_call_target="tpu_custom_call" | custom-call | tf_op jit(solution)/shard_map/relax/pallas_call | solution.py:358
  91.6 5.3 %all-to-all-start.4 = ((f32[32,1,128]{2,1,0:T(1,128)}), f32[32,1,128]{2,1,0:T(1,128)S(1)}, u32[]{:S(2)}, u32[]{:S(2)}) async-start(f32[32,1,128]{2,1,0:T(1,128)} %get-tuple-element.11), calls=%async_computation.4 | async-start | bytes 32768 | tf_op jit(solution)/shard_map/all_to_all | solution.py:365
  97.6 8.7 %all-to-all-done.4 = f32[32,1,128]{2,1,0:T(1,128)S(1)} async-done(((f32[32,1,128]{2,1,0:T(1,128)}), f32[32,1,128]{2,1,0:T(1,128)S(1)}, u32[]{:S(2)}, u32[]{:S(2)}) %all-to-all-start.4) | async-done | bytes 16416 | tf_op jit(solution)/shard_map/all_to_all | solution.py:365
  106.3 0.6 slice_reduce_fusion
  106.9 0.0 collective-permute-done.1
  106.9 1.9 %add_bitcast_fusion = f32[1,64,2048]{2,1,0:T(8,128)} fusion(f32[64,2048]{1,0:T(8,128)S(1)} %get-tuple-element.10, f32[64,2048]{1,0:T(8,128)} %broadcast_select_fusion, f32[64,2048]{1,0:T(8,128)} %collective-permute-done.1, pred[]{:T(512)} %bitcast), kind=kLoop, calls=%fused_computation.1 | loop fusion | flops 262144 | bytes 2097153 | tf_op jit(solution)/shard_map/broadcast_in_dim | solution.py:367
  (3 shorter events, 0.0 us)
Async XLA Ops:
  0.6 53.4 %copy-start.10 = (s32[2,16]{1,0:T(2,128)S(1)}, s32[2,16]{1,0:T(2,128)}, u32[]{:S(2)}) copy-start(s32[2,16]{1,0:T(2,128)} %sel_ref.3) | copy-start | bytes 388
  1.3 1.0 copy-start.2
  2.3 0.7 copy-start.5
  9.3 12.9 %all-to-all-start = ((f32[4,16,128]{2,1,0:T(8,128)}), f32[4,16,128]{2,1,0:T(8,128)S(1)}, u32[]{:S(2)}, u32[]{:S(2)}) async-start(f32[4,16,128]{2,1,0:T(8,128)} %observe.1), calls=%async_computation | async-start | bytes 65536 | tf_op jit(solution)/shard_map/all_to_all | solution.py:324
  17.1 55.2 %collective-permute-start = (f32[64,2048]{1,0:T(8,128)}, f32[64,2048]{1,0:T(8,128)}, u32[]{:S(2)}, u32[]{:S(2)}) collective-permute-start(f32[64,2048]{1,0:T(8,128)} %bitcast.17), channel_id=1, source_target_pairs={{0,32},{32,0},{64,96},{96,64},{128,160},{160,128},{192,224},{224,1... | collective-permute-start | bytes 1572872 | tf_op jit(solution)/shard_map/ppermute | solution.py:296
  21.3 39.1 %copy-start.4 = (bf16[256,512]{1,0:T(8,128)(2,1)S(1)}, bf16[256,512]{1,0:T(8,128)(2,1)}, u32[]{:S(2)}) copy-start(bf16[256,512]{1,0:T(8,128)(2,1)} %constant.32.clone.ht_ref) | copy-start | bytes 786436
  21.3 39.1 %copy-start.8 = (f32[16,512]{1,0:T(8,128)S(1)}, f32[16,512]{1,0:T(8,128)}, u32[]{:S(2)}) copy-start(f32[16,512]{1,0:T(8,128)} %spec_ref.1) | copy-start | bytes 98308
  23.6 10.3 %all-to-all-start.2 = ((bf16[4,16,512]{2,1,0:T(8,128)(2,1)}), bf16[4,16,512]{2,1,0:T(8,128)(2,1)S(1)}, u32[]{:S(2)}, u32[]{:S(2)}) async-start(bf16[4,16,512]{2,1,0:T(8,128)(2,1)} %broadcast_in_dim.15), calls=%async_computation.2 | async-start | bytes 131072 | tf_op jit(solution)/shard_map/all_to_all | solution.py:326
  27.1 1.6 %copy-start = (bf16[512,2048]{1,0:T(8,128)(2,1)S(1)}, bf16[512,2048]{1,0:T(8,128)(2,1)}, u32[]{:S(2)}) copy-start(bf16[512,2048]{1,0:T(8,128)(2,1)} %constant.31.clone.tt_ref) | copy-start | bytes 6291460
  28.6 0.7 copy-start.6
  29.3 0.7 copy-start.9
  30.0 30.4 %copy-start.1 = (bf16[512,2048]{1,0:T(8,128)(2,1)S(1)}, bf16[512,2048]{1,0:T(8,128)(2,1)}, u32[]{:S(2)}) copy-start(bf16[512,2048]{1,0:T(8,128)(2,1)} %constant.31.clone.tt_ref) | copy-start | bytes 6291460
  33.9 26.4 %all-to-all-start.1 = ((bf16[32,8,128]{2,1,0:T(8,128)(2,1)}), bf16[32,8,128]{2,1,0:T(8,128)(2,1)S(1)}, u32[]{:S(2)}, u32[]{:S(2)}) async-start(bf16[32,8,128]{2,1,0:T(8,128)(2,1)} %get-tuple-element.8), calls=%async_computation.1 | async-start | bytes 131072 | tf_op jit(solution)/shard_map/all_to_all | solution.py:336
  47.0 8.3 %collective-permute-start.2 = (f32[1,2048]{1,0:T(1,128)S(1)}, f32[1,2048]{1,0:T(1,128)S(1)}, u32[]{:S(2)}, u32[]{:S(2)}) collective-permute-start(f32[1,2048]{1,0:T(1,128)S(1)} %get-tuple-element.13), channel_id=1, source_target_pairs={{0,1},{1,2},{2,3},{3,4},{4,5},{5,6},{6,7},{7,8},{8,9},{9,10},{10,1... | collective-permute-start | bytes 24584 | tf_op jit(solution)/shard_map/ppermute | solution.py:347
  51.4 5.9 %collective-permute-start.3 = (f32[1,2048]{1,0:T(1,128)S(1)}, f32[1,2048]{1,0:T(1,128)S(1)}, u32[]{:S(2)}, u32[]{:S(2)}) collective-permute-start(f32[1,2048]{1,0:T(1,128)S(1)} %get-tuple-element.12), channel_id=1, source_target_pairs={{1,0},{2,1},{3,2},{4,3},{5,4},{6,5},{7,6},{8,7},{9,8},{10,9},{11,1... | collective-permute-start | bytes 24584 | tf_op jit(solution)/shard_map/ppermute | solution.py:348
  57.3 15.0 %copy-start.3 = (f32[1,64,2048]{2,1,0:T(8,128)S(1)}, f32[1,64,2048]{2,1,0:T(8,128)}, u32[]{:S(2)}) copy-start(f32[1,64,2048]{2,1,0:T(8,128)} %param.12) | copy-start | bytes 1572868
  63.0 21.1 %copy-start.7 = (s32[64,16]{0,1:T(8,128)S(1)}, s32[64,16]{0,1:T(8,128)}, u32[]{:S(2)}) copy-start(s32[64,16]{0,1:T(8,128)} %param.14) | copy-start | bytes 12292
  63.0 21.1 %all-to-all-start.3 = ((bf16[32,24,128]{2,1,0:T(8,128)(2,1)}), bf16[32,24,128]{2,1,0:T(8,128)(2,1)S(1)}, u32[]{:S(2)}, u32[]{:S(2)}) async-start(bf16[32,24,128]{2,1,0:T(8,128)(2,1)} %spectral.1), calls=%async_computation.3 | async-start | bytes 393216 | tf_op jit(solution)/shard_map/all_to_all | solution.py:345
  73.2 33.7 %collective-permute-start.1 = (f32[64,2048]{1,0:T(8,128)}, f32[64,2048]{1,0:T(8,128)}, u32[]{:S(2)}, u32[]{:S(2)}) collective-permute-start(f32[64,2048]{1,0:T(8,128)} %broadcast_select_fusion), channel_id=1, source_target_pairs={{0,64},{32,96},{64,0},{96,32},{128,192},{160,224},{192,128},{224,1... | collective-permute-start | bytes 1572872 | tf_op jit(solution)/shard_map/ppermute | solution.py:296
  91.6 14.7 %all-to-all-start.4 = ((f32[32,1,128]{2,1,0:T(1,128)}), f32[32,1,128]{2,1,0:T(1,128)S(1)}, u32[]{:S(2)}, u32[]{:S(2)}) async-start(f32[32,1,128]{2,1,0:T(1,128)} %get-tuple-element.11), calls=%async_computation.4 | async-start | bytes 32768 | tf_op jit(solution)/shard_map/all_to_all | solution.py:365

commit v2 on v1

--- a/solution.py
+++ b/solution.py
@@ -38,11 +38,6 @@
     return out.reshape(bands * 8, y_table.shape[1])
 
 
-def pack(values):
-    rows, per_row = values.shape
-    return values.reshape(rows // 8, 8, per_row).transpose(1, 0, 2).reshape(8, rows // 8 * per_row)
-
-
 def lane_iota():
     return lax.broadcasted_iota(jnp.int32, (8, LANES), 1)
 
@@ -60,96 +55,138 @@
     return jnp.where(sel_ref[0, one] < 1, one, one ^ 1)
 
 
-def fill_cols(col_ref, col_scr):
-    per_row, rows = col_ref.shape
-    col_scr[:, 0:per_row] = col_ref[...].T
-
-
-def gather_rows(field_ref, col_scr, seen_scr, per_row):
+def fill_tile(source_ref, scr):
+    per_row = source_ref.shape[0]
+    scr[...] = jnp.zeros(scr.shape, scr.dtype)
+    scr[:, 0:per_row] = source_ref[...].T
+
+
+def gather_rows(field_ref, col_scr, seen_scr):
     rows, columns = field_ref.shape
-    lane = lane_iota()
-
-    def one_group(group, carry):
-        at = pl.multiple_of(group * 8, 8)
-        cols = col_scr[pl.ds(at, 8), :]
+    for at in range(0, rows, 8):
+        cols = col_scr[at : at + 8, :]
         high, low = cols >> 7, cols & 127
         seen = jnp.zeros((8, LANES), jnp.float32)
-        for j in range(per_row):
-            high_j = jnp.broadcast_to(high[:, j : j + 1], (8, LANES))
-            low_j = jnp.broadcast_to(low[:, j : j + 1], (8, LANES))
-            picked = field_ref[pl.ds(at, 8), 0:LANES]
-            for chunk in range(1, columns // LANES):
-                picked = jnp.where(
-                    high_j == chunk,
-                    field_ref[pl.ds(at, 8), chunk * LANES : (chunk + 1) * LANES],
-                    picked,
-                )
-            value = jnp.sum(jnp.where(lane == low_j, picked, 0.0), axis=1, keepdims=True)
-            seen = jnp.where(lane == j, value, seen)
-        seen_scr[pl.ds(at, 8), :] = seen
-        return carry
-
-    lax.fori_loop(0, rows // 8, one_group, 0)
-
-
-def packed(scr, per_row):
-    groups = scr.shape[0] // 8
+        for chunk in range(columns // LANES):
+            here = field_ref[at : at + 8, chunk * LANES : (chunk + 1) * LANES]
+            got = jnp.take_along_axis(here, low, axis=1, mode="promise_in_bounds")
+            seen = jnp.where(high == chunk, got, seen)
+        seen_scr[at : at + 8, :] = seen
+
+
+def packed(tile, per_row):
     lane = lane_iota()
-    out = scr[0:8, :]
-    for group in range(1, groups):
-        rolled = pltpu.roll(scr[group * 8 : group * 8 + 8, :], group * per_row, axis=1)
+    out = tile[0:8, :]
+    for group in range(1, tile.shape[0] // 8):
+        rolled = pltpu.roll(tile[group * 8 : group * 8 + 8, :], group * per_row, axis=1)
         out = jnp.where(lane // per_row == group, rolled, out)
     return out
 
 
-def observe_kernel(lw_ref, col_ref, stream_ref, out_ref, col_scr, seen_scr):
+def observe_kernel(
+    lw_ref, col_hbm, val_hbm, wgt_hbm, noise_hbm, stream_hbm, out_ref, col_scr, wgt_scr,
+    col_ref, val_ref, wgt_ref, noise_ref, stream_ref, val_scr, seen_scr, sems,
+):
+    copies = [
+        pltpu.make_async_copy(source, to, sems.at[at])
+        for at, (source, to) in enumerate(
+            (
+                (col_hbm, col_ref),
+                (val_hbm, val_ref),
+                (stream_hbm, stream_ref),
+                (noise_hbm, noise_ref),
+                (wgt_hbm, wgt_ref),
+            )
+        )
+    ]
+    for copy in copies:
+        copy.start()
     per_row = col_ref.shape[0]
-    fill_cols(col_ref, col_scr)
-    gather_rows(stream_ref, col_scr, seen_scr, per_row)
-    seen = packed(seen_scr, per_row)
+    modes_here, n_modes = noise_ref.shape
+    copies[0].wait()
+    copies[1].wait()
+    fill_tile(col_ref, col_scr)
+    fill_tile(val_ref, val_scr)
+    copies[2].wait()
+    gather_rows(stream_ref, col_scr, seen_scr)
+    mismatch = packed(val_scr[...] - seen_scr[...], per_row)
     weight = jnp.full((8, LANES), lw_ref[0], jnp.float32)
+    row = lax.broadcasted_iota(jnp.int32, (8, LANES), 0)
+    high, mid, low = split3(weight)
+    weight = jnp.where(row == 0, high, jnp.where(row == 1, mid, jnp.where(row == 2, low, 0.0)))
+    values = jnp.concatenate(list(split3(mismatch)) + [weight], axis=0).astype(jnp.bfloat16)
+    copies[4].wait()
+    fill_tile(wgt_ref, wgt_scr)
+    copies[3].wait()
+    noise = noise_ref[...]
+    chunks = n_modes // LANES
     for peer in range(GROUP):
-        out_ref[peer, 0:8, :] = seen
-        out_ref[peer, 8:16, :] = weight
+        for chunk in range(chunks):
+            out_ref[peer, chunk * modes_here : (chunk + 1) * modes_here, :] = noise[
+                :, chunk * LANES : (chunk + 1) * LANES
+            ]
+        out_ref[peer, chunks * modes_here :, :] = values
 
 
 def gradient_kernel(
-    meta_ref, sel_ref, col_ref, val_ref, wgt_ref, seen_ref, tt_ref, send_ref, miss_ref, part_ref,
-    col_scr, wm_scr, grad_scr,
+    meta_ref, sel_ref, col_scr, wgt_scr, seen_ref, tt_hbm, send_ref, miss_ref, part_ref,
+    tt_ref, grad_scr, sem,
 ):
-    per_row, rows = col_ref.shape
+    load = pltpu.make_async_copy(tt_hbm, tt_ref, sem)
+    load.start()
+    rows = grad_scr.shape[0]
+    per_row = LANES * 8 // rows
     columns = tt_ref.shape[1]
-    position = source_slot(sel_ref, meta_ref) % GROUP
-    fill_cols(col_ref, col_scr)
-    both = seen_ref[position]
-    mismatch = val_ref[...] - both[0:8]
-    weighted = wgt_ref[...] * mismatch
-    miss_ref[0:8, :] = mismatch
-    miss_ref[8:16, :] = both[8:16]
+    position = source_slot(sel_ref, meta_ref) & (GROUP - 1)
+    first = seen_ref.shape[1] - 32
+    sent = seen_ref[position][first:, :].astype(jnp.float32)
+    mismatch = sent[0:8] + sent[8:16] + sent[16:24]
+    weight = sent[24:25] + sent[25:26] + sent[26:27]
+    miss_ref[rows:, :] = jnp.broadcast_to(weight, (8, LANES))
+    tiles = [mismatch] + [
+        pltpu.roll(mismatch, LANES - group * per_row, axis=1) for group in range(1, rows // 8)
+    ]
+    mismatch = jnp.concatenate(tiles, axis=0)
+    miss_ref[0:rows, :] = mismatch
+    weighted = wgt_scr[...] * mismatch
     part_ref[...] = jnp.full((8, LANES), 0.5 * jnp.sum(weighted * mismatch), jnp.float32)
+
+    def repeated(tile):
+        step = per_row
+        while step < LANES:
+            tile = tile + pltpu.roll(tile, step, axis=1)
+            step *= 2
+        return tile
+
+    diagonal = lane_iota() // per_row == lax.broadcasted_iota(jnp.int32, (8, LANES), 0)
+    row_f = lax.broadcasted_iota(jnp.int32, (LANES, LANES), 0).astype(jnp.float32)
     for group in range(rows // 8):
-        shift = (LANES - group * per_row) % LANES
-        wm_scr[group * 8 : group * 8 + 8, :] = (
-            pltpu.roll(weighted, shift, axis=1) if shift else weighted
+        at = group * 8
+        cols = repeated(col_scr[at : at + 8, :])
+        high = jnp.where(diagonal, cols >> 7, -1)
+        low = jnp.sum(
+            jnp.where(diagonal, (cols & 127).astype(jnp.float32), 0.0), axis=0, keepdims=True
         )
-    lane = lane_iota()
-
-    def one_group(group, carry):
-        at = pl.multiple_of(group * 8, 8)
-        cols = col_scr[pl.ds(at, 8), :]
-        wms = wm_scr[pl.ds(at, 8), :]
-        col_j = [jnp.broadcast_to(cols[:, j : j + 1], (8, LANES)) for j in range(per_row)]
-        wm_j = [jnp.broadcast_to(wms[:, j : j + 1], (8, LANES)) for j in range(per_row)]
+        one_hot = jnp.where(row_f == low, 1.0, 0.0).astype(jnp.bfloat16)
+        left = []
+        for piece in split3(repeated(weighted[at : at + 8, :])):
+            left.append(
+                jnp.concatenate(
+                    [jnp.where(high == chunk, piece, 0.0) for chunk in range(columns // LANES)], axis=0
+                ).astype(jnp.bfloat16)
+            )
+        spread = lax.dot_general(
+            jnp.concatenate(left, axis=1),
+            jnp.concatenate([one_hot] * 3, axis=1),
+            (((1,), (1,)), ((), ())),
+            preferred_element_type=jnp.float32,
+        )
         for chunk in range(columns // LANES):
-            here = lane + chunk * LANES
-            total = jnp.where(col_j[0] == here, wm_j[0], 0.0)
-            for j in range(1, per_row):
-                total = total + jnp.where(col_j[j] == here, wm_j[j], 0.0)
-            grad_scr[pl.ds(at, 8), chunk * LANES : (chunk + 1) * LANES] = total
-        return carry
-
-    lax.fori_loop(0, rows // 8, one_group, 0)
+            grad_scr[at : at + 8, chunk * LANES : (chunk + 1) * LANES] = spread[
+                chunk * 8 : chunk * 8 + 8, :
+            ]
     gradient = grad_scr[...].astype(jnp.bfloat16)
+    load.wait()
     modes = lax.dot_general(
         tt_ref[...], gradient, (((1,), (1,)), ((), ())), preferred_element_type=jnp.float32
     )
@@ -166,8 +203,8 @@
     modes_here, n_modes = spec_ref.shape
     rows = tt_ref.shape[1]
     norm_factor = 4.0 / (rows * rows)
-    position = source_slot(sel_ref, meta_ref) % GROUP
-    me = meta_ref[1] % 8
+    position = source_slot(sel_ref, meta_ref) & (GROUP - 1)
+    me = meta_ref[1] & 7
     lane = lane_iota()
     low = lane < half
     tops, bottoms = [], []
@@ -185,7 +222,11 @@
     scaled = norm_factor * spec_ref[...]
     weighted = coefficients * scaled
     energy = jnp.sum(coefficients * weighted)
-    shaped = (jnp.sqrt(scaled) * noise_ref[position].astype(jnp.float32)).astype(jnp.bfloat16)
+    noise = noise_ref[position][0 : noise_ref.shape[1] - 32, :]
+    noise = jnp.concatenate(
+        [noise[at : at + modes_here] for at in range(0, noise.shape[0], modes_here)], axis=1
+    )
+    shaped = (jnp.sqrt(scaled) * noise.astype(jnp.float32)).astype(jnp.bfloat16)
     weighted = weighted.astype(jnp.bfloat16)
     stacked = jnp.concatenate([weighted, shaped], axis=0)
     inverted = jnp.dot(stacked, tt_ref[...], preferred_element_type=jnp.float32)
@@ -224,14 +265,19 @@
 
 
 def relax_kernel(
-    target_ref, col_ref, wgt_ref, miss_ref, rate_ref, modes_ref, tt_ref, field_ref, part_ref,
-    col_scr, seen_scr, inc_scr, one_scr,
+    target_ref, col_scr, wgt_scr, miss_ref, depth_hbm, above_ref, below_ref, modes_ref, tt_ref,
+    field_ref, part_ref, seen_scr, inc_scr, one_scr, rate_ref, depth_ref, sem,
 ):
-    per_row, rows = col_ref.shape
+    depth = pltpu.make_async_copy(depth_hbm, depth_ref, sem)
+    depth.start()
+    rows = depth_ref.shape[0]
+
+    def rate(depth):
+        return RELAX_RATE * depth / (4.0 * depth + STRETCH)
+
     bands, _, _ = modes_ref.shape
     n_modes, columns = tt_ref.shape
     modes_here = n_modes // bands
-    fill_cols(col_ref, col_scr)
     lane = lane_iota()
     quads, scalars = [], jnp.zeros((8, LANES), jnp.float32)
     for quad in range(bands // 8):
@@ -246,7 +292,7 @@
     row = lax.broadcasted_iota(jnp.int32, (8, LANES), 0)
     misfit = jnp.sum(jnp.where(row < 3, scalars, 0.0))
     energy = jnp.sum(jnp.where((row >= 3) & (row < 6), scalars, 0.0))
-    weight = jnp.max(miss_ref[8:16, :])
+    weight = jnp.max(miss_ref[rows:, :])
     misfit_v = jnp.full((8, LANES), misfit + weight - target_ref[0], jnp.float32)
     step = (misfit_v / jnp.full((8, LANES), energy + 1.0, jnp.float32))[0:1, 0:1]
     main = modes_ref[:, 0:modes_here, :].reshape(n_modes, LANES)
@@ -257,6 +303,11 @@
     inc_scr[6:8, :] = edge[0:2]
     inc_scr[8 + rows : 10 + rows, :] = edge[2:4]
 
+    depth.wait()
+    rate_ref[7:8, :] = rate(above_ref[...])
+    rate_ref[8 : 8 + rows, :] = rate(depth_ref[...])
+    rate_ref[8 + rows : 9 + rows, :] = rate(below_ref[...])
+
     def beside(values):
         return pltpu.roll(values, 1, axis=1) + pltpu.roll(values, columns - 1, axis=1)
 
@@ -268,14 +319,18 @@
     field_ref[...] = (1.0 - RELAX_RATE) * here + rate_ref[8 : 8 + rows, :] * (
         around - inc_scr[8 : 8 + rows, :]
     )
-    gather_rows(field_ref, col_scr, seen_scr, per_row)
-    left_over = miss_ref[0:8, :] - packed(seen_scr, per_row)
-    part = 0.5 * jnp.sum(wgt_ref[...] * left_over * left_over)
+    gather_rows(field_ref, col_scr, seen_scr)
+    left_over = miss_ref[0:rows, :] - seen_scr[...]
+    part = 0.5 * jnp.sum(wgt_scr[...] * left_over * left_over)
     part_ref[...] = jnp.full(part_ref.shape, part, jnp.float32)
 
 
 SMEM = pl.BlockSpec(memory_space=pltpu.SMEM)
 VMEM = pl.BlockSpec(memory_space=pltpu.VMEM)
+HBM = pl.BlockSpec(memory_space=pltpu.HBM)
+
+
+COST = {"observe": 40, "gradient": 40, "spectral": 1, "relax": 1}
 
 
 def call(kernel, in_specs, out_shape, scratch, name):
@@ -286,8 +341,15 @@
         out_shape=out_shape,
         scratch_shapes=scratch,
         name=name,
+        cost_estimate=pl.CostEstimate(
+            flops=COST[name] * 10**9, transcendentals=0, bytes_accessed=4 * 10**6
+        ),
         compiler_params=pltpu.CompilerParams(vmem_limit_bytes=VMEM_LIMIT),
     )
+
+
+def in_hbm(value):
+    return pltpu.with_memory_space_constraint(value, pltpu.HBM)
 
 
 def swapped(value, axis, bit):
@@ -314,26 +376,42 @@
     slot = lax.axis_index("particle")
     meta = jnp.stack([slot, lax.axis_index("space")]).astype(jnp.int32)
     own = stream[0]
-    col_t = obs_col.T
-    tile = pltpu.VMEM((rows, LANES), f32)
-    col_tile = pltpu.VMEM((rows, LANES), jnp.int32)
-
-    seen = call(
-        observe_kernel, [SMEM, VMEM, VMEM], shape((GROUP, 16, LANES), f32), [col_tile, tile], "observe"
-    )(log_weight, col_t, own)
-    seen = lax.all_to_all(seen, "particle", 0, 0, axis_index_groups=groups, tiled=True)
-    noise = jnp.broadcast_to(noise_coef, (GROUP,) + noise_coef.shape[1:])
-    noise = lax.all_to_all(noise, "particle", 0, 0, axis_index_groups=groups, tiled=True)
-
-    weight_p = pack(obs_weight)
+    col_t, val_t, wgt_t = obs_col.T, obs_val.T, obs_weight.T
+    vmem = pltpu.VMEM
+    tile = vmem((rows, LANES), f32)
+    whole = vmem((rows, columns), f32)
+    padded = vmem((rows + 16, columns), f32)
+    small = (per_row, rows)
+    dma = pltpu.SemaphoreType.DMA
+
+    sent, col_tile, wgt_tile = call(
+        observe_kernel,
+        [SMEM, HBM, HBM, HBM, HBM, HBM],
+        (
+            shape((GROUP, modes_here * n_modes // LANES + 32, LANES), bf16),
+            shape((rows, LANES), jnp.int32),
+            shape((rows, LANES), f32),
+        ),
+        [vmem(small, jnp.int32), vmem(small, f32), vmem(small, f32), vmem((modes_here, n_modes), bf16),
+         whole, tile, tile, dma((5,))],
+        "observe",
+    )(log_weight, *map(in_hbm, (col_t, val_t, wgt_t, noise_coef[0], own)))
+    sent, held = lax.optimization_barrier((sent, own))
+    sent = lax.all_to_all(sent, "particle", 0, 0, axis_index_groups=groups, tiled=True)
+    swap = swapped(held, "particle", 0)
+
     send, miss, part = call(
         gradient_kernel,
-        [SMEM, SMEM, VMEM, VMEM, VMEM, VMEM, VMEM],
-        (shape((bands, 8, LANES), bf16), shape((16, LANES), f32), shape((8, LANES), f32)),
-        [col_tile, tile, pltpu.VMEM((rows, columns), f32)],
+        [SMEM, SMEM, VMEM, VMEM, VMEM, HBM],
+        (shape((bands, 8, LANES), bf16), shape((rows + 8, LANES), f32), shape((8, LANES), f32)),
+        [vmem((n_modes, columns), bf16), whole, dma(())],
         "gradient",
-    )(meta, selection, col_t, pack(obs_val), weight_p, seen, tt_all)
+    )(meta, selection, col_tile, wgt_tile, sent, in_hbm(tt_all))
     col_modes = lax.all_to_all(send, "space", 0, 0, tiled=True)
+
+    near = jnp.where(selection[0, slot] < 1, own, swap)
+    far = swapped(near, "particle", 1)
+    col_modes, near = lax.optimization_barrier((col_modes, near))
 
     send = call(
         spectral_kernel,
@@ -341,30 +419,24 @@
         shape((bands, modes_here + 8, LANES), bf16),
         [],
         "spectral",
-    )(meta, selection, col_modes, noise, spectrum, part, tt_all, ht_all)
+    )(meta, selection, col_modes, sent, spectrum, part, tt_all, ht_all)
+    send, depth = lax.optimization_barrier((send, depth_field))
     band_modes = lax.all_to_all(send, "space", 0, 0, tiled=True)
-
-    above = lax.ppermute(depth_field[-1:], "space", [(i, i + 1) for i in range(bands - 1)])
-    below = lax.ppermute(depth_field[:1], "space", [(i + 1, i) for i in range(bands - 1)])
-    blank = jnp.zeros((7, columns), f32)
-    depth = jnp.concatenate([blank, above, depth_field, below, blank], axis=0)
-    rate = RELAX_RATE * depth / (4.0 * depth + STRETCH)
-
-    fields = own
-    for section in range(2):
-        chosen = selection[section, slot]
-        fields = jnp.where(chosen < 1, fields, swapped(fields, "particle", section))
+    above = lax.ppermute(depth[-1:], "space", [(i, i + 1) for i in range(bands - 1)])
+    below = lax.ppermute(depth[:1], "space", [(i + 1, i) for i in range(bands - 1)])
 
     field, part = call(
         relax_kernel,
-        [SMEM, VMEM, VMEM, VMEM, VMEM, VMEM, VMEM],
+        [SMEM, VMEM, VMEM, VMEM, HBM, VMEM, VMEM, VMEM, VMEM],
         (shape((rows, columns), f32), shape((bands, 1, LANES), f32)),
-        [col_tile, tile, pltpu.VMEM((rows + 16, columns), f32), pltpu.VMEM((rows + 16, columns), f32)],
+        [tile, padded, padded, padded, whole, dma(())],
         "relax",
-    )(target, col_t, weight_p, miss, rate, band_modes, tt_all)
+    )(target, col_tile, wgt_tile, miss, in_hbm(depth_field), above, below, band_modes, tt_all)
     parts = lax.all_to_all(part, "space", 0, 0, tiled=True)
+    analysis = field + jnp.where(selection[1, slot] < 1, near, far)
+    parts, analysis = lax.optimization_barrier((parts, analysis))
     misfit_out = jnp.sum(parts[:, 0, 0:1], axis=0)
-    return (fields + field)[None], misfit_out
+    return analysis[None], misfit_out
 
 
 def solution(mesh):

time: 110 us -> 83.6 us (0.76)
  local copies, waits for them, and re-layouts: 12.5 us -> 1.56 us
  Pallas kernels: 20.3 us -> 12.4 us
  starting transfers between devices: 52.6 us -> 46.1 us
  other arithmetic: 4.69 us -> 2.9 us
  waiting for transfers between devices: 15.4 us -> 16.7 us
    pallas_call x3, Pallas kernels: 17.7 us -> 9.82 us  [the longest x1 4.22 us: per_device(): call(gradient_kernel, [SMEM, SMEM, VMEM, VMEM, VMEM, HBM], (shape((bands,...]
    unnamed x24 -> x8, local copies, waits for them, and re-layouts: 6.29 us -> 0.02 us
    all_to_all x1, waiting for transfers between devices: 0.01 us -> 5.06 us  [per_device(): col_modes = lax.all_to_all(send, 'space', 0, 0, tiled=True)]
    all_to_all x1, starting transfers between devices: 9.28 us -> 5.03 us  [per_device(): band_modes = lax.all_to_all(send, 'space', 0, 0, tiled=True)]
    all_to_all x2 -> x1, starting transfers between devices: 11.2 us -> 7.82 us  [per_device(): lax.all_to_all(sent, 'particle', 0, 0, axis_index_groups=groups, tiled=True)]
    concatenate x1 -> x0, local copies, waits for them, and re-layouts: 3.09 us -> none  [per_device(): depth = jnp.concatenate([blank, above, depth_field, below, blank], axis=0)]
    all_to_all x1, starting transfers between devices: 5.34 us -> 8.19 us  [per_device(): parts = lax.all_to_all(part, 'space', 0, 0, tiled=True)]
    ppermute x2, waiting for transfers between devices: 1.98 us -> 0.01 us  [the longest x1 0.01 us: per_device(): lax.ppermute(depth[:1], 'space', [(i + 1, i) for i in range(bands - 1)])]
  transfers between devices with their start and end apart: 9 -> 8, of which waited for: 3 -> 3; matrix products, arithmetic and copies ran while one was open for 10% -> 5% of each run, Pallas kernels for 13% -> 12%
where the time goes in v2:
time: 83.6 us; the launch traced here: 82.9 us
  starting transfers between devices  46.1 us (55%)
  waiting for transfers between devices  16.7 us (20%)
  Pallas kernels  12.4 us (15%)
  between operations  3.26 us (4%)
  other arithmetic  2.9 us (3%)
  local copies, waits for them, and re-layouts  1.56 us (2%)
    all_to_all x1, starting transfers between devices, per_device(): col_modes = lax.all_to_all(send, 'space', 0, 0, tiled=True)  11.8 us
    all_to_all x1, waiting for transfers between devices, per_device(): parts = lax.all_to_all(part, 'space', 0, 0, tiled=True)  8.42 us
    all_to_all x1, starting transfers between devices, per_device(): parts = lax.all_to_all(part, 'space', 0, 0, tiled=True)  8.19 us
    all_to_all x1, starting transfers between devices, per_device(): lax.all_to_all(sent, 'particle', 0, 0, axis_index_groups=groups, tiled=True)  7.82 us
    ppermute x2, starting transfers between devices, swapped(): return lax.ppermute(value, axis, pairs)  6.76 us
    all_to_all x1, waiting for transfers between devices, per_device(): col_modes = lax.all_to_all(send, 'space', 0, 0, tiled=True)  5.06 us
    all_to_all x1, starting transfers between devices, per_device(): band_modes = lax.all_to_all(send, 'space', 0, 0, tiled=True)  5.03 us
    ppermute x1, starting transfers between devices, per_device(): lax.ppermute(depth[-1:], 'space', [(i, i + 1) for i in range(bands - 1)])  4.32 us
  transfers between devices with their start and end apart: 8, of which 3 were waited for; matrix products, arithmetic and copies ran while one was open for 5% of the time, Pallas kernels for 12%

profile of v2, /device:TPU:1, one launch (start us, length us, event | category | flops | bytes accessed | tf_op | source)
XLA Modules:
  0.0 82.9 jit_solution(8831671422069796753)
XLA Ops:
  1.3 0.0 copy-start
  1.3 2.2 %observe.1 = (bf16[4,96,128]{2,1,0:T(8,128)(2,1)}, s32[64,128]{1,0:T(8,128)S(1)}, f32[64,128]{1,0:T(8,128)S(1)}) custom-call(f32[1]{0:T(128)S(6)} %copy.14.lw_ref, s32[16,64]{1,0:T(8,128)} %bitcast.14, f32[16,64]{1,0:T(8,128)} %bitcast.15, f32[16,64]{1,0:T(8,128)} %bitcast.16, bf16[16,512]{1,0:T(8,128)(2,1)} %bitcast.13, f32[64,2048]{1,0:T(8,128)} %bitcast.4.stream_hbm), custom_call_target="tpu_custom_call" | custom-call | flops 40000000000 | bytes 4000000 | tf_op jit(solution)/shard_map/observe/pallas_call | solution.py:387
  3.5 7.8 %all-to-all-start = ((bf16[4,96,128]{2,1,0:T(8,128)(2,1)}), bf16[4,96,128]{2,1,0:T(8,128)(2,1)S(1)}, u32[]{:S(2)}, u32[]{:S(2)}) async-start(bf16[4,96,128]{2,1,0:T(8,128)(2,1)} %get-tuple-element.21), calls=%async_computation | async-start | bytes 196608 | tf_op jit(solution)/shard_map/all_to_all | solution.py:400
  11.3 3.4 %collective-permute-start = (f32[64,2048]{1,0:T(8,128)}, f32[64,2048]{1,0:T(8,128)}, u32[]{:S(2)}, u32[]{:S(2)}) collective-permute-start(f32[64,2048]{1,0:T(8,128)} %bitcast.4.stream_hbm), channel_id=1, source_target_pairs={{0,32},{32,0},{64,96},{96,64},{128,160},{160,128},{192,224},{224,1... | collective-permute-start | bytes 1572872 | tf_op jit(solution)/shard_map/ppermute | solution.py:358
  14.7 0.0 copy-done
  14.7 0.7 constant_dynamic-slice_fusion
  15.9 0.1 pad_add_fusion.meta_ref
  16.0 0.0 all-to-all-done.seen_ref.noise_ref
  16.0 0.0 copy-start.1
  16.0 0.0 copy-start.2
  16.0 0.0 copy-start.3
  16.0 4.2 %gradient.1 = (bf16[32,8,128]{2,1,0:T(8,128)(2,1)}, f32[72,128]{1,0:T(8,128)S(1)}, f32[8,128]{1,0:T(8,128)S(1)}) custom-call(s32[2]{0:T(128)S(1)} %pad_add_fusion.meta_ref, s32[2,16]{1,0:T(2,128)S(1)} %copy-done, s32[64,128]{1,0:T(8,128)S(1)} %get-tuple-element.18.col_scr, f32[64,128]{1,0:T(8,128)S(1)} %get-tuple-element.19.wgt_scr, ...), custom_call_target="tpu_custom_call" | custom-call | flops 40000000000 | bytes 4000000 | tf_op jit(solution)/shard_map/gradient/pallas_call | solution.py:403
  20.2 11.8 %all-to-all-start.1 = ((bf16[32,8,128]{2,1,0:T(8,128)(2,1)}), bf16[32,8,128]{2,1,0:T(8,128)(2,1)S(1)}, u32[]{:S(2)}, u32[]{:S(2)}) async-start(bf16[32,8,128]{2,1,0:T(8,128)(2,1)} %get-tuple-element.23), calls=%async_computation.1 | async-start | bytes 131072 | tf_op jit(solution)/shard_map/all_to_all | solution.py:410
  32.1 0.0 collective-permute-done
  32.1 1.3 %broadcast_select_fusion = f32[64,2048]{1,0:T(8,128)S(1)} fusion(f32[64,2048]{1,0:T(8,128)} %collective-permute-done, pred[]{:T(512)} %bitcast.7, f32[1,64,2048]{2,1,0:T(8,128)} %param.12), kind=kLoop, calls=%fused_computation.1 | loop fusion | flops 131072 | bytes 1572865 | tf_op jit(solution)/shard_map/jit(_where)/select_n | solution.py:412
  33.4 3.4 %collective-permute-start.3 = (f32[64,2048]{1,0:T(8,128)S(1)}, f32[64,2048]{1,0:T(8,128)}, u32[]{:S(2)}, u32[]{:S(2)}) collective-permute-start(f32[64,2048]{1,0:T(8,128)S(1)} %broadcast_select_fusion), channel_id=1, source_target_pairs={{0,64},{32,96},{64,0},{96,32},{128,192},{160,224},{192,128},{224,1... | collective-permute-start | bytes 1572872 | tf_op jit(solution)/shard_map/ppermute | solution.py:358
  36.8 5.1 %all-to-all-done.1.modes_ref = bf16[32,8,128]{2,1,0:T(8,128)(2,1)S(1)} async-done(((bf16[32,8,128]{2,1,0:T(8,128)(2,1)}), bf16[32,8,128]{2,1,0:T(8,128)(2,1)S(1)}, u32[]{:S(2)}, u32[]{:S(2)}) %all-to-all-start.1) | async-done | bytes 65568 | tf_op jit(solution)/shard_map/all_to_all | solution.py:410
  41.8 0.0 copy-done.1
  41.8 0.0 copy-done.2
  41.8 0.0 copy-done.3
  41.9 2.6 %spectral.1 = bf16[32,24,128]{2,1,0:T(8,128)(2,1)} custom-call(s32[2]{0:T(128)S(1)} %pad_add_fusion.meta_ref, s32[2,16]{1,0:T(2,128)S(1)} %copy-done, bf16[32,8,128]{2,1,0:T(8,128)(2,1)S(1)} %all-to-all-done.1.modes_ref, bf16[4,96,128]{2,1,0:T(8,128)(2,1)S(1)} %all-to-all-done.seen_ref.noise_ref, f32[16,512]{1,0:T(8,128)S(1)} %copy-done.1, ...), custom_call_target="tpu_custom_call" | custom-call | flops 1000000000 | bytes 4000000 | tf_op jit(solution)/shard_map/spectral/pallas_call | solution.py:416
  44.4 5.0 %all-to-all-start.2 = ((bf16[32,24,128]{2,1,0:T(8,128)(2,1)}), bf16[32,24,128]{2,1,0:T(8,128)(2,1)S(1)}, u32[]{:S(2)}, u32[]{:S(2)}) async-start(bf16[32,24,128]{2,1,0:T(8,128)(2,1)} %spectral.1), calls=%async_computation.2 | async-start | bytes 393216 | tf_op jit(solution)/shard_map/all_to_all | solution.py:424
  49.5 0.9 %fusion = (f32[1,2048]{1,0:T(1,128)S(1)}, f32[1,2048]{1,0:T(1,128)S(1)}) fusion(f32[64,2048]{1,0:T(8,128)} %depth_hbm.1), kind=kLoop, calls=%fused_computation.6 | loop fusion | bytes 32768 | tf_op jit(solution)/shard_map/slice | solution.py:426
  50.4 2.1 %collective-permute-start.2 = (f32[1,2048]{1,0:T(1,128)S(1)}, f32[1,2048]{1,0:T(1,128)S(1)}, u32[]{:S(2)}, u32[]{:S(2)}) collective-permute-start(f32[1,2048]{1,0:T(1,128)S(1)} %get-tuple-element.34), channel_id=1, source_target_pairs={{1,0},{2,1},{3,2},{4,3},{5,4},{6,5},{7,6},{8,7},{9,8},{10,9},{11,1... | collective-permute-start | bytes 24584 | tf_op jit(solution)/shard_map/ppermute | solution.py:426
  52.5 4.3 %collective-permute-start.1 = (f32[1,2048]{1,0:T(1,128)S(1)}, f32[1,2048]{1,0:T(1,128)S(1)}, u32[]{:S(2)}, u32[]{:S(2)}) collective-permute-start(f32[1,2048]{1,0:T(1,128)S(1)} %get-tuple-element.35), channel_id=1, source_target_pairs={{0,1},{1,2},{2,3},{3,4},{4,5},{5,6},{6,7},{7,8},{8,9},{9,10},{10,1... | collective-permute-start | bytes 24584 | tf_op jit(solution)/shard_map/ppermute | solution.py:425
  58.1 0.0 collective-permute-done.2.below_ref
  58.1 0.0 collective-permute-done.1.above_ref
  58.1 3.1 %all-to-all-done.2.modes_ref = bf16[32,24,128]{2,1,0:T(8,128)(2,1)S(1)} async-done(((bf16[32,24,128]{2,1,0:T(8,128)(2,1)}), bf16[32,24,128]{2,1,0:T(8,128)(2,1)S(1)}, u32[]{:S(2)}, u32[]{:S(2)}) %all-to-all-start.2) | async-done | bytes 196640 | tf_op jit(solution)/shard_map/all_to_all | solution.py:424
  61.3 3.4 %relax.1 = (f32[64,2048]{1,0:T(8,128)S(1)}, f32[32,1,128]{2,1,0:T(1,128)}) custom-call(f32[1]{0:T(128)S(6)} %copy.15.target_ref, s32[64,128]{1,0:T(8,128)S(1)} %get-tuple-element.18.col_scr, f32[64,128]{1,0:T(8,128)S(1)} %get-tuple-element.19.wgt_scr, f32[72,128]{1,0:T(8,128)S(1)} %get-tuple-element.22.miss_ref, f32[64,2048]{1,0:T(8,128)} %depth_hbm.1, ...), custom_call_target="tpu_custom_call" | custom-call | flops 1000000000 | bytes 4000000 | tf_op jit(solution)/shard_map/relax/pallas_call | solution.py:428
  64.7 8.2 %all-to-all-start.3 = ((f32[32,1,128]{2,1,0:T(1,128)}), f32[32,1,128]{2,1,0:T(1,128)S(1)}, u32[]{:S(2)}, u32[]{:S(2)}) async-start(f32[32,1,128]{2,1,0:T(1,128)} %get-tuple-element.29), calls=%async_computation.3 | async-start | bytes 32768 | tf_op jit(solution)/shard_map/all_to_all | solution.py:435
  72.9 0.0 collective-permute-done.3
  72.9 0.9 %select_add_fusion = f32[64,2048]{1,0:T(8,128)} fusion(f32[64,2048]{1,0:T(8,128)S(1)} %get-tuple-element.30, f32[64,2048]{1,0:T(8,128)S(1)} %broadcast_select_fusion, f32[64,2048]{1,0:T(8,128)} %collective-permute-done.3, pred[]{:T(512)} %bitcast.8), kind=kLoop, calls=%fused_computation | loop fusion | flops 262144 | bytes 2097153 | tf_op jit(solution)/shard_map/add | solution.py:436
  73.8 8.4 %all-to-all-done.3 = f32[32,1,128]{2,1,0:T(1,128)S(1)} async-done(((f32[32,1,128]{2,1,0:T(1,128)}), f32[32,1,128]{2,1,0:T(1,128)S(1)}, u32[]{:S(2)}, u32[]{:S(2)}) %all-to-all-start.3) | async-done | bytes 16416 | tf_op jit(solution)/shard_map/all_to_all | solution.py:435
  82.2 0.6 slice_reduce_fusion
Async XLA Ops:
  1.3 13.4 %copy-start = (s32[2,16]{1,0:T(2,128)S(1)}, s32[2,16]{1,0:T(2,128)}, u32[]{:S(2)}) copy-start(s32[2,16]{1,0:T(2,128)} %sel_ref.3) | copy-start | bytes 388
  3.5 12.5 %all-to-all-start = ((bf16[4,96,128]{2,1,0:T(8,128)(2,1)}), bf16[4,96,128]{2,1,0:T(8,128)(2,1)S(1)}, u32[]{:S(2)}, u32[]{:S(2)}) async-start(bf16[4,96,128]{2,1,0:T(8,128)(2,1)} %get-tuple-element.21), calls=%async_computation | async-start | bytes 196608 | tf_op jit(solution)/shard_map/all_to_all | solution.py:400
  11.3 20.8 %collective-permute-start = (f32[64,2048]{1,0:T(8,128)}, f32[64,2048]{1,0:T(8,128)}, u32[]{:S(2)}, u32[]{:S(2)}) collective-permute-start(f32[64,2048]{1,0:T(8,128)} %bitcast.4.stream_hbm), channel_id=1, source_target_pairs={{0,32},{32,0},{64,96},{96,64},{128,160},{160,128},{192,224},{224,1... | collective-permute-start | bytes 1572872 | tf_op jit(solution)/shard_map/ppermute | solution.py:358
  16.0 25.8 %copy-start.1 = (f32[16,512]{1,0:T(8,128)S(1)}, f32[16,512]{1,0:T(8,128)}, u32[]{:S(2)}) copy-start(f32[16,512]{1,0:T(8,128)} %spec_ref.1) | copy-start | bytes 98308
  16.0 25.8 %copy-start.2 = (bf16[512,2048]{1,0:T(8,128)(2,1)S(1)}, bf16[512,2048]{1,0:T(8,128)(2,1)}, u32[]{:S(2)}) copy-start(bf16[512,2048]{1,0:T(8,128)(2,1)} %constant.24.clone.tt_hbm.tt_ref) | copy-start | bytes 6291460
  16.0 25.8 %copy-start.3 = (bf16[256,512]{1,0:T(8,128)(2,1)S(1)}, bf16[256,512]{1,0:T(8,128)(2,1)}, u32[]{:S(2)}) copy-start(bf16[256,512]{1,0:T(8,128)(2,1)} %constant.25.clone.ht_ref) | copy-start | bytes 786436
  20.2 21.6 %all-to-all-start.1 = ((bf16[32,8,128]{2,1,0:T(8,128)(2,1)}), bf16[32,8,128]{2,1,0:T(8,128)(2,1)S(1)}, u32[]{:S(2)}, u32[]{:S(2)}) async-start(bf16[32,8,128]{2,1,0:T(8,128)(2,1)} %get-tuple-element.23), calls=%async_computation.1 | async-start | bytes 131072 | tf_op jit(solution)/shard_map/all_to_all | solution.py:410
  33.4 39.5 %collective-permute-start.3 = (f32[64,2048]{1,0:T(8,128)S(1)}, f32[64,2048]{1,0:T(8,128)}, u32[]{:S(2)}, u32[]{:S(2)}) collective-permute-start(f32[64,2048]{1,0:T(8,128)S(1)} %broadcast_select_fusion), channel_id=1, source_target_pairs={{0,64},{32,96},{64,0},{96,32},{128,192},{160,224},{192,128},{224,1... | collective-permute-start | bytes 1572872 | tf_op jit(solution)/shard_map/ppermute | solution.py:358
  44.4 16.8 %all-to-all-start.2 = ((bf16[32,24,128]{2,1,0:T(8,128)(2,1)}), bf16[32,24,128]{2,1,0:T(8,128)(2,1)S(1)}, u32[]{:S(2)}, u32[]{:S(2)}) async-start(bf16[32,24,128]{2,1,0:T(8,128)(2,1)} %spectral.1), calls=%async_computation.2 | async-start | bytes 393216 | tf_op jit(solution)/shard_map/all_to_all | solution.py:424
  50.4 7.8 %collective-permute-start.2 = (f32[1,2048]{1,0:T(1,128)S(1)}, f32[1,2048]{1,0:T(1,128)S(1)}, u32[]{:S(2)}, u32[]{:S(2)}) collective-permute-start(f32[1,2048]{1,0:T(1,128)S(1)} %get-tuple-element.34), channel_id=1, source_target_pairs={{1,0},{2,1},{3,2},{4,3},{5,4},{6,5},{7,6},{8,7},{9,8},{10,9},{11,1... | collective-permute-start | bytes 24584 | tf_op jit(solution)/shard_map/ppermute | solution.py:426
  52.5 5.6 %collective-permute-start.1 = (f32[1,2048]{1,0:T(1,128)S(1)}, f32[1,2048]{1,0:T(1,128)S(1)}, u32[]{:S(2)}, u32[]{:S(2)}) collective-permute-start(f32[1,2048]{1,0:T(1,128)S(1)} %get-tuple-element.35), channel_id=1, source_target_pairs={{0,1},{1,2},{2,3},{3,4},{4,5},{5,6},{6,7},{7,8},{8,9},{9,10},{10,1... | collective-permute-start | bytes 24584 | tf_op jit(solution)/shard_map/ppermute | solution.py:425
  64.7 17.5 %all-to-all-start.3 = ((f32[32,1,128]{2,1,0:T(1,128)}), f32[32,1,128]{2,1,0:T(1,128)S(1)}, u32[]{:S(2)}, u32[]{:S(2)}) async-start(f32[32,1,128]{2,1,0:T(1,128)} %get-tuple-element.29), calls=%async_computation.3 | async-start | bytes 32768 | tf_op jit(solution)/shard_map/all_to_all | solution.py:435

commit v3 on v2

--- a/solution.py
+++ b/solution.py
@@ -84,30 +84,31 @@
 
 
 def observe_kernel(
-    lw_ref, col_hbm, val_hbm, wgt_hbm, noise_hbm, stream_hbm, out_ref, col_scr, wgt_scr,
-    col_ref, val_ref, wgt_ref, noise_ref, stream_ref, val_scr, seen_scr, sems,
+    lw_ref, col_hbm, val_hbm, wgt_hbm, noise_hbm, stream_hbm, depth_hbm, tt_hbm,
+    out_ref, col_scr, wgt_scr, tt_ref, first_ref, last_ref,
+    col_ref, val_ref, wgt_ref, noise_ref, stream_ref, depth_ref, val_scr, seen_scr, sems,
 ):
-    copies = [
-        pltpu.make_async_copy(source, to, sems.at[at])
-        for at, (source, to) in enumerate(
-            (
-                (col_hbm, col_ref),
-                (val_hbm, val_ref),
-                (stream_hbm, stream_ref),
-                (noise_hbm, noise_ref),
-                (wgt_hbm, wgt_ref),
-            )
-        )
-    ]
-    for copy in copies:
-        copy.start()
+    rows = depth_hbm.shape[0]
+    pairs = (
+        (col_hbm, col_ref),
+        (val_hbm, val_ref),
+        (stream_hbm, stream_ref),
+        (noise_hbm, noise_ref),
+        (wgt_hbm, wgt_ref),
+        (depth_hbm.at[0:8, :], depth_ref.at[0:8, :]),
+        (depth_hbm.at[rows - 8 : rows, :], depth_ref.at[8:16, :]),
+        (tt_hbm, tt_ref),
+    )
+    loads = [pltpu.make_async_copy(a, b, sems.at[at]) for at, (a, b) in enumerate(pairs)]
+    for load in loads:
+        load.start()
     per_row = col_ref.shape[0]
     modes_here, n_modes = noise_ref.shape
-    copies[0].wait()
-    copies[1].wait()
+    loads[0].wait()
+    loads[1].wait()
     fill_tile(col_ref, col_scr)
     fill_tile(val_ref, val_scr)
-    copies[2].wait()
+    loads[2].wait()
     gather_rows(stream_ref, col_scr, seen_scr)
     mismatch = packed(val_scr[...] - seen_scr[...], per_row)
     weight = jnp.full((8, LANES), lw_ref[0], jnp.float32)
@@ -115,9 +116,9 @@
     high, mid, low = split3(weight)
     weight = jnp.where(row == 0, high, jnp.where(row == 1, mid, jnp.where(row == 2, low, 0.0)))
     values = jnp.concatenate(list(split3(mismatch)) + [weight], axis=0).astype(jnp.bfloat16)
-    copies[4].wait()
+    loads[4].wait()
     fill_tile(wgt_ref, wgt_scr)
-    copies[3].wait()
+    loads[3].wait()
     noise = noise_ref[...]
     chunks = n_modes // LANES
     for peer in range(GROUP):
@@ -126,14 +127,16 @@
                 :, chunk * LANES : (chunk + 1) * LANES
             ]
         out_ref[peer, chunks * modes_here :, :] = values
+    loads[5].wait()
+    loads[6].wait()
+    first_ref[...] = depth_ref[0:1, :]
+    last_ref[...] = depth_ref[15:16, :]
+    loads[7].wait()
 
 
 def gradient_kernel(
-    meta_ref, sel_ref, col_scr, wgt_scr, seen_ref, tt_hbm, send_ref, miss_ref, part_ref,
-    tt_ref, grad_scr, sem,
+    meta_ref, sel_ref, col_scr, wgt_scr, seen_ref, tt_ref, send_ref, miss_ref, part_ref, grad_scr,
 ):
-    load = pltpu.make_async_copy(tt_hbm, tt_ref, sem)
-    load.start()
     rows = grad_scr.shape[0]
     per_row = LANES * 8 // rows
     columns = tt_ref.shape[1]
@@ -186,7 +189,6 @@
                 chunk * 8 : chunk * 8 + 8, :
             ]
     gradient = grad_scr[...].astype(jnp.bfloat16)
-    load.wait()
     modes = lax.dot_general(
         tt_ref[...], gradient, (((1,), (1,)), ((), ())), preferred_element_type=jnp.float32
     )
@@ -333,11 +335,11 @@
 COST = {"observe": 40, "gradient": 40, "spectral": 1, "relax": 1}
 
 
-def call(kernel, in_specs, out_shape, scratch, name):
+def call(kernel, in_specs, out_shape, scratch, name, out_specs=None):
     return pl.pallas_call(
         kernel,
         in_specs=in_specs,
-        out_specs=jax.tree.map(lambda _: VMEM, out_shape),
+        out_specs=out_specs or jax.tree.map(lambda _: VMEM, out_shape),
         out_shape=out_shape,
         scratch_shapes=scratch,
         name=name,
@@ -384,29 +386,32 @@
     small = (per_row, rows)
     dma = pltpu.SemaphoreType.DMA
 
-    sent, col_tile, wgt_tile = call(
+    sent, col_tile, wgt_tile, tt, first, last = call(
         observe_kernel,
-        [SMEM, HBM, HBM, HBM, HBM, HBM],
+        [SMEM] + [HBM] * 7,
         (
             shape((GROUP, modes_here * n_modes // LANES + 32, LANES), bf16),
             shape((rows, LANES), jnp.int32),
             shape((rows, LANES), f32),
+            shape((n_modes, columns), bf16),
+            shape((1, columns), f32),
+            shape((1, columns), f32),
         ),
-        [vmem(small, jnp.int32), vmem(small, f32), vmem(small, f32), vmem((modes_here, n_modes), bf16),
-         whole, tile, tile, dma((5,))],
+        [vmem(small, jnp.int32), vmem(small, f32), vmem(small, f32),
+         vmem((modes_here, n_modes), bf16), whole, vmem((16, columns), f32), tile, tile, dma((8,))],
         "observe",
-    )(log_weight, *map(in_hbm, (col_t, val_t, wgt_t, noise_coef[0], own)))
+    )(log_weight, *map(in_hbm, (col_t, val_t, wgt_t, noise_coef[0], own, depth_field, tt_all)))
     sent, held = lax.optimization_barrier((sent, own))
     sent = lax.all_to_all(sent, "particle", 0, 0, axis_index_groups=groups, tiled=True)
     swap = swapped(held, "particle", 0)
 
     send, miss, part = call(
         gradient_kernel,
-        [SMEM, SMEM, VMEM, VMEM, VMEM, HBM],
+        [SMEM, SMEM, VMEM, VMEM, VMEM, VMEM],
         (shape((bands, 8, LANES), bf16), shape((rows + 8, LANES), f32), shape((8, LANES), f32)),
-        [vmem((n_modes, columns), bf16), whole, dma(())],
+        [whole],
         "gradient",
-    )(meta, selection, col_tile, wgt_tile, sent, in_hbm(tt_all))
+    )(meta, selection, col_tile, wgt_tile, sent, tt)
     col_modes = lax.all_to_all(send, "space", 0, 0, tiled=True)
 
     near = jnp.where(selection[0, slot] < 1, own, swap)
@@ -419,11 +424,11 @@
         shape((bands, modes_here + 8, LANES), bf16),
         [],
         "spectral",
-    )(meta, selection, col_modes, sent, spectrum, part, tt_all, ht_all)
-    send, depth = lax.optimization_barrier((send, depth_field))
+    )(meta, selection, col_modes, sent, spectrum, part, tt, ht_all)
+    send, first, last = lax.optimization_barrier((send, first, last))
     band_modes = lax.all_to_all(send, "space", 0, 0, tiled=True)
-    above = lax.ppermute(depth[-1:], "space", [(i, i + 1) for i in range(bands - 1)])
-    below = lax.ppermute(depth[:1], "space", [(i + 1, i) for i in range(bands - 1)])
+    above = lax.ppermute(last, "space", [(i, i + 1) for i in range(bands - 1)])
+    below = lax.ppermute(first, "space", [(i + 1, i) for i in range(bands - 1)])
 
     field, part = call(
         relax_kernel,
@@ -431,7 +436,7 @@
         (shape((rows, columns), f32), shape((bands, 1, LANES), f32)),
         [tile, padded, padded, padded, whole, dma(())],
         "relax",
-    )(target, col_tile, wgt_tile, miss, in_hbm(depth_field), above, below, band_modes, tt_all)
+    )(target, col_tile, wgt_tile, miss, in_hbm(depth_field), above, below, band_modes, tt)
     parts = lax.all_to_all(part, "space", 0, 0, tiled=True)
     analysis = field + jnp.where(selection[1, slot] < 1, near, far)
     parts, analysis = lax.optimization_barrier((parts, analysis))

time: 83.6 us -> 81.4 us (0.974)
  starting transfers between devices: 46.1 us -> 44.5 us
  Pallas kernels: 12.4 us -> 11.3 us
  other arithmetic: 2.9 us -> 3.93 us
  local copies, waits for them, and re-layouts: 1.56 us -> 0.66 us
    ppermute x2, waiting for transfers between devices: 0.01 us -> 3.06 us  [the longest x1 3.06 us: per_device(): below = lax.ppermute(first, 'space', [(i + 1, i) for i in range(bands - 1)])]
    all_to_all x1, waiting for transfers between devices: 3.14 us -> 1.3 us  [per_device(): band_modes = lax.all_to_all(send, 'space', 0, 0, tiled=True)]
    all_to_all x1, starting transfers between devices: 8.19 us -> 7.05 us  [per_device(): parts = lax.all_to_all(part, 'space', 0, 0, tiled=True)]
    pallas_call x2, Pallas kernels: 6.42 us -> 5.38 us  [the longest x1 2.76 us: per_device(): call(gradient_kernel, [SMEM, SMEM, VMEM, VMEM, VMEM, VMEM], (shape((bands...]
    add x1, other arithmetic: 0.92 us -> 1.95 us  [per_device(): analysis = field + jnp.where(selection[1, slot] < 1, near, far)]
    all_to_all x1, waiting for transfers between devices: 8.42 us -> 7.39 us  [per_device(): parts = lax.all_to_all(part, 'space', 0, 0, tiled=True)]
    slice x1 -> x0, local copies, waits for them, and re-layouts: 0.89 us -> none  [per_device(): depth[:1]]
  transfers between devices with their start and end apart: 8 -> 8, of which waited for: 3 -> 5; matrix products, arithmetic and copies ran while one was open for 5% -> 5% of each run, Pallas kernels for 12% -> 11%
where the time goes in v3:
time: 81.4 us; the launch traced here: 80.8 us
  starting transfers between devices  44.5 us (55%)
  waiting for transfers between devices  17 us (21%)
  Pallas kernels  11.3 us (14%)
  other arithmetic  3.93 us (5%)
  between operations  3.32 us (4%)
    all_to_all x1, starting transfers between devices, per_device(): col_modes = lax.all_to_all(send, 'space', 0, 0, tiled=True)  11.7 us
    all_to_all x1, starting transfers between devices, per_device(): lax.all_to_all(sent, 'particle', 0, 0, axis_index_groups=groups, tiled=True)  7.82 us
    all_to_all x1, waiting for transfers between devices, per_device(): parts = lax.all_to_all(part, 'space', 0, 0, tiled=True)  7.39 us
    all_to_all x1, starting transfers between devices, per_device(): parts = lax.all_to_all(part, 'space', 0, 0, tiled=True)  7.05 us
    ppermute x2, starting transfers between devices, swapped(): return lax.ppermute(value, axis, pairs)  6.63 us
    all_to_all x1, waiting for transfers between devices, per_device(): col_modes = lax.all_to_all(send, 'space', 0, 0, tiled=True)  5.18 us
    all_to_all x1, starting transfers between devices, per_device(): band_modes = lax.all_to_all(send, 'space', 0, 0, tiled=True)  4.91 us
    ppermute x1, starting transfers between devices, per_device(): above = lax.ppermute(last, 'space', [(i, i + 1) for i in range(bands - 1)])  4.44 us
  transfers between devices with their start and end apart: 8, of which 5 were waited for; matrix products, arithmetic and copies ran while one was open for 5% of the time, Pallas kernels for 11%

profile of v3, /device:TPU:1, one launch (start us, length us, event | category | flops | bytes accessed | tf_op | source)
XLA Modules:
  0.0 80.8 jit_solution(14917869944158607076)
XLA Ops:
  1.3 0.0 copy-start.3
  1.3 0.0 copy-start
  1.3 2.6 %observe.1 = (bf16[4,96,128]{2,1,0:T(8,128)(2,1)}, s32[64,128]{1,0:T(8,128)S(1)}, f32[64,128]{1,0:T(8,128)S(1)}, bf16[512,2048]{1,0:T(8,128)(2,1)S(1)}, f32[1,2048]{1,0:T(1,128)S(1)}, /*index=5*/f32[1,2048]{1,0:T(1,128)S(1)}) custom-call(f32[1]{0:T(128)S(6)} %copy.14.lw_ref, s32[16,64]{1,0:T(8,128)} %bitcast.16, f32[16,64]{1,0:T(8,128)} %bitcast.17, ...), custom_call_target="tpu_custom_call" | custom-call | flops 40000000000 | bytes 4000000 | tf_op jit(solution)/shard_map/observe/pallas_call | solution.py:389
  3.9 7.8 %all-to-all-start = ((bf16[4,96,128]{2,1,0:T(8,128)(2,1)}), bf16[4,96,128]{2,1,0:T(8,128)(2,1)S(1)}, u32[]{:S(2)}, u32[]{:S(2)}) async-start(bf16[4,96,128]{2,1,0:T(8,128)(2,1)} %get-tuple-element.25), calls=%async_computation | async-start | bytes 196608 | tf_op jit(solution)/shard_map/all_to_all | solution.py:405
  11.7 0.0 copy-done.3
  11.8 3.4 %collective-permute-start = (f32[64,2048]{1,0:T(8,128)S(1)}, f32[64,2048]{1,0:T(8,128)}, u32[]{:S(2)}, u32[]{:S(2)}) collective-permute-start(f32[64,2048]{1,0:T(8,128)S(1)} %bitcast.14), channel_id=1, source_target_pairs={{0,32},{32,0},{64,96},{96,64},{128,160},{160,128},{192,224},{224,1... | collective-permute-start | bytes 1572872 | tf_op jit(solution)/shard_map/ppermute | solution.py:360
  15.1 0.0 copy-done
  15.1 0.6 constant_dynamic-slice_fusion
  16.4 0.1 pad_add_fusion.meta_ref
  16.5 0.1 all-to-all-done.seen_ref.noise_ref
  16.5 0.0 copy-start.1
  16.5 0.0 copy-start.2
  16.5 2.8 %gradient.1 = (bf16[32,8,128]{2,1,0:T(8,128)(2,1)}, f32[72,128]{1,0:T(8,128)S(1)}, f32[8,128]{1,0:T(8,128)S(1)}) custom-call(s32[2]{0:T(128)S(1)} %pad_add_fusion.meta_ref, s32[2,16]{1,0:T(2,128)S(1)} %copy-done, s32[64,128]{1,0:T(8,128)S(1)} %get-tuple-element.22.col_scr, f32[64,128]{1,0:T(8,128)S(1)} %get-tuple-element.23.wgt_scr, ...), custom_call_target="tpu_custom_call" | custom-call | flops 40000000000 | bytes 4000000 | tf_op jit(solution)/shard_map/gradient/pallas_call | solution.py:408
  19.3 11.7 %all-to-all-start.1 = ((bf16[32,8,128]{2,1,0:T(8,128)(2,1)}), bf16[32,8,128]{2,1,0:T(8,128)(2,1)S(1)}, u32[]{:S(2)}, u32[]{:S(2)}) async-start(bf16[32,8,128]{2,1,0:T(8,128)(2,1)} %get-tuple-element.28), calls=%async_computation.1 | async-start | bytes 131072 | tf_op jit(solution)/shard_map/all_to_all | solution.py:415
  31.0 0.0 collective-permute-done
  31.1 1.3 %broadcast_select_fusion = f32[64,2048]{1,0:T(8,128)S(1)} fusion(f32[64,2048]{1,0:T(8,128)} %collective-permute-done, pred[]{:T(512)} %bitcast.7, f32[1,64,2048]{2,1,0:T(8,128)} %param.12), kind=kLoop, calls=%fused_computation.1 | loop fusion | flops 131072 | bytes 1572865 | tf_op jit(solution)/shard_map/jit(_where)/select_n | solution.py:417
  32.3 3.3 %collective-permute-start.3 = (f32[64,2048]{1,0:T(8,128)S(1)}, f32[64,2048]{1,0:T(8,128)}, u32[]{:S(2)}, u32[]{:S(2)}) collective-permute-start(f32[64,2048]{1,0:T(8,128)S(1)} %broadcast_select_fusion), channel_id=1, source_target_pairs={{0,64},{32,96},{64,0},{96,32},{128,192},{160,224},{192,128},{224,1... | collective-permute-start | bytes 1572872 | tf_op jit(solution)/shard_map/ppermute | solution.py:360
  35.6 5.2 %all-to-all-done.1.modes_ref = bf16[32,8,128]{2,1,0:T(8,128)(2,1)S(1)} async-done(((bf16[32,8,128]{2,1,0:T(8,128)(2,1)}), bf16[32,8,128]{2,1,0:T(8,128)(2,1)S(1)}, u32[]{:S(2)}, u32[]{:S(2)}) %all-to-all-start.1) | async-done | bytes 65568 | tf_op jit(solution)/shard_map/all_to_all | solution.py:415
  40.8 0.0 copy-done.1
  40.8 0.0 copy-done.2
  40.8 2.6 %spectral.1 = bf16[32,24,128]{2,1,0:T(8,128)(2,1)} custom-call(s32[2]{0:T(128)S(1)} %pad_add_fusion.meta_ref, s32[2,16]{1,0:T(2,128)S(1)} %copy-done, bf16[32,8,128]{2,1,0:T(8,128)(2,1)S(1)} %all-to-all-done.1.modes_ref, bf16[4,96,128]{2,1,0:T(8,128)(2,1)S(1)} %all-to-all-done.seen_ref.noise_ref, f32[16,512]{1,0:T(8,128)S(1)} %copy-done.1, ...), custom_call_target="tpu_custom_call" | custom-call | flops 1000000000 | bytes 4000000 | tf_op jit(solution)/shard_map/spectral/pallas_call | solution.py:421
  43.4 4.9 %all-to-all-start.2 = ((bf16[32,24,128]{2,1,0:T(8,128)(2,1)}), bf16[32,24,128]{2,1,0:T(8,128)(2,1)S(1)}, u32[]{:S(2)}, u32[]{:S(2)}) async-start(bf16[32,24,128]{2,1,0:T(8,128)(2,1)} %spectral.1), calls=%async_computation.2 | async-start | bytes 393216 | tf_op jit(solution)/shard_map/all_to_all | solution.py:429
  48.3 4.4 %collective-permute-start.1 = (f32[1,2048]{1,0:T(1,128)S(1)}, f32[1,2048]{1,0:T(1,128)S(1)}, u32[]{:S(2)}, u32[]{:S(2)}) collective-permute-start(f32[1,2048]{1,0:T(1,128)S(1)} %get-tuple-element.34), channel_id=1, source_target_pairs={{0,1},{1,2},{2,3},{3,4},{4,5},{5,6},{6,7},{7,8},{8,9},{9,10},{10,1... | collective-permute-start | bytes 24584 | tf_op jit(solution)/shard_map/ppermute | solution.py:430
  52.7 1.9 %collective-permute-start.2 = (f32[1,2048]{1,0:T(1,128)S(1)}, f32[1,2048]{1,0:T(1,128)S(1)}, u32[]{:S(2)}, u32[]{:S(2)}) collective-permute-start(f32[1,2048]{1,0:T(1,128)S(1)} %get-tuple-element.35), channel_id=1, source_target_pairs={{1,0},{2,1},{3,2},{4,3},{5,4},{6,5},{7,6},{8,7},{9,8},{10,9},{11,1... | collective-permute-start | bytes 24584 | tf_op jit(solution)/shard_map/ppermute | solution.py:431
  55.9 0.0 collective-permute-done.1.above_ref
  56.0 3.1 %collective-permute-done.2.below_ref = f32[1,2048]{1,0:T(1,128)S(1)} collective-permute-done((f32[1,2048]{1,0:T(1,128)S(1)}, f32[1,2048]{1,0:T(1,128)S(1)}, u32[]{:S(2)}, u32[]{:S(2)}) %collective-permute-start.2) | collective-permute-done | bytes 8224 | tf_op jit(solution)/shard_map/ppermute | solution.py:431
  59.0 1.3 %all-to-all-done.2.modes_ref = bf16[32,24,128]{2,1,0:T(8,128)(2,1)S(1)} async-done(((bf16[32,24,128]{2,1,0:T(8,128)(2,1)}), bf16[32,24,128]{2,1,0:T(8,128)(2,1)S(1)}, u32[]{:S(2)}, u32[]{:S(2)}) %all-to-all-start.2) | async-done | bytes 196640 | tf_op jit(solution)/shard_map/all_to_all | solution.py:429
  60.3 3.4 %relax.1 = (f32[64,2048]{1,0:T(8,128)S(1)}, f32[32,1,128]{2,1,0:T(1,128)}) custom-call(f32[1]{0:T(128)S(6)} %copy.15.target_ref, s32[64,128]{1,0:T(8,128)S(1)} %get-tuple-element.22.col_scr, f32[64,128]{1,0:T(8,128)S(1)} %get-tuple-element.23.wgt_scr, f32[72,128]{1,0:T(8,128)S(1)} %get-tuple-element.27.miss_ref, f32[64,2048]{1,0:T(8,128)} %depth_hbm.3, ...), custom_call_target="tpu_custom_call" | custom-call | flops 1000000000 | bytes 4000000 | tf_op jit(solution)/shard_map/relax/pallas_call | solution.py:433
  63.7 7.1 %all-to-all-start.3 = ((f32[32,1,128]{2,1,0:T(1,128)}), f32[32,1,128]{2,1,0:T(1,128)S(1)}, u32[]{:S(2)}, u32[]{:S(2)}) async-start(f32[32,1,128]{2,1,0:T(1,128)} %get-tuple-element.37), calls=%async_computation.3 | async-start | bytes 32768 | tf_op jit(solution)/shard_map/all_to_all | solution.py:440
  70.8 0.0 collective-permute-done.3
  70.8 2.0 %select_add_fusion = f32[64,2048]{1,0:T(8,128)} fusion(f32[64,2048]{1,0:T(8,128)S(1)} %get-tuple-element.38, f32[64,2048]{1,0:T(8,128)S(1)} %broadcast_select_fusion, f32[64,2048]{1,0:T(8,128)} %collective-permute-done.3, pred[]{:T(512)} %bitcast.8), kind=kLoop, calls=%fused_computation | loop fusion | flops 262144 | bytes 2097153 | tf_op jit(solution)/shard_map/add | solution.py:441
  72.7 7.4 %all-to-all-done.3 = f32[32,1,128]{2,1,0:T(1,128)S(1)} async-done(((f32[32,1,128]{2,1,0:T(1,128)}), f32[32,1,128]{2,1,0:T(1,128)S(1)}, u32[]{:S(2)}, u32[]{:S(2)}) %all-to-all-start.3) | async-done | bytes 16416 | tf_op jit(solution)/shard_map/all_to_all | solution.py:440
  80.1 0.6 slice_reduce_fusion
Async XLA Ops:
  1.3 10.5 %copy-start.3 = (f32[1,64,2048]{2,1,0:T(8,128)S(1)}, f32[1,64,2048]{2,1,0:T(8,128)}, u32[]{:S(2)}) copy-start(f32[1,64,2048]{2,1,0:T(8,128)} %param.12) | copy-start | bytes 1572868
  1.3 13.8 %copy-start = (s32[2,16]{1,0:T(2,128)S(1)}, s32[2,16]{1,0:T(2,128)}, u32[]{:S(2)}) copy-start(s32[2,16]{1,0:T(2,128)} %sel_ref.3) | copy-start | bytes 388
  3.9 12.6 %all-to-all-start = ((bf16[4,96,128]{2,1,0:T(8,128)(2,1)}), bf16[4,96,128]{2,1,0:T(8,128)(2,1)S(1)}, u32[]{:S(2)}, u32[]{:S(2)}) async-start(bf16[4,96,128]{2,1,0:T(8,128)(2,1)} %get-tuple-element.25), calls=%async_computation | async-start | bytes 196608 | tf_op jit(solution)/shard_map/all_to_all | solution.py:405
  11.8 19.3 %collective-permute-start = (f32[64,2048]{1,0:T(8,128)S(1)}, f32[64,2048]{1,0:T(8,128)}, u32[]{:S(2)}, u32[]{:S(2)}) collective-permute-start(f32[64,2048]{1,0:T(8,128)S(1)} %bitcast.14), channel_id=1, source_target_pairs={{0,32},{32,0},{64,96},{96,64},{128,160},{160,128},{192,224},{224,1... | collective-permute-start | bytes 1572872 | tf_op jit(solution)/shard_map/ppermute | solution.py:360
  16.5 24.3 %copy-start.1 = (f32[16,512]{1,0:T(8,128)S(1)}, f32[16,512]{1,0:T(8,128)}, u32[]{:S(2)}) copy-start(f32[16,512]{1,0:T(8,128)} %spec_ref.1) | copy-start | bytes 98308
  16.5 24.3 %copy-start.2 = (bf16[256,512]{1,0:T(8,128)(2,1)S(1)}, bf16[256,512]{1,0:T(8,128)(2,1)}, u32[]{:S(2)}) copy-start(bf16[256,512]{1,0:T(8,128)(2,1)} %constant.25.clone.ht_ref) | copy-start | bytes 786436
  19.3 21.5 %all-to-all-start.1 = ((bf16[32,8,128]{2,1,0:T(8,128)(2,1)}), bf16[32,8,128]{2,1,0:T(8,128)(2,1)S(1)}, u32[]{:S(2)}, u32[]{:S(2)}) async-start(bf16[32,8,128]{2,1,0:T(8,128)(2,1)} %get-tuple-element.28), calls=%async_computation.1 | async-start | bytes 131072 | tf_op jit(solution)/shard_map/all_to_all | solution.py:415
  32.3 38.5 %collective-permute-start.3 = (f32[64,2048]{1,0:T(8,128)S(1)}, f32[64,2048]{1,0:T(8,128)}, u32[]{:S(2)}, u32[]{:S(2)}) collective-permute-start(f32[64,2048]{1,0:T(8,128)S(1)} %broadcast_select_fusion), channel_id=1, source_target_pairs={{0,64},{32,96},{64,0},{96,32},{128,192},{160,224},{192,128},{224,1... | collective-permute-start | bytes 1572872 | tf_op jit(solution)/shard_map/ppermute | solution.py:360
  43.4 16.9 %all-to-all-start.2 = ((bf16[32,24,128]{2,1,0:T(8,128)(2,1)}), bf16[32,24,128]{2,1,0:T(8,128)(2,1)S(1)}, u32[]{:S(2)}, u32[]{:S(2)}) async-start(bf16[32,24,128]{2,1,0:T(8,128)(2,1)} %spectral.1), calls=%async_computation.2 | async-start | bytes 393216 | tf_op jit(solution)/shard_map/all_to_all | solution.py:429
  48.3 7.7 %collective-permute-start.1 = (f32[1,2048]{1,0:T(1,128)S(1)}, f32[1,2048]{1,0:T(1,128)S(1)}, u32[]{:S(2)}, u32[]{:S(2)}) collective-permute-start(f32[1,2048]{1,0:T(1,128)S(1)} %get-tuple-element.34), channel_id=1, source_target_pairs={{0,1},{1,2},{2,3},{3,4},{4,5},{5,6},{6,7},{7,8},{8,9},{9,10},{10,1... | collective-permute-start | bytes 24584 | tf_op jit(solution)/shard_map/ppermute | solution.py:430
  52.7 6.3 %collective-permute-start.2 = (f32[1,2048]{1,0:T(1,128)S(1)}, f32[1,2048]{1,0:T(1,128)S(1)}, u32[]{:S(2)}, u32[]{:S(2)}) collective-permute-start(f32[1,2048]{1,0:T(1,128)S(1)} %get-tuple-element.35), channel_id=1, source_target_pairs={{1,0},{2,1},{3,2},{4,3},{5,4},{6,5},{7,6},{8,7},{9,8},{10,9},{11,1... | collective-permute-start | bytes 24584 | tf_op jit(solution)/shard_map/ppermute | solution.py:431
  63.7 16.4 %all-to-all-start.3 = ((f32[32,1,128]{2,1,0:T(1,128)}), f32[32,1,128]{2,1,0:T(1,128)S(1)}, u32[]{:S(2)}, u32[]{:S(2)}) async-start(f32[32,1,128]{2,1,0:T(1,128)} %get-tuple-element.37), calls=%async_computation.3 | async-start | bytes 32768 | tf_op jit(solution)/shard_map/all_to_all | solution.py:440

commit v4 on v3

--- a/solution.py
+++ b/solution.py
@@ -31,7 +31,7 @@
     width = rows // bands
     out = np.zeros((bands, 2, 4, y_table.shape[1]), dtype=y_table.dtype)
     for band in range(bands):
-        for at, row in enumerate((-2, -1, width, width + 1)):
+        for at, row in enumerate((width, width + 1, -2, -1)):
             source = band * width + row
             if 0 <= source < rows:
                 out[band, :, at] = y_table[source]
@@ -40,6 +40,10 @@
 
 def lane_iota():
     return lax.broadcasted_iota(jnp.int32, (8, LANES), 1)
+
+
+def summed(values):
+    return jnp.sum(jnp.sum(values, axis=0, keepdims=True), axis=1, keepdims=True)
 
 
 def split3(value):
@@ -152,7 +156,7 @@
     mismatch = jnp.concatenate(tiles, axis=0)
     miss_ref[0:rows, :] = mismatch
     weighted = wgt_scr[...] * mismatch
-    part_ref[...] = jnp.full((8, LANES), 0.5 * jnp.sum(weighted * mismatch), jnp.float32)
+    part_ref[...] = jnp.broadcast_to(0.5 * summed(weighted * mismatch), (8, LANES))
 
     def repeated(tile):
         step = per_row
@@ -223,7 +227,7 @@
     )
     scaled = norm_factor * spec_ref[...]
     weighted = coefficients * scaled
-    energy = jnp.sum(coefficients * weighted)
+    energy = summed(coefficients * weighted)
     noise = noise_ref[position][0 : noise_ref.shape[1] - 32, :]
     noise = jnp.concatenate(
         [noise[at : at + modes_here] for at in range(0, noise.shape[0], modes_here)], axis=1
@@ -256,7 +260,7 @@
     placed = jnp.where(row8 < 4, as_first, as_second)
     pieces = jnp.zeros((8, LANES), jnp.float32)
     row = lax.broadcasted_iota(jnp.int32, (8, LANES), 0)
-    energy = jnp.full((8, LANES), energy, jnp.float32)
+    energy = jnp.broadcast_to(energy, (8, LANES))
     for at_row, piece in enumerate(split3(part_ref[...]) + split3(energy)):
         pieces = jnp.where(row == at_row, piece, pieces)
     pieces = jnp.broadcast_to(pieces[None], (bands, 8, LANES))
@@ -292,39 +296,53 @@
         quads.append(total)
     halo = jnp.concatenate(quads, axis=1)
     row = lax.broadcasted_iota(jnp.int32, (8, LANES), 0)
-    misfit = jnp.sum(jnp.where(row < 3, scalars, 0.0))
-    energy = jnp.sum(jnp.where((row >= 3) & (row < 6), scalars, 0.0))
-    weight = jnp.max(miss_ref[rows:, :])
-    misfit_v = jnp.full((8, LANES), misfit + weight - target_ref[0], jnp.float32)
-    step = (misfit_v / jnp.full((8, LANES), energy + 1.0, jnp.float32))[0:1, 0:1]
+    misfit = summed(jnp.where(row < 3, scalars, 0.0))
+    energy = summed(jnp.where((row >= 3) & (row < 6), scalars, 0.0))
+    weight = miss_ref[rows : rows + 1, 0:1]
+    step = (misfit + weight - target_ref[0]) / (energy + 1.0)
     main = modes_ref[:, 0:modes_here, :].reshape(n_modes, LANES)
-    left = jnp.concatenate([main.astype(jnp.float32).T, halo], axis=0).astype(jnp.bfloat16)
-    pulled = jnp.dot(left, tt_ref[...], preferred_element_type=jnp.float32)
-    inc_scr[8 : 8 + rows, :] = step * pulled[0:rows] + NOISE_AMP * pulled[rows : 2 * rows]
-    edge = step * pulled[2 * rows : 2 * rows + 4] + NOISE_AMP * pulled[2 * rows + 4 : 2 * rows + 8]
-    inc_scr[6:8, :] = edge[0:2]
-    inc_scr[8 + rows : 10 + rows, :] = edge[2:4]
-
+    pulled = lax.dot_general(main, tt_ref[...], (((0,), (0,)), ((), ())), preferred_element_type=jnp.float32)
+    pulled_h = jnp.dot(halo.astype(jnp.bfloat16), tt_ref[...], preferred_element_type=jnp.float32)
+    for at in range(0, rows, 8):
+        inc_scr[at : at + 8, :] = step * pulled[at : at + 8] + NOISE_AMP * pulled[rows + at : rows + at + 8]
+    edge = pulled_h
+    edge = step * edge + NOISE_AMP * pltpu.roll(edge, 4, axis=0)
+    row8 = lax.broadcasted_iota(jnp.int32, (8, columns), 0)
+    inc_scr[rows:, :] = jnp.where(row8 < 2, edge, jnp.where(row8 < 6, 0.0, pltpu.roll(edge, 4, axis=0)))
     depth.wait()
-    rate_ref[7:8, :] = rate(above_ref[...])
-    rate_ref[8 : 8 + rows, :] = rate(depth_ref[...])
-    rate_ref[8 + rows : 9 + rows, :] = rate(below_ref[...])
-
-    def beside(values):
-        return pltpu.roll(values, 1, axis=1) + pltpu.roll(values, columns - 1, axis=1)
-
-    here = inc_scr[7 : 9 + rows, :]
-    around = inc_scr[6 : 8 + rows, :] + inc_scr[8 : 10 + rows, :] + beside(here)
-    one_scr[7 : 9 + rows, :] = (1.0 - RELAX_RATE) * here + rate_ref[7 : 9 + rows, :] * (around - here)
-    here = one_scr[8 : 8 + rows, :]
-    around = one_scr[7 : 7 + rows, :] + one_scr[9 : 9 + rows, :] + beside(here)
-    field_ref[...] = (1.0 - RELAX_RATE) * here + rate_ref[8 : 8 + rows, :] * (
-        around - inc_scr[8 : 8 + rows, :]
-    )
+
+    def rate(depth):
+        return RELAX_RATE * depth / (4.0 * depth + STRETCH)
+
+    rate_ref[rows:, :] = jnp.where(
+        row8 == 0, rate(below_ref[...]), jnp.where(row8 == 7, rate(above_ref[...]), 0.0)
+    )
+    for at in range(0, rows, 8):
+        rate_ref[at : at + 8, :] = rate(depth_ref[at : at + 8, :])
+    length = rows + 8
+
+    def relaxed(source_ref, at):
+        here = source_ref[at : at + 8, :]
+        before = source_ref[(at - 8) % length : (at - 8) % length + 8, :]
+        after = source_ref[(at + 8) % length : (at + 8) % length + 8, :]
+        around = (
+            pltpu.roll(jnp.where(row8 == 7, before, here), 1, axis=0)
+            + pltpu.roll(jnp.where(row8 == 0, after, here), 7, axis=0)
+            + pltpu.roll(here, 1, axis=1)
+            + pltpu.roll(here, columns - 1, axis=1)
+        )
+        return (1.0 - RELAX_RATE) * here + rate_ref[at : at + 8, :] * (
+            around - inc_scr[at : at + 8, :]
+        )
+
+    for at in range(0, length, 8):
+        one_scr[at : at + 8, :] = relaxed(inc_scr, at)
+    for at in range(0, rows, 8):
+        field_ref[at : at + 8, :] = relaxed(one_scr, at)
     gather_rows(field_ref, col_scr, seen_scr)
     left_over = miss_ref[0:rows, :] - seen_scr[...]
-    part = 0.5 * jnp.sum(wgt_scr[...] * left_over * left_over)
-    part_ref[...] = jnp.full(part_ref.shape, part, jnp.float32)
+    part = 0.5 * summed(wgt_scr[...] * left_over * left_over)
+    part_ref[...] = jnp.broadcast_to(part[None], part_ref.shape)
 
 
 SMEM = pl.BlockSpec(memory_space=pltpu.SMEM)
@@ -382,7 +400,7 @@
     vmem = pltpu.VMEM
     tile = vmem((rows, LANES), f32)
     whole = vmem((rows, columns), f32)
-    padded = vmem((rows + 16, columns), f32)
+    padded = vmem((rows + 8, columns), f32)
     small = (per_row, rows)
     dma = pltpu.SemaphoreType.DMA
 

time: 81.4 us -> 81 us (level)
  transfers between devices with their start and end apart: 8 -> 8, of which waited for: 5 -> 5; matrix products, arithmetic and copies ran while one was open for 5% -> 5% of each run, Pallas kernels for 11% -> 10%
where the time goes in v4:
time: 81 us; the launch traced here: 80.3 us
  starting transfers between devices  44.4 us (55%)
  waiting for transfers between devices  17.1 us (21%)
  Pallas kernels  10.9 us (13%)
  other arithmetic  3.93 us (5%)
  between operations  3.32 us (4%)
    all_to_all x1, starting transfers between devices, per_device(): col_modes = lax.all_to_all(send, 'space', 0, 0, tiled=True)  11.7 us
    all_to_all x1, starting transfers between devices, per_device(): lax.all_to_all(sent, 'particle', 0, 0, axis_index_groups=groups, tiled=True)  7.82 us
    all_to_all x1, waiting for transfers between devices, per_device(): parts = lax.all_to_all(part, 'space', 0, 0, tiled=True)  7.39 us
    all_to_all x1, starting transfers between devices, per_device(): parts = lax.all_to_all(part, 'space', 0, 0, tiled=True)  6.9 us
    ppermute x2, starting transfers between devices, swapped(): return lax.ppermute(value, axis, pairs)  6.63 us
    all_to_all x1, waiting for transfers between devices, per_device(): col_modes = lax.all_to_all(send, 'space', 0, 0, tiled=True)  5.18 us
    all_to_all x1, starting transfers between devices, per_device(): band_modes = lax.all_to_all(send, 'space', 0, 0, tiled=True)  4.91 us
    ppermute x1, starting transfers between devices, per_device(): above = lax.ppermute(last, 'space', [(i, i + 1) for i in range(bands - 1)])  4.44 us
  transfers between devices with their start and end apart: 8, of which 5 were waited for; matrix products, arithmetic and copies ran while one was open for 5% of the time, Pallas kernels for 10%

profile of v4, /device:TPU:1, one launch (start us, length us, event | category | flops | bytes accessed | tf_op | source)
XLA Modules:
  0.0 80.3 jit_solution(18219825588907790364)
XLA Ops:
  1.3 0.0 copy-start.3
  1.3 0.0 copy-start
  1.3 2.6 %observe.1 = (bf16[4,96,128]{2,1,0:T(8,128)(2,1)}, s32[64,128]{1,0:T(8,128)S(1)}, f32[64,128]{1,0:T(8,128)S(1)}, bf16[512,2048]{1,0:T(8,128)(2,1)S(1)}, f32[1,2048]{1,0:T(1,128)S(1)}, /*index=5*/f32[1,2048]{1,0:T(1,128)S(1)}) custom-call(f32[1]{0:T(128)S(6)} %copy.14.lw_ref, s32[16,64]{1,0:T(8,128)} %bitcast.16, f32[16,64]{1,0:T(8,128)} %bitcast.17, ...), custom_call_target="tpu_custom_call" | custom-call | flops 40000000000 | bytes 4000000 | tf_op jit(solution)/shard_map/observe/pallas_call | solution.py:407
  3.9 7.8 %all-to-all-start = ((bf16[4,96,128]{2,1,0:T(8,128)(2,1)}), bf16[4,96,128]{2,1,0:T(8,128)(2,1)S(1)}, u32[]{:S(2)}, u32[]{:S(2)}) async-start(bf16[4,96,128]{2,1,0:T(8,128)(2,1)} %get-tuple-element.25), calls=%async_computation | async-start | bytes 196608 | tf_op jit(solution)/shard_map/all_to_all | solution.py:423
  11.7 0.0 copy-done.3
  11.8 3.4 %collective-permute-start = (f32[64,2048]{1,0:T(8,128)S(1)}, f32[64,2048]{1,0:T(8,128)}, u32[]{:S(2)}, u32[]{:S(2)}) collective-permute-start(f32[64,2048]{1,0:T(8,128)S(1)} %bitcast.14), channel_id=1, source_target_pairs={{0,32},{32,0},{64,96},{96,64},{128,160},{160,128},{192,224},{224,1... | collective-permute-start | bytes 1572872 | tf_op jit(solution)/shard_map/ppermute | solution.py:378
  15.1 0.0 copy-done
  15.1 0.6 constant_dynamic-slice_fusion
  16.4 0.1 pad_add_fusion.meta_ref
  16.5 0.1 all-to-all-done.seen_ref.noise_ref
  16.5 0.0 copy-start.1
  16.5 0.0 copy-start.2
  16.5 2.8 %gradient.1 = (bf16[32,8,128]{2,1,0:T(8,128)(2,1)}, f32[72,128]{1,0:T(8,128)S(1)}, f32[8,128]{1,0:T(8,128)S(1)}) custom-call(s32[2]{0:T(128)S(1)} %pad_add_fusion.meta_ref, s32[2,16]{1,0:T(2,128)S(1)} %copy-done, s32[64,128]{1,0:T(8,128)S(1)} %get-tuple-element.22.col_scr, f32[64,128]{1,0:T(8,128)S(1)} %get-tuple-element.23.wgt_scr, ...), custom_call_target="tpu_custom_call" | custom-call | flops 40000000000 | bytes 4000000 | tf_op jit(solution)/shard_map/gradient/pallas_call | solution.py:426
  19.3 11.7 %all-to-all-start.1 = ((bf16[32,8,128]{2,1,0:T(8,128)(2,1)}), bf16[32,8,128]{2,1,0:T(8,128)(2,1)S(1)}, u32[]{:S(2)}, u32[]{:S(2)}) async-start(bf16[32,8,128]{2,1,0:T(8,128)(2,1)} %get-tuple-element.28), calls=%async_computation.1 | async-start | bytes 131072 | tf_op jit(solution)/shard_map/all_to_all | solution.py:433
  31.0 0.0 collective-permute-done
  31.0 1.3 %broadcast_select_fusion = f32[64,2048]{1,0:T(8,128)S(1)} fusion(f32[64,2048]{1,0:T(8,128)} %collective-permute-done, pred[]{:T(512)} %bitcast.7, f32[1,64,2048]{2,1,0:T(8,128)} %param.12), kind=kLoop, calls=%fused_computation.1 | loop fusion | flops 131072 | bytes 1572865 | tf_op jit(solution)/shard_map/jit(_where)/select_n | solution.py:435
  32.3 3.3 %collective-permute-start.3 = (f32[64,2048]{1,0:T(8,128)S(1)}, f32[64,2048]{1,0:T(8,128)}, u32[]{:S(2)}, u32[]{:S(2)}) collective-permute-start(f32[64,2048]{1,0:T(8,128)S(1)} %broadcast_select_fusion), channel_id=1, source_target_pairs={{0,64},{32,96},{64,0},{96,32},{128,192},{160,224},{192,128},{224,1... | collective-permute-start | bytes 1572872 | tf_op jit(solution)/shard_map/ppermute | solution.py:378
  35.6 5.2 %all-to-all-done.1.modes_ref = bf16[32,8,128]{2,1,0:T(8,128)(2,1)S(1)} async-done(((bf16[32,8,128]{2,1,0:T(8,128)(2,1)}), bf16[32,8,128]{2,1,0:T(8,128)(2,1)S(1)}, u32[]{:S(2)}, u32[]{:S(2)}) %all-to-all-start.1) | async-done | bytes 65568 | tf_op jit(solution)/shard_map/all_to_all | solution.py:433
  40.8 0.0 copy-done.1
  40.8 0.0 copy-done.2
  40.8 2.6 %spectral.1 = bf16[32,24,128]{2,1,0:T(8,128)(2,1)} custom-call(s32[2]{0:T(128)S(1)} %pad_add_fusion.meta_ref, s32[2,16]{1,0:T(2,128)S(1)} %copy-done, bf16[32,8,128]{2,1,0:T(8,128)(2,1)S(1)} %all-to-all-done.1.modes_ref, bf16[4,96,128]{2,1,0:T(8,128)(2,1)S(1)} %all-to-all-done.seen_ref.noise_ref, f32[16,512]{1,0:T(8,128)S(1)} %copy-done.1, ...), custom_call_target="tpu_custom_call" | custom-call | flops 1000000000 | bytes 4000000 | tf_op jit(solution)/shard_map/spectral/pallas_call | solution.py:439
  43.4 4.9 %all-to-all-start.2 = ((bf16[32,24,128]{2,1,0:T(8,128)(2,1)}), bf16[32,24,128]{2,1,0:T(8,128)(2,1)S(1)}, u32[]{:S(2)}, u32[]{:S(2)}) async-start(bf16[32,24,128]{2,1,0:T(8,128)(2,1)} %spectral.1), calls=%async_computation.2 | async-start | bytes 393216 | tf_op jit(solution)/shard_map/all_to_all | solution.py:447
  48.3 4.4 %collective-permute-start.1 = (f32[1,2048]{1,0:T(1,128)S(1)}, f32[1,2048]{1,0:T(1,128)S(1)}, u32[]{:S(2)}, u32[]{:S(2)}) collective-permute-start(f32[1,2048]{1,0:T(1,128)S(1)} %get-tuple-element.34), channel_id=1, source_target_pairs={{0,1},{1,2},{2,3},{3,4},{4,5},{5,6},{6,7},{7,8},{8,9},{9,10},{10,1... | collective-permute-start | bytes 24584 | tf_op jit(solution)/shard_map/ppermute | solution.py:448
  52.7 1.9 %collective-permute-start.2 = (f32[1,2048]{1,0:T(1,128)S(1)}, f32[1,2048]{1,0:T(1,128)S(1)}, u32[]{:S(2)}, u32[]{:S(2)}) collective-permute-start(f32[1,2048]{1,0:T(1,128)S(1)} %get-tuple-element.35), channel_id=1, source_target_pairs={{1,0},{2,1},{3,2},{4,3},{5,4},{6,5},{7,6},{8,7},{9,8},{10,9},{11,1... | collective-permute-start | bytes 24584 | tf_op jit(solution)/shard_map/ppermute | solution.py:449
  55.9 0.0 collective-permute-done.1.above_ref
  55.9 3.1 %collective-permute-done.2.below_ref = f32[1,2048]{1,0:T(1,128)S(1)} collective-permute-done((f32[1,2048]{1,0:T(1,128)S(1)}, f32[1,2048]{1,0:T(1,128)S(1)}, u32[]{:S(2)}, u32[]{:S(2)}) %collective-permute-start.2) | collective-permute-done | bytes 8224 | tf_op jit(solution)/shard_map/ppermute | solution.py:449
  59.0 1.5 %all-to-all-done.2.modes_ref = bf16[32,24,128]{2,1,0:T(8,128)(2,1)S(1)} async-done(((bf16[32,24,128]{2,1,0:T(8,128)(2,1)}), bf16[32,24,128]{2,1,0:T(8,128)(2,1)S(1)}, u32[]{:S(2)}, u32[]{:S(2)}) %all-to-all-start.2) | async-done | bytes 196640 | tf_op jit(solution)/shard_map/all_to_all | solution.py:447
  60.5 3.0 %relax.1 = (f32[64,2048]{1,0:T(8,128)S(1)}, f32[32,1,128]{2,1,0:T(1,128)}) custom-call(f32[1]{0:T(128)S(6)} %copy.15.target_ref, s32[64,128]{1,0:T(8,128)S(1)} %get-tuple-element.22.col_scr, f32[64,128]{1,0:T(8,128)S(1)} %get-tuple-element.23.wgt_scr, f32[72,128]{1,0:T(8,128)S(1)} %get-tuple-element.27.miss_ref, f32[64,2048]{1,0:T(8,128)} %depth_hbm.3, ...), custom_call_target="tpu_custom_call" | custom-call | flops 1000000000 | bytes 4000000 | tf_op jit(solution)/shard_map/relax/pallas_call | solution.py:451
  63.4 6.9 %all-to-all-start.3 = ((f32[32,1,128]{2,1,0:T(1,128)}), f32[32,1,128]{2,1,0:T(1,128)S(1)}, u32[]{:S(2)}, u32[]{:S(2)}) async-start(f32[32,1,128]{2,1,0:T(1,128)} %get-tuple-element.37), calls=%async_computation.3 | async-start | bytes 32768 | tf_op jit(solution)/shard_map/all_to_all | solution.py:458
  70.3 0.0 collective-permute-done.3
  70.3 2.0 %select_add_fusion = f32[64,2048]{1,0:T(8,128)} fusion(f32[64,2048]{1,0:T(8,128)S(1)} %get-tuple-element.38, f32[64,2048]{1,0:T(8,128)S(1)} %broadcast_select_fusion, f32[64,2048]{1,0:T(8,128)} %collective-permute-done.3, pred[]{:T(512)} %bitcast.8), kind=kLoop, calls=%fused_computation | loop fusion | flops 262144 | bytes 2097153 | tf_op jit(solution)/shard_map/add | solution.py:459
  72.3 7.4 %all-to-all-done.3 = f32[32,1,128]{2,1,0:T(1,128)S(1)} async-done(((f32[32,1,128]{2,1,0:T(1,128)}), f32[32,1,128]{2,1,0:T(1,128)S(1)}, u32[]{:S(2)}, u32[]{:S(2)}) %all-to-all-start.3) | async-done | bytes 16416 | tf_op jit(solution)/shard_map/all_to_all | solution.py:458
  79.7 0.6 slice_reduce_fusion
Async XLA Ops:
  1.3 10.5 %copy-start.3 = (f32[1,64,2048]{2,1,0:T(8,128)S(1)}, f32[1,64,2048]{2,1,0:T(8,128)}, u32[]{:S(2)}) copy-start(f32[1,64,2048]{2,1,0:T(8,128)} %param.12) | copy-start | bytes 1572868
  1.3 13.8 %copy-start = (s32[2,16]{1,0:T(2,128)S(1)}, s32[2,16]{1,0:T(2,128)}, u32[]{:S(2)}) copy-start(s32[2,16]{1,0:T(2,128)} %sel_ref.3) | copy-start | bytes 388
  3.9 12.6 %all-to-all-start = ((bf16[4,96,128]{2,1,0:T(8,128)(2,1)}), bf16[4,96,128]{2,1,0:T(8,128)(2,1)S(1)}, u32[]{:S(2)}, u32[]{:S(2)}) async-start(bf16[4,96,128]{2,1,0:T(8,128)(2,1)} %get-tuple-element.25), calls=%async_computation | async-start | bytes 196608 | tf_op jit(solution)/shard_map/all_to_all | solution.py:423
  11.8 19.3 %collective-permute-start = (f32[64,2048]{1,0:T(8,128)S(1)}, f32[64,2048]{1,0:T(8,128)}, u32[]{:S(2)}, u32[]{:S(2)}) collective-permute-start(f32[64,2048]{1,0:T(8,128)S(1)} %bitcast.14), channel_id=1, source_target_pairs={{0,32},{32,0},{64,96},{96,64},{128,160},{160,128},{192,224},{224,1... | collective-permute-start | bytes 1572872 | tf_op jit(solution)/shard_map/ppermute | solution.py:378
  16.5 24.2 %copy-start.1 = (f32[16,512]{1,0:T(8,128)S(1)}, f32[16,512]{1,0:T(8,128)}, u32[]{:S(2)}) copy-start(f32[16,512]{1,0:T(8,128)} %spec_ref.1) | copy-start | bytes 98308
  16.5 24.2 %copy-start.2 = (bf16[256,512]{1,0:T(8,128)(2,1)S(1)}, bf16[256,512]{1,0:T(8,128)(2,1)}, u32[]{:S(2)}) copy-start(bf16[256,512]{1,0:T(8,128)(2,1)} %constant.25.clone.ht_ref) | copy-start | bytes 786436
  19.3 21.5 %all-to-all-start.1 = ((bf16[32,8,128]{2,1,0:T(8,128)(2,1)}), bf16[32,8,128]{2,1,0:T(8,128)(2,1)S(1)}, u32[]{:S(2)}, u32[]{:S(2)}) async-start(bf16[32,8,128]{2,1,0:T(8,128)(2,1)} %get-tuple-element.28), calls=%async_computation.1 | async-start | bytes 131072 | tf_op jit(solution)/shard_map/all_to_all | solution.py:433
  32.3 38.0 %collective-permute-start.3 = (f32[64,2048]{1,0:T(8,128)S(1)}, f32[64,2048]{1,0:T(8,128)}, u32[]{:S(2)}, u32[]{:S(2)}) collective-permute-start(f32[64,2048]{1,0:T(8,128)S(1)} %broadcast_select_fusion), channel_id=1, source_target_pairs={{0,64},{32,96},{64,0},{96,32},{128,192},{160,224},{192,128},{224,1... | collective-permute-start | bytes 1572872 | tf_op jit(solution)/shard_map/ppermute | solution.py:378
  43.4 17.1 %all-to-all-start.2 = ((bf16[32,24,128]{2,1,0:T(8,128)(2,1)}), bf16[32,24,128]{2,1,0:T(8,128)(2,1)S(1)}, u32[]{:S(2)}, u32[]{:S(2)}) async-start(bf16[32,24,128]{2,1,0:T(8,128)(2,1)} %spectral.1), calls=%async_computation.2 | async-start | bytes 393216 | tf_op jit(solution)/shard_map/all_to_all | solution.py:447
  48.3 7.7 %collective-permute-start.1 = (f32[1,2048]{1,0:T(1,128)S(1)}, f32[1,2048]{1,0:T(1,128)S(1)}, u32[]{:S(2)}, u32[]{:S(2)}) collective-permute-start(f32[1,2048]{1,0:T(1,128)S(1)} %get-tuple-element.34), channel_id=1, source_target_pairs={{0,1},{1,2},{2,3},{3,4},{4,5},{5,6},{6,7},{7,8},{8,9},{9,10},{10,1... | collective-permute-start | bytes 24584 | tf_op jit(solution)/shard_map/ppermute | solution.py:448
  52.7 6.3 %collective-permute-start.2 = (f32[1,2048]{1,0:T(1,128)S(1)}, f32[1,2048]{1,0:T(1,128)S(1)}, u32[]{:S(2)}, u32[]{:S(2)}) collective-permute-start(f32[1,2048]{1,0:T(1,128)S(1)} %get-tuple-element.35), channel_id=1, source_target_pairs={{1,0},{2,1},{3,2},{4,3},{5,4},{6,5},{7,6},{8,7},{9,8},{10,9},{11,1... | collective-permute-start | bytes 24584 | tf_op jit(solution)/shard_map/ppermute | solution.py:449
  63.4 16.3 %all-to-all-start.3 = ((f32[32,1,128]{2,1,0:T(1,128)}), f32[32,1,128]{2,1,0:T(1,128)S(1)}, u32[]{:S(2)}, u32[]{:S(2)}) async-start(f32[32,1,128]{2,1,0:T(1,128)} %get-tuple-element.37), calls=%async_computation.3 | async-start | bytes 32768 | tf_op jit(solution)/shard_map/all_to_all | solution.py:458

commit v5 on v4

--- a/solution.py
+++ b/solution.py
@@ -29,13 +29,13 @@
 def halo_table(y_table, bands):
     rows = y_table.shape[0]
     width = rows // bands
-    out = np.zeros((bands, 2, 4, y_table.shape[1]), dtype=y_table.dtype)
+    out = np.zeros((4, bands, y_table.shape[1]), dtype=y_table.dtype)
     for band in range(bands):
         for at, row in enumerate((width, width + 1, -2, -1)):
             source = band * width + row
             if 0 <= source < rows:
-                out[band, :, at] = y_table[source]
-    return out.reshape(bands * 8, y_table.shape[1])
+                out[at, band] = y_table[source]
+    return out.reshape(bands * 4, y_table.shape[1])
 
 
 def lane_iota():
@@ -202,7 +202,7 @@
 
 
 def spectral_kernel(
-    meta_ref, sel_ref, modes_ref, noise_ref, spec_ref, part_ref, tt_ref, ht_ref, send_ref,
+    meta_ref, sel_ref, modes_ref, noise_ref, spec_ref, part_ref, tt_ref, ht_ref, send_ref, pack_scr,
 ):
     bands = modes_ref.shape[0]
     half = LANES // 2
@@ -210,7 +210,6 @@
     rows = tt_ref.shape[1]
     norm_factor = 4.0 / (rows * rows)
     position = source_slot(sel_ref, meta_ref) & (GROUP - 1)
-    me = meta_ref[1] & 7
     lane = lane_iota()
     low = lane < half
     tops, bottoms = [], []
@@ -236,43 +235,47 @@
     weighted = weighted.astype(jnp.bfloat16)
     stacked = jnp.concatenate([weighted, shaped], axis=0)
     inverted = jnp.dot(stacked, tt_ref[...], preferred_element_type=jnp.float32)
+    block = modes_here + 2
     low16 = lax.broadcasted_iota(jnp.int32, (modes_here, LANES), 1) < half
     for pair in range(bands // 2):
         first = inverted[0:modes_here, pair * LANES : (pair + 1) * LANES]
         second = inverted[modes_here:, pair * LANES : (pair + 1) * LANES]
-        send_ref[2 * pair, 0:modes_here, :] = jnp.where(
+        at = 2 * pair * block
+        pack_scr[at : at + modes_here, :] = jnp.where(
             low16, first, pltpu.roll(second, half, axis=1)
-        ).astype(jnp.bfloat16)
-        send_ref[2 * pair + 1, 0:modes_here, :] = jnp.where(
+        )
+        at += block
+        pack_scr[at : at + modes_here, :] = jnp.where(
             low16, pltpu.roll(first, half, axis=1), second
-        ).astype(jnp.bfloat16)
+        )
     halo = lax.dot_general(
         ht_ref[...], stacked, (((1,), (1,)), ((), ())), preferred_element_type=jnp.float32
     )
-    halo = halo.reshape(bands, 8, 2 * modes_here)
-    row8 = lax.broadcasted_iota(jnp.int32, (bands, 8, LANES), 1)
-    lane8 = lax.broadcasted_iota(jnp.int32, (bands, 8, LANES), 2)
-    wide = jnp.concatenate([halo, jnp.zeros((bands, 8, LANES - 2 * modes_here), jnp.float32)], axis=2)
-    wide = wide.reshape(bands * 8, LANES)
-    at = me * modes_here
-    as_first = pltpu.roll(wide, at, axis=1).reshape(bands, 8, LANES)
-    as_second = pltpu.roll(wide, (at + LANES - modes_here) % LANES, axis=1).reshape(bands, 8, LANES)
-    placed = jnp.where(row8 < 4, as_first, as_second)
-    pieces = jnp.zeros((8, LANES), jnp.float32)
-    row = lax.broadcasted_iota(jnp.int32, (8, LANES), 0)
-    energy = jnp.broadcast_to(energy, (8, LANES))
-    for at_row, piece in enumerate(split3(part_ref[...]) + split3(energy)):
-        pieces = jnp.where(row == at_row, piece, pieces)
-    pieces = jnp.broadcast_to(pieces[None], (bands, 8, LANES))
-    mine = lane8 // modes_here == me
-    scalar_at = lane8 == ((me + 1) % 8) * modes_here
-    tail = jnp.where(mine, placed, jnp.where(scalar_at, pieces, 0.0))
-    send_ref[:, modes_here:, :] = tail.astype(jnp.bfloat16)
+    halo = jnp.concatenate(
+        [halo, jnp.zeros((4 * bands, LANES - 2 * modes_here), jnp.float32)], axis=1
+    )
+    window = lax.broadcasted_iota(jnp.int32, (bands, LANES), 1) // modes_here
+    edges = jnp.zeros((bands, LANES), jnp.float32)
+    for at in range(8):
+        field, row = at // 4, at % 4
+        shift = (at - field) * modes_here % LANES
+        value = halo[row * bands : (row + 1) * bands]
+        edges = jnp.where(window == at, pltpu.roll(value, shift, axis=1) if shift else value, edges)
+    lane1 = lax.broadcasted_iota(jnp.int32, (1, LANES), 1)
+    pieces = jnp.zeros((1, LANES), jnp.float32)
+    for at, piece in enumerate(split3(part_ref[0:1, 0:1]) + split3(energy)):
+        pieces = jnp.where(lane1 == at, piece, pieces)
+    for band in range(bands):
+        at = band * block + modes_here
+        pack_scr[at : at + 1, :] = edges[band : band + 1]
+        pack_scr[at + 1 : at + 2, :] = pieces
+    send_ref[...] = pack_scr[...].astype(jnp.bfloat16)
 
 
 def relax_kernel(
     target_ref, col_scr, wgt_scr, miss_ref, depth_hbm, above_ref, below_ref, modes_ref, tt_ref,
-    field_ref, part_ref, seen_scr, inc_scr, one_scr, rate_ref, depth_ref, sem,
+    field_ref, part_ref, unpack_scr, seen_scr, inc_scr, one_scr, rate_ref, depth_ref,
+    sem,
 ):
     depth = pltpu.make_async_copy(depth_hbm, depth_ref, sem)
     depth.start()
@@ -281,26 +284,34 @@
     def rate(depth):
         return RELAX_RATE * depth / (4.0 * depth + STRETCH)
 
-    bands, _, _ = modes_ref.shape
     n_modes, columns = tt_ref.shape
+    bands = part_ref.shape[0]
     modes_here = n_modes // bands
     lane = lane_iota()
-    quads, scalars = [], jnp.zeros((8, LANES), jnp.float32)
-    for quad in range(bands // 8):
-        total = jnp.zeros((8, LANES), jnp.float32)
-        for at in range(8):
-            tail = modes_ref[quad * 8 + at, modes_here:, :].astype(jnp.float32)
-            window = lane // modes_here
-            total = jnp.where(window == at, tail, total)
-            scalars = scalars + jnp.where(window == (at + 1) % 8, tail, 0.0)
-        quads.append(total)
+    block = modes_here + 2
+    unpack_scr[...] = modes_ref[...].astype(jnp.float32)
+    edges = unpack_scr[pl.ds(modes_here, bands, stride=block), :]
+    scalars = unpack_scr[pl.ds(modes_here + 1, bands, stride=block), :]
+    row = lax.broadcasted_iota(jnp.int32, (8, LANES), 0)
+    window = lane // modes_here
+    quads = []
+    for quad in range(0, bands, 8):
+        tile = edges[quad : quad + 8]
+        for bit in (1, 2, 4):
+            up = pltpu.roll(pltpu.roll(tile, 8 - bit, axis=0), bit * modes_here, axis=1)
+            down = pltpu.roll(pltpu.roll(tile, bit, axis=0), LANES - bit * modes_here, axis=1)
+            upper, later = (row & bit) == 0, (window & bit) == 0
+            tile = jnp.where(upper == later, tile, jnp.where(upper, up, down))
+        quads.append(tile)
     halo = jnp.concatenate(quads, axis=1)
-    row = lax.broadcasted_iota(jnp.int32, (8, LANES), 0)
-    misfit = summed(jnp.where(row < 3, scalars, 0.0))
-    energy = summed(jnp.where((row >= 3) & (row < 6), scalars, 0.0))
+    lanes = lax.broadcasted_iota(jnp.int32, scalars.shape, 1)
+    misfit = summed(jnp.where(lanes < 3, scalars, 0.0))
+    energy = summed(jnp.where((lanes >= 3) & (lanes < 6), scalars, 0.0))
     weight = miss_ref[rows : rows + 1, 0:1]
     step = (misfit + weight - target_ref[0]) / (energy + 1.0)
-    main = modes_ref[:, 0:modes_here, :].reshape(n_modes, LANES)
+    main = jnp.concatenate(
+        [unpack_scr[at * block : at * block + modes_here, :] for at in range(bands)], axis=0
+    ).astype(jnp.bfloat16)
     pulled = lax.dot_general(main, tt_ref[...], (((0,), (0,)), ((), ())), preferred_element_type=jnp.float32)
     pulled_h = jnp.dot(halo.astype(jnp.bfloat16), tt_ref[...], preferred_element_type=jnp.float32)
     for at in range(0, rows, 8):
@@ -439,12 +450,14 @@
     send = call(
         spectral_kernel,
         [SMEM, SMEM, VMEM, VMEM, VMEM, VMEM, VMEM, VMEM],
-        shape((bands, modes_here + 8, LANES), bf16),
-        [],
+        shape((bands * (modes_here + 2), LANES), bf16),
+        [vmem((bands * (modes_here + 2), LANES), f32)],
         "spectral",
     )(meta, selection, col_modes, sent, spectrum, part, tt, ht_all)
     send, first, last = lax.optimization_barrier((send, first, last))
+    send = send.reshape(bands, modes_here // 2 + 1, 2, LANES)
     band_modes = lax.all_to_all(send, "space", 0, 0, tiled=True)
+    band_modes = band_modes.reshape(bands * (modes_here + 2), LANES)
     above = lax.ppermute(last, "space", [(i, i + 1) for i in range(bands - 1)])
     below = lax.ppermute(first, "space", [(i + 1, i) for i in range(bands - 1)])
 
@@ -452,7 +465,7 @@
         relax_kernel,
         [SMEM, VMEM, VMEM, VMEM, HBM, VMEM, VMEM, VMEM, VMEM],
         (shape((rows, columns), f32), shape((bands, 1, LANES), f32)),
-        [tile, padded, padded, padded, whole, dma(())],
+        [vmem((bands * (modes_here + 2), LANES), f32), tile, padded, padded, padded, whole, dma(())],
         "relax",
     )(target, col_tile, wgt_tile, miss, in_hbm(depth_field), above, below, band_modes, tt)
     parts = lax.all_to_all(part, "space", 0, 0, tiled=True)

time: 81 us -> 80.7 us (level)
  starting transfers between devices: 44.4 us -> 45.9 us
  other arithmetic: 3.93 us -> 2.9 us
    all_to_all x1, starting transfers between devices: 6.9 us -> 8.1 us  [per_device(): parts = lax.all_to_all(part, 'space', 0, 0, tiled=True)]
    all_to_all x1, waiting for transfers between devices: 1.45 us -> 0.26 us  [per_device(): band_modes = lax.all_to_all(send, 'space', 0, 0, tiled=True)]
    add x1, other arithmetic: 1.95 us -> 0.92 us  [per_device(): analysis = field + jnp.where(selection[1, slot] < 1, near, far)]
    all_to_all x1, waiting for transfers between devices: 7.39 us -> 8.42 us  [per_device(): parts = lax.all_to_all(part, 'space', 0, 0, tiled=True)]
  transfers between devices with their start and end apart: 8 -> 8, of which waited for: 5 -> 4; matrix products, arithmetic and copies ran while one was open for 5% -> 4% of each run, Pallas kernels for 10% -> 10%
where the time goes in v5:
time: 80.7 us; the launch traced here: 80 us
  starting transfers between devices  45.9 us (57%)
  waiting for transfers between devices  16.9 us (21%)
  Pallas kernels  10.5 us (13%)
  between operations  3.24 us (4%)
  other arithmetic  2.9 us (4%)
    all_to_all x1, starting transfers between devices, per_device(): col_modes = lax.all_to_all(send, 'space', 0, 0, tiled=True)  11.8 us
    all_to_all x1, waiting for transfers between devices, per_device(): parts = lax.all_to_all(part, 'space', 0, 0, tiled=True)  8.42 us
    all_to_all x1, starting transfers between devices, per_device(): parts = lax.all_to_all(part, 'space', 0, 0, tiled=True)  8.1 us
    all_to_all x1, starting transfers between devices, per_device(): lax.all_to_all(sent, 'particle', 0, 0, axis_index_groups=groups, tiled=True)  7.82 us
    ppermute x2, starting transfers between devices, swapped(): return lax.ppermute(value, axis, pairs)  6.78 us
    all_to_all x1, starting transfers between devices, per_device(): band_modes = lax.all_to_all(send, 'space', 0, 0, tiled=True)  5.05 us
    all_to_all x1, waiting for transfers between devices, per_device(): col_modes = lax.all_to_all(send, 'space', 0, 0, tiled=True)  5.04 us
    ppermute x1, starting transfers between devices, per_device(): above = lax.ppermute(last, 'space', [(i, i + 1) for i in range(bands - 1)])  4.44 us
  transfers between devices with their start and end apart: 8, of which 4 were waited for; matrix products, arithmetic and copies ran while one was open for 4% of the time, Pallas kernels for 10%

profile of v5, /device:TPU:1, one launch (start us, length us, event | category | flops | bytes accessed | tf_op | source)
XLA Modules:
  0.0 80.0 jit_solution(10881495475719538053)
XLA Ops:
  1.3 0.0 copy-start
  1.3 2.6 %observe.1 = (bf16[4,96,128]{2,1,0:T(8,128)(2,1)}, s32[64,128]{1,0:T(8,128)S(1)}, f32[64,128]{1,0:T(8,128)S(1)}, bf16[512,2048]{1,0:T(8,128)(2,1)S(1)}, f32[1,2048]{1,0:T(1,128)S(1)}, /*index=5*/f32[1,2048]{1,0:T(1,128)S(1)}) custom-call(f32[1]{0:T(128)S(6)} %copy.14.lw_ref, s32[16,64]{1,0:T(8,128)} %bitcast.17, f32[16,64]{1,0:T(8,128)} %bitcast.18, ...), custom_call_target="tpu_custom_call" | custom-call | flops 40000000000 | bytes 4000000 | tf_op jit(solution)/shard_map/observe/pallas_call | solution.py:418
  3.9 7.8 %all-to-all-start = ((bf16[4,96,128]{2,1,0:T(8,128)(2,1)}), bf16[4,96,128]{2,1,0:T(8,128)(2,1)S(1)}, u32[]{:S(2)}, u32[]{:S(2)}) async-start(bf16[4,96,128]{2,1,0:T(8,128)(2,1)} %get-tuple-element.25), calls=%async_computation | async-start | bytes 196608 | tf_op jit(solution)/shard_map/all_to_all | solution.py:434
  11.7 3.4 %collective-permute-start = (f32[64,2048]{1,0:T(8,128)}, f32[64,2048]{1,0:T(8,128)}, u32[]{:S(2)}, u32[]{:S(2)}) collective-permute-start(f32[64,2048]{1,0:T(8,128)} %bitcast.4.stream_hbm), channel_id=1, source_target_pairs={{0,32},{32,0},{64,96},{96,64},{128,160},{160,128},{192,224},{224,1... | collective-permute-start | bytes 1572872 | tf_op jit(solution)/shard_map/ppermute | solution.py:389
  15.1 0.0 copy-done
  15.1 0.6 constant_dynamic-slice_fusion
  16.3 0.1 pad_add_fusion.meta_ref
  16.4 0.0 all-to-all-done.seen_ref.noise_ref
  16.4 0.0 copy-start.1
  16.4 0.0 copy-start.2
  16.4 2.8 %gradient.1 = (bf16[32,8,128]{2,1,0:T(8,128)(2,1)}, f32[72,128]{1,0:T(8,128)S(1)}, f32[8,128]{1,0:T(8,128)S(1)}) custom-call(s32[2]{0:T(128)S(1)} %pad_add_fusion.meta_ref, s32[2,16]{1,0:T(2,128)S(1)} %copy-done, s32[64,128]{1,0:T(8,128)S(1)} %get-tuple-element.22.col_scr, f32[64,128]{1,0:T(8,128)S(1)} %get-tuple-element.23.wgt_scr, ...), custom_call_target="tpu_custom_call" | custom-call | flops 40000000000 | bytes 4000000 | tf_op jit(solution)/shard_map/gradient/pallas_call | solution.py:437
  19.2 11.8 %all-to-all-start.1 = ((bf16[32,8,128]{2,1,0:T(8,128)(2,1)}), bf16[32,8,128]{2,1,0:T(8,128)(2,1)S(1)}, u32[]{:S(2)}, u32[]{:S(2)}) async-start(bf16[32,8,128]{2,1,0:T(8,128)(2,1)} %get-tuple-element.28), calls=%async_computation.1 | async-start | bytes 131072 | tf_op jit(solution)/shard_map/all_to_all | solution.py:444
  31.0 0.0 collective-permute-done
  31.0 1.3 %broadcast_select_fusion = f32[64,2048]{1,0:T(8,128)S(1)} fusion(f32[64,2048]{1,0:T(8,128)} %collective-permute-done, pred[]{:T(512)} %bitcast.7, f32[1,64,2048]{2,1,0:T(8,128)} %param.12), kind=kLoop, calls=%fused_computation.1 | loop fusion | flops 131072 | bytes 1572865 | tf_op jit(solution)/shard_map/jit(_where)/select_n | solution.py:446
  32.3 3.4 %collective-permute-start.3 = (f32[64,2048]{1,0:T(8,128)S(1)}, f32[64,2048]{1,0:T(8,128)}, u32[]{:S(2)}, u32[]{:S(2)}) collective-permute-start(f32[64,2048]{1,0:T(8,128)S(1)} %broadcast_select_fusion), channel_id=1, source_target_pairs={{0,64},{32,96},{64,0},{96,32},{128,192},{160,224},{192,128},{224,1... | collective-permute-start | bytes 1572872 | tf_op jit(solution)/shard_map/ppermute | solution.py:389
  35.7 5.0 %all-to-all-done.1.modes_ref = bf16[32,8,128]{2,1,0:T(8,128)(2,1)S(1)} async-done(((bf16[32,8,128]{2,1,0:T(8,128)(2,1)}), bf16[32,8,128]{2,1,0:T(8,128)(2,1)S(1)}, u32[]{:S(2)}, u32[]{:S(2)}) %all-to-all-start.1) | async-done | bytes 65568 | tf_op jit(solution)/shard_map/all_to_all | solution.py:444
  40.7 0.0 copy-done.1
  40.7 0.0 copy-done.2
  40.7 2.4 %spectral.1 = bf16[576,128]{1,0:T(8,128)(2,1)} custom-call(s32[2]{0:T(128)S(1)} %pad_add_fusion.meta_ref, s32[2,16]{1,0:T(2,128)S(1)} %copy-done, bf16[32,8,128]{2,1,0:T(8,128)(2,1)S(1)} %all-to-all-done.1.modes_ref, bf16[4,96,128]{2,1,0:T(8,128)(2,1)S(1)} %all-to-all-done.seen_ref.noise_ref, f32[16,512]{1,0:T(8,128)S(1)} %copy-done.1, ...), custom_call_target="tpu_custom_call" | custom-call | flops 1000000000 | bytes 4000000 | tf_op jit(solution)/shard_map/spectral/pallas_call | solution.py:450
  43.2 5.1 %all-to-all-start.2 = ((bf16[32,9,2,128]{3,2,1,0:T(2,128)(2,1)}), bf16[32,9,2,128]{3,2,1,0:T(2,128)(2,1)S(1)}, u32[]{:S(2)}, u32[]{:S(2)}) async-start(bf16[32,9,2,128]{3,2,1,0:T(2,128)(2,1)} %bitcast.8), calls=%async_computation.2 | async-start | bytes 294912 | tf_op jit(solution)/shard_map/all_to_all | solution.py:459
  48.3 4.4 %collective-permute-start.1 = (f32[1,2048]{1,0:T(1,128)S(1)}, f32[1,2048]{1,0:T(1,128)S(1)}, u32[]{:S(2)}, u32[]{:S(2)}) collective-permute-start(f32[1,2048]{1,0:T(1,128)S(1)} %get-tuple-element.34), channel_id=1, source_target_pairs={{0,1},{1,2},{2,3},{3,4},{4,5},{5,6},{6,7},{7,8},{8,9},{9,10},{10,1... | collective-permute-start | bytes 24584 | tf_op jit(solution)/shard_map/ppermute | solution.py:461
  52.7 1.9 %collective-permute-start.2 = (f32[1,2048]{1,0:T(1,128)S(1)}, f32[1,2048]{1,0:T(1,128)S(1)}, u32[]{:S(2)}, u32[]{:S(2)}) collective-permute-start(f32[1,2048]{1,0:T(1,128)S(1)} %get-tuple-element.35), channel_id=1, source_target_pairs={{1,0},{2,1},{3,2},{4,3},{5,4},{6,5},{7,6},{8,7},{9,8},{10,9},{11,1... | collective-permute-start | bytes 24584 | tf_op jit(solution)/shard_map/ppermute | solution.py:462
  55.8 0.0 collective-permute-done.1.above_ref
  55.8 3.1 %collective-permute-done.2.below_ref = f32[1,2048]{1,0:T(1,128)S(1)} collective-permute-done((f32[1,2048]{1,0:T(1,128)S(1)}, f32[1,2048]{1,0:T(1,128)S(1)}, u32[]{:S(2)}, u32[]{:S(2)}) %collective-permute-start.2) | collective-permute-done | bytes 8224 | tf_op jit(solution)/shard_map/ppermute | solution.py:462
  59.0 0.3 all-to-all-done.2
  59.2 2.7 %relax.1 = (f32[64,2048]{1,0:T(8,128)S(1)}, f32[32,1,128]{2,1,0:T(1,128)}) custom-call(f32[1]{0:T(128)S(6)} %copy.15.target_ref, s32[64,128]{1,0:T(8,128)S(1)} %get-tuple-element.22.col_scr, f32[64,128]{1,0:T(8,128)S(1)} %get-tuple-element.23.wgt_scr, f32[72,128]{1,0:T(8,128)S(1)} %get-tuple-element.27.miss_ref, f32[64,2048]{1,0:T(8,128)} %depth_hbm.3, ...), custom_call_target="tpu_custom_call" | custom-call | flops 1000000000 | bytes 4000000 | tf_op jit(solution)/shard_map/relax/pallas_call | solution.py:464
  61.9 8.1 %all-to-all-start.3 = ((f32[32,1,128]{2,1,0:T(1,128)}), f32[32,1,128]{2,1,0:T(1,128)S(1)}, u32[]{:S(2)}, u32[]{:S(2)}) async-start(f32[32,1,128]{2,1,0:T(1,128)} %get-tuple-element.37), calls=%async_computation.3 | async-start | bytes 32768 | tf_op jit(solution)/shard_map/all_to_all | solution.py:471
  70.0 0.0 collective-permute-done.3
  70.0 0.9 %select_add_fusion = f32[64,2048]{1,0:T(8,128)} fusion(f32[64,2048]{1,0:T(8,128)S(1)} %get-tuple-element.38, f32[64,2048]{1,0:T(8,128)S(1)} %broadcast_select_fusion, f32[64,2048]{1,0:T(8,128)} %collective-permute-done.3, pred[]{:T(512)} %bitcast.10), kind=kLoop, calls=%fused_computation | loop fusion | flops 262144 | bytes 2097153 | tf_op jit(solution)/shard_map/add | solution.py:472
  71.0 8.4 %all-to-all-done.3 = f32[32,1,128]{2,1,0:T(1,128)S(1)} async-done(((f32[32,1,128]{2,1,0:T(1,128)}), f32[32,1,128]{2,1,0:T(1,128)S(1)}, u32[]{:S(2)}, u32[]{:S(2)}) %all-to-all-start.3) | async-done | bytes 16416 | tf_op jit(solution)/shard_map/all_to_all | solution.py:471
  79.4 0.6 slice_reduce_fusion
Async XLA Ops:
  1.3 13.8 %copy-start = (s32[2,16]{1,0:T(2,128)S(1)}, s32[2,16]{1,0:T(2,128)}, u32[]{:S(2)}) copy-start(s32[2,16]{1,0:T(2,128)} %sel_ref.3) | copy-start | bytes 388
  3.9 12.5 %all-to-all-start = ((bf16[4,96,128]{2,1,0:T(8,128)(2,1)}), bf16[4,96,128]{2,1,0:T(8,128)(2,1)S(1)}, u32[]{:S(2)}, u32[]{:S(2)}) async-start(bf16[4,96,128]{2,1,0:T(8,128)(2,1)} %get-tuple-element.25), calls=%async_computation | async-start | bytes 196608 | tf_op jit(solution)/shard_map/all_to_all | solution.py:434
  11.7 19.3 %collective-permute-start = (f32[64,2048]{1,0:T(8,128)}, f32[64,2048]{1,0:T(8,128)}, u32[]{:S(2)}, u32[]{:S(2)}) collective-permute-start(f32[64,2048]{1,0:T(8,128)} %bitcast.4.stream_hbm), channel_id=1, source_target_pairs={{0,32},{32,0},{64,96},{96,64},{128,160},{160,128},{192,224},{224,1... | collective-permute-start | bytes 1572872 | tf_op jit(solution)/shard_map/ppermute | solution.py:389
  16.4 24.3 %copy-start.1 = (f32[16,512]{1,0:T(8,128)S(1)}, f32[16,512]{1,0:T(8,128)}, u32[]{:S(2)}) copy-start(f32[16,512]{1,0:T(8,128)} %spec_ref.1) | copy-start | bytes 98308
  16.4 24.3 %copy-start.2 = (bf16[128,512]{1,0:T(8,128)(2,1)S(1)}, bf16[128,512]{1,0:T(8,128)(2,1)}, u32[]{:S(2)}) copy-start(bf16[128,512]{1,0:T(8,128)(2,1)} %constant.25.clone.ht_ref) | copy-start | bytes 393220
  19.2 21.6 %all-to-all-start.1 = ((bf16[32,8,128]{2,1,0:T(8,128)(2,1)}), bf16[32,8,128]{2,1,0:T(8,128)(2,1)S(1)}, u32[]{:S(2)}, u32[]{:S(2)}) async-start(bf16[32,8,128]{2,1,0:T(8,128)(2,1)} %get-tuple-element.28), calls=%async_computation.1 | async-start | bytes 131072 | tf_op jit(solution)/shard_map/all_to_all | solution.py:444
  32.3 37.8 %collective-permute-start.3 = (f32[64,2048]{1,0:T(8,128)S(1)}, f32[64,2048]{1,0:T(8,128)}, u32[]{:S(2)}, u32[]{:S(2)}) collective-permute-start(f32[64,2048]{1,0:T(8,128)S(1)} %broadcast_select_fusion), channel_id=1, source_target_pairs={{0,64},{32,96},{64,0},{96,32},{128,192},{160,224},{192,128},{224,1... | collective-permute-start | bytes 1572872 | tf_op jit(solution)/shard_map/ppermute | solution.py:389
  43.2 16.0 %all-to-all-start.2 = ((bf16[32,9,2,128]{3,2,1,0:T(2,128)(2,1)}), bf16[32,9,2,128]{3,2,1,0:T(2,128)(2,1)S(1)}, u32[]{:S(2)}, u32[]{:S(2)}) async-start(bf16[32,9,2,128]{3,2,1,0:T(2,128)(2,1)} %bitcast.8), calls=%async_computation.2 | async-start | bytes 294912 | tf_op jit(solution)/shard_map/all_to_all | solution.py:459
  48.3 7.6 %collective-permute-start.1 = (f32[1,2048]{1,0:T(1,128)S(1)}, f32[1,2048]{1,0:T(1,128)S(1)}, u32[]{:S(2)}, u32[]{:S(2)}) collective-permute-start(f32[1,2048]{1,0:T(1,128)S(1)} %get-tuple-element.34), channel_id=1, source_target_pairs={{0,1},{1,2},{2,3},{3,4},{4,5},{5,6},{6,7},{7,8},{8,9},{9,10},{10,1... | collective-permute-start | bytes 24584 | tf_op jit(solution)/shard_map/ppermute | solution.py:461
  52.7 6.3 %collective-permute-start.2 = (f32[1,2048]{1,0:T(1,128)S(1)}, f32[1,2048]{1,0:T(1,128)S(1)}, u32[]{:S(2)}, u32[]{:S(2)}) collective-permute-start(f32[1,2048]{1,0:T(1,128)S(1)} %get-tuple-element.35), channel_id=1, source_target_pairs={{1,0},{2,1},{3,2},{4,3},{5,4},{6,5},{7,6},{8,7},{9,8},{10,9},{11,1... | collective-permute-start | bytes 24584 | tf_op jit(solution)/shard_map/ppermute | solution.py:462
  61.9 17.5 %all-to-all-start.3 = ((f32[32,1,128]{2,1,0:T(1,128)}), f32[32,1,128]{2,1,0:T(1,128)S(1)}, u32[]{:S(2)}, u32[]{:S(2)}) async-start(f32[32,1,128]{2,1,0:T(1,128)} %get-tuple-element.37), calls=%async_computation.3 | async-start | bytes 32768 | tf_op jit(solution)/shard_map/all_to_all | solution.py:471

commit v6 on v5

--- a/solution.py
+++ b/solution.py
@@ -139,7 +139,8 @@
 
 
 def gradient_kernel(
-    meta_ref, sel_ref, col_scr, wgt_scr, seen_ref, tt_ref, send_ref, miss_ref, part_ref, grad_scr,
+    meta_ref, sel_ref, target_ref, col_scr, wgt_scr, seen_ref, tt_ref, top_ref, bottom_ref,
+    send_ref, miss_ref, part_ref, first_ref, second_ref, grad_scr, pack_scr,
 ):
     rows = grad_scr.shape[0]
     per_row = LANES * 8 // rows
@@ -148,7 +149,11 @@
     first = seen_ref.shape[1] - 32
     sent = seen_ref[position][first:, :].astype(jnp.float32)
     mismatch = sent[0:8] + sent[8:16] + sent[16:24]
-    weight = sent[24:25] + sent[25:26] + sent[26:27]
+    weight = sent[24:25] + sent[25:26] + sent[26:27] - target_ref[0]
+    slot = meta_ref[0]
+    for section, stay_ref in enumerate((first_ref, second_ref)):
+        stay = jnp.where(sel_ref[section, slot] < 1, 1.0, 0.0)
+        stay_ref[...] = jnp.full(stay_ref.shape, stay, jnp.float32)
     miss_ref[rows:, :] = jnp.broadcast_to(weight, (8, LANES))
     tiles = [mismatch] + [
         pltpu.roll(mismatch, LANES - group * per_row, axis=1) for group in range(1, rows // 8)
@@ -196,17 +201,39 @@
     modes = lax.dot_general(
         tt_ref[...], gradient, (((1,), (1,)), ((), ())), preferred_element_type=jnp.float32
     )
-    bands = send_ref.shape[0]
+    bands = modes.shape[0] // 16
+    block = send_ref.shape[0] // bands
     split = modes.reshape(bands, 2, 8, rows)
-    send_ref[...] = jnp.concatenate([split[:, 0], split[:, 1]], axis=2).astype(jnp.bfloat16)
+    values = jnp.concatenate([split[:, 0], split[:, 1]], axis=2)
+    pairs = columns // LANES
+    top, bottom = (
+        jnp.concatenate(
+            [ref[:, pair * LANES : (pair + 1) * LANES] for pair in range(pairs)], axis=0
+        )
+        for ref in (top_ref, bottom_ref)
+    )
+    half = LANES // 2
+    low = lax.broadcasted_iota(jnp.int32, (pairs, LANES), 1) < half
+    even = split3(jnp.where(low, top, pltpu.roll(bottom, half, axis=1)))
+    odd = split3(jnp.where(low, pltpu.roll(top, half, axis=1), bottom))
+    for band in range(bands):
+        at = band * block
+        pack_scr[at : at + 8, :] = values[band]
+        for piece in range(3):
+            row = (odd if band % 2 else even)[piece][band // 2 : band // 2 + 1]
+            pack_scr[at + 8 + piece : at + 9 + piece, :] = row
+        pack_scr[at + 11 : at + 12, :] = jnp.zeros((1, LANES), jnp.float32)
+    send_ref[...] = pack_scr[...].astype(jnp.bfloat16)
 
 
 def spectral_kernel(
     meta_ref, sel_ref, modes_ref, noise_ref, spec_ref, part_ref, tt_ref, ht_ref, send_ref, pack_scr,
+    unpack_scr,
 ):
-    bands = modes_ref.shape[0]
     half = LANES // 2
     modes_here, n_modes = spec_ref.shape
+    bands = n_modes // modes_here
+    unpack_scr[...] = modes_ref[...].astype(jnp.float32)
     rows = tt_ref.shape[1]
     norm_factor = 4.0 / (rows * rows)
     position = source_slot(sel_ref, meta_ref) & (GROUP - 1)
@@ -214,8 +241,8 @@
     low = lane < half
     tops, bottoms = [], []
     for pair in range(bands // 2):
-        even = modes_ref[2 * pair].astype(jnp.float32)
-        odd = modes_ref[2 * pair + 1].astype(jnp.float32)
+        even = unpack_scr[24 * pair : 24 * pair + 8, :]
+        odd = unpack_scr[24 * pair + 12 : 24 * pair + 20, :]
         tops.append(jnp.where(low, even, pltpu.roll(odd, half, axis=1)))
         bottoms.append(jnp.where(low, pltpu.roll(even, half, axis=1), odd))
     columns = jnp.concatenate(
@@ -235,7 +262,13 @@
     weighted = weighted.astype(jnp.bfloat16)
     stacked = jnp.concatenate([weighted, shaped], axis=0)
     inverted = jnp.dot(stacked, tt_ref[...], preferred_element_type=jnp.float32)
-    block = modes_here + 2
+    depth = sum(unpack_scr[pl.ds(8 + piece, bands, stride=12), :] for piece in range(3))
+    band_row = lax.broadcasted_iota(jnp.int32, (bands, LANES), 0)
+    band_low = lax.broadcasted_iota(jnp.int32, (bands, LANES), 1) < half
+    above = jnp.where(band_row > 0, pltpu.roll(depth, 1, axis=0), 0.0)
+    below = jnp.where(band_row < bands - 1, pltpu.roll(depth, bands - 1, axis=0), 0.0)
+    beside = split3(pltpu.roll(jnp.where(band_low, below, above), half, axis=1))
+    block = modes_here + 6
     low16 = lax.broadcasted_iota(jnp.int32, (modes_here, LANES), 1) < half
     for pair in range(bands // 2):
         first = inverted[0:modes_here, pair * LANES : (pair + 1) * LANES]
@@ -269,11 +302,14 @@
         at = band * block + modes_here
         pack_scr[at : at + 1, :] = edges[band : band + 1]
         pack_scr[at + 1 : at + 2, :] = pieces
+        for piece in range(3):
+            pack_scr[at + 2 + piece : at + 3 + piece, :] = beside[piece][band : band + 1]
+        pack_scr[at + 5 : at + 6, :] = jnp.zeros((1, LANES), jnp.float32)
     send_ref[...] = pack_scr[...].astype(jnp.bfloat16)
 
 
 def relax_kernel(
-    target_ref, col_scr, wgt_scr, miss_ref, depth_hbm, above_ref, below_ref, modes_ref, tt_ref,
+    col_scr, wgt_scr, miss_ref, depth_hbm, modes_ref, tt_ref,
     field_ref, part_ref, unpack_scr, seen_scr, inc_scr, one_scr, rate_ref, depth_ref,
     sem,
 ):
@@ -288,7 +324,7 @@
     bands = part_ref.shape[0]
     modes_here = n_modes // bands
     lane = lane_iota()
-    block = modes_here + 2
+    block = modes_here + 6
     unpack_scr[...] = modes_ref[...].astype(jnp.float32)
     edges = unpack_scr[pl.ds(modes_here, bands, stride=block), :]
     scalars = unpack_scr[pl.ds(modes_here + 1, bands, stride=block), :]
@@ -308,7 +344,7 @@
     misfit = summed(jnp.where(lanes < 3, scalars, 0.0))
     energy = summed(jnp.where((lanes >= 3) & (lanes < 6), scalars, 0.0))
     weight = miss_ref[rows : rows + 1, 0:1]
-    step = (misfit + weight - target_ref[0]) / (energy + 1.0)
+    step = (misfit + weight) / (energy + 1.0)
     main = jnp.concatenate(
         [unpack_scr[at * block : at * block + modes_here, :] for at in range(bands)], axis=0
     ).astype(jnp.bfloat16)
@@ -325,9 +361,22 @@
     def rate(depth):
         return RELAX_RATE * depth / (4.0 * depth + STRETCH)
 
-    rate_ref[rows:, :] = jnp.where(
-        row8 == 0, rate(below_ref[...]), jnp.where(row8 == 7, rate(above_ref[...]), 0.0)
-    )
+    even, odd = (
+        sum(
+            unpack_scr[pl.ds(start + piece, bands // 2, stride=2 * block), :] for piece in range(3)
+        )
+        for start in (modes_here + 2, modes_here + 2 + block)
+    )
+    half = LANES // 2
+    low = lax.broadcasted_iota(jnp.int32, (bands // 2, LANES), 1) < half
+    above = rate(jnp.where(low, even, pltpu.roll(odd, half, axis=1)))
+    below = rate(jnp.where(low, pltpu.roll(even, half, axis=1), odd))
+    for pair in range(bands // 2):
+        rate_ref[rows:, pair * LANES : (pair + 1) * LANES] = jnp.where(
+            row == 0,
+            below[pair : pair + 1],
+            jnp.where(row == 7, above[pair : pair + 1], 0.0),
+        )
     for at in range(0, rows, 8):
         rate_ref[at : at + 8, :] = rate(depth_ref[at : at + 8, :])
     length = rows + 8
@@ -434,42 +483,46 @@
     sent = lax.all_to_all(sent, "particle", 0, 0, axis_index_groups=groups, tiled=True)
     swap = swapped(held, "particle", 0)
 
-    send, miss, part = call(
+    send, miss, part, stay_first, stay_second = call(
         gradient_kernel,
-        [SMEM, SMEM, VMEM, VMEM, VMEM, VMEM],
-        (shape((bands, 8, LANES), bf16), shape((rows + 8, LANES), f32), shape((8, LANES), f32)),
-        [whole],
+        [SMEM, SMEM, SMEM] + [VMEM] * 6,
+        (
+            shape((bands * 12, LANES), bf16),
+            shape((rows + 8, LANES), f32),
+            shape((8, LANES), f32),
+            shape((1, columns), f32),
+            shape((1, columns), f32),
+        ),
+        [whole, vmem((bands * 12, LANES), f32)],
         "gradient",
-    )(meta, selection, col_tile, wgt_tile, sent, tt)
-    col_modes = lax.all_to_all(send, "space", 0, 0, tiled=True)
-
-    near = jnp.where(selection[0, slot] < 1, own, swap)
+    )(meta, selection, target, col_tile, wgt_tile, sent, tt, first, last)
+    send = send.reshape(bands, 6, 2, LANES)
+    col_modes = lax.all_to_all(send, "space", 0, 0, tiled=True).reshape(bands * 12, LANES)
+
+    near = jnp.where(stay_first > 0.0, own, swap)
     far = swapped(near, "particle", 1)
     col_modes, near = lax.optimization_barrier((col_modes, near))
 
     send = call(
         spectral_kernel,
         [SMEM, SMEM, VMEM, VMEM, VMEM, VMEM, VMEM, VMEM],
-        shape((bands * (modes_here + 2), LANES), bf16),
-        [vmem((bands * (modes_here + 2), LANES), f32)],
+        shape((bands * (modes_here + 6), LANES), bf16),
+        [vmem((bands * (modes_here + 6), LANES), f32), vmem((bands * 12, LANES), f32)],
         "spectral",
     )(meta, selection, col_modes, sent, spectrum, part, tt, ht_all)
-    send, first, last = lax.optimization_barrier((send, first, last))
-    send = send.reshape(bands, modes_here // 2 + 1, 2, LANES)
+    send = send.reshape(bands, modes_here // 2 + 3, 2, LANES)
     band_modes = lax.all_to_all(send, "space", 0, 0, tiled=True)
-    band_modes = band_modes.reshape(bands * (modes_here + 2), LANES)
-    above = lax.ppermute(last, "space", [(i, i + 1) for i in range(bands - 1)])
-    below = lax.ppermute(first, "space", [(i + 1, i) for i in range(bands - 1)])
+    band_modes = band_modes.reshape(bands * (modes_here + 6), LANES)
 
     field, part = call(
         relax_kernel,
-        [SMEM, VMEM, VMEM, VMEM, HBM, VMEM, VMEM, VMEM, VMEM],
+        [VMEM, VMEM, VMEM, HBM, VMEM, VMEM],
         (shape((rows, columns), f32), shape((bands, 1, LANES), f32)),
-        [vmem((bands * (modes_here + 2), LANES), f32), tile, padded, padded, padded, whole, dma(())],
+        [vmem((bands * (modes_here + 6), LANES), f32), tile, padded, padded, padded, whole, dma(())],
         "relax",
-    )(target, col_tile, wgt_tile, miss, in_hbm(depth_field), above, below, band_modes, tt)
+    )(col_tile, wgt_tile, miss, in_hbm(depth_field), band_modes, tt)
     parts = lax.all_to_all(part, "space", 0, 0, tiled=True)
-    analysis = field + jnp.where(selection[1, slot] < 1, near, far)
+    analysis = field + jnp.where(stay_second > 0.0, near, far)
     parts, analysis = lax.optimization_barrier((parts, analysis))
     misfit_out = jnp.sum(parts[:, 0, 0:1], axis=0)
     return analysis[None], misfit_out

time: 80.7 us -> 76.4 us (0.947)
  starting transfers between devices: 45.9 us -> 33.5 us
  waiting for transfers between devices: 16.9 us -> 25.8 us
  between operations: 3.24 us -> 2.02 us
  other arithmetic: 2.9 us -> 4.01 us
    all_to_all x1, waiting for transfers between devices: 0.26 us -> 11.6 us  [per_device(): band_modes = lax.all_to_all(send, 'space', 0, 0, tiled=True)]
    ppermute x2 -> x0, starting transfers between devices: 6.36 us -> none  [the longest x1 4.44 us: per_device(): above = lax.ppermute(last, 'space', [(i, i + 1) for i in range(bands - 1)])]
    all_to_all x1, starting transfers between devices: 8.1 us -> 3.69 us  [per_device(): parts = lax.all_to_all(part, 'space', 0, 0, tiled=True)]
    ppermute x2 -> x0, waiting for transfers between devices: 3.14 us -> none  [the longest x1 3.13 us: per_device(): below = lax.ppermute(first, 'space', [(i + 1, i) for i in range(bands - 1)])]
    add x1, other arithmetic: 0.92 us -> 1.96 us  [per_device(): analysis = field + jnp.where(stay_second > 0.0, near, far)]
    all_to_all x1, starting transfers between devices: 5.05 us -> 4.02 us  [per_device(): band_modes = lax.all_to_all(send, 'space', 0, 0, tiled=True)]
    all_to_all x1, waiting for transfers between devices: 5.04 us -> 6.07 us  [per_device(): lax.all_to_all(send, 'space', 0, 0, tiled=True).reshape(bands * 12, LANES)]
    all_to_all x1, waiting for transfers between devices: 8.42 us -> 7.51 us  [per_device(): parts = lax.all_to_all(part, 'space', 0, 0, tiled=True)]
  transfers between devices with their start and end apart: 8 -> 6, of which waited for: 4 -> 4; matrix products, arithmetic and copies ran while one was open for 4% -> 4% of each run, Pallas kernels for 10% -> 10%
where the time goes in v6:
time: 76.4 us; the launch traced here: 75.8 us
  starting transfers between devices  33.5 us (44%)
  waiting for transfers between devices  25.8 us (34%)
  Pallas kernels  10.5 us (14%)
  other arithmetic  4.01 us (5%)
  between operations  2.02 us (3%)
    all_to_all x1, starting transfers between devices, per_device(): lax.all_to_all(send, 'space', 0, 0, tiled=True).reshape(bands * 12, LANES)  11.8 us
    all_to_all x1, waiting for transfers between devices, per_device(): band_modes = lax.all_to_all(send, 'space', 0, 0, tiled=True)  11.6 us
    all_to_all x1, starting transfers between devices, per_device(): lax.all_to_all(sent, 'particle', 0, 0, axis_index_groups=groups, tiled=True)  7.82 us
    all_to_all x1, waiting for transfers between devices, per_device(): parts = lax.all_to_all(part, 'space', 0, 0, tiled=True)  7.51 us
    ppermute x2, starting transfers between devices, swapped(): return lax.ppermute(value, axis, pairs)  6.17 us
    all_to_all x1, waiting for transfers between devices, per_device(): lax.all_to_all(send, 'space', 0, 0, tiled=True).reshape(bands * 12, LANES)  6.07 us
    all_to_all x1, starting transfers between devices, per_device(): band_modes = lax.all_to_all(send, 'space', 0, 0, tiled=True)  4.02 us
    all_to_all x1, starting transfers between devices, per_device(): parts = lax.all_to_all(part, 'space', 0, 0, tiled=True)  3.69 us
  transfers between devices with their start and end apart: 6, of which 4 were waited for; matrix products, arithmetic and copies ran while one was open for 4% of the time, Pallas kernels for 10%

profile of v6, /device:TPU:1, one launch (start us, length us, event | category | flops | bytes accessed | tf_op | source)
XLA Modules:
  0.0 75.8 jit_solution(14940435642278979399)
XLA Ops:
  1.3 0.0 copy-start.1
  1.3 2.6 %observe.1 = (bf16[4,96,128]{2,1,0:T(8,128)(2,1)}, s32[64,128]{1,0:T(8,128)S(1)}, f32[64,128]{1,0:T(8,128)S(1)}, bf16[512,2048]{1,0:T(8,128)(2,1)S(1)}, f32[1,2048]{1,0:T(1,128)S(1)}, /*index=5*/f32[1,2048]{1,0:T(1,128)S(1)}) custom-call(f32[1]{0:T(128)S(6)} %copy.14.lw_ref, s32[16,64]{1,0:T(8,128)} %bitcast.18, f32[16,64]{1,0:T(8,128)} %bitcast.19, ...), custom_call_target="tpu_custom_call" | custom-call | flops 40000000000 | bytes 4000000 | tf_op jit(solution)/shard_map/observe/pallas_call | solution.py:467
  3.9 7.8 %all-to-all-start = ((bf16[4,96,128]{2,1,0:T(8,128)(2,1)}), bf16[4,96,128]{2,1,0:T(8,128)(2,1)S(1)}, u32[]{:S(2)}, u32[]{:S(2)}) async-start(bf16[4,96,128]{2,1,0:T(8,128)(2,1)} %get-tuple-element.24), calls=%async_computation | async-start | bytes 196608 | tf_op jit(solution)/shard_map/all_to_all | solution.py:483
  11.7 3.4 %collective-permute-start = (f32[64,2048]{1,0:T(8,128)}, f32[64,2048]{1,0:T(8,128)}, u32[]{:S(2)}, u32[]{:S(2)}) collective-permute-start(f32[64,2048]{1,0:T(8,128)} %bitcast.4.stream_hbm), channel_id=1, source_target_pairs={{0,32},{32,0},{64,96},{96,64},{128,160},{160,128},{192,224},{224,1... | collective-permute-start | bytes 1572872 | tf_op jit(solution)/shard_map/ppermute | solution.py:438
  15.7 0.1 pad_add_fusion.meta_ref
  15.8 0.6 all-to-all-done.seen_ref.noise_ref
  16.4 0.0 copy-done.1
  16.4 0.0 copy-start
  16.4 0.0 copy-start.2
  16.4 2.8 %gradient.1 = (bf16[384,128]{1,0:T(8,128)(2,1)}, f32[72,128]{1,0:T(8,128)S(1)}, f32[8,128]{1,0:T(8,128)S(1)}, f32[1,2048]{1,0:T(1,128)S(1)}, f32[1,2048]{1,0:T(1,128)S(1)}) custom-call(s32[2]{0:T(128)S(1)} %pad_add_fusion.meta_ref, s32[2,16]{1,0:T(2,128)S(1)} %copy-done.1, f32[1]{0:T(128)S(6)} %copy.15.target_ref, s32[64,128]{1,0:T(8,128)S(1)} %get-tuple-element.21.col_scr, ...), custom_call_target="tpu_custom_call" | custom-call | flops 40000000000 | bytes 4000000 | tf_op jit(solution)/shard_map/gradient/pallas_call | solution.py:486
  19.2 11.8 %all-to-all-start.1 = ((bf16[32,6,2,128]{3,2,1,0:T(2,128)(2,1)}), bf16[32,6,2,128]{3,2,1,0:T(2,128)(2,1)S(1)}, u32[]{:S(2)}, u32[]{:S(2)}) async-start(bf16[32,6,2,128]{3,2,1,0:T(2,128)(2,1)} %bitcast.7), calls=%async_computation.1 | async-start | bytes 196608 | tf_op jit(solution)/shard_map/all_to_all | solution.py:500
  31.1 0.0 collective-permute-done
  31.1 1.3 %broadcast_select_fusion = f32[64,2048]{1,0:T(8,128)S(1)} fusion(f32[64,2048]{1,0:T(8,128)} %collective-permute-done, pred[2048]{0:T(1024)(128)(4,1)S(1)} %compare_reduce_fusion.1, f32[1,64,2048]{2,1,0:T(8,128)} %param.12), kind=kLoop, calls=%fused_computation.1 | loop fusion | flops 131072 | bytes 1574912 | tf_op jit(solution)/shard_map/jit(_where)/select_n | solution.py:502
  32.3 2.8 %collective-permute-start.1 = (f32[64,2048]{1,0:T(8,128)S(1)}, f32[64,2048]{1,0:T(8,128)}, u32[]{:S(2)}, u32[]{:S(2)}) collective-permute-start(f32[64,2048]{1,0:T(8,128)S(1)} %broadcast_select_fusion), channel_id=1, source_target_pairs={{0,64},{32,96},{64,0},{96,32},{128,192},{160,224},{192,128},{224,1... | collective-permute-start | bytes 1572872 | tf_op jit(solution)/shard_map/ppermute | solution.py:438
  35.2 6.1 %all-to-all-done.1 = bf16[32,6,2,128]{3,2,1,0:T(2,128)(2,1)S(1)} async-done(((bf16[32,6,2,128]{3,2,1,0:T(2,128)(2,1)}), bf16[32,6,2,128]{3,2,1,0:T(2,128)(2,1)S(1)}, u32[]{:S(2)}, u32[]{:S(2)}) %all-to-all-start.1) | async-done | bytes 98336 | tf_op jit(solution)/shard_map/all_to_all | solution.py:500
  41.2 0.0 copy-done
  41.2 0.0 copy-done.2
  41.2 2.5 %spectral.1 = bf16[704,128]{1,0:T(8,128)(2,1)} custom-call(s32[2]{0:T(128)S(1)} %pad_add_fusion.meta_ref, s32[2,16]{1,0:T(2,128)S(1)} %copy-done.1, bf16[384,128]{1,0:T(8,128)(2,1)S(1)} %bitcast.15, bf16[4,96,128]{2,1,0:T(8,128)(2,1)S(1)} %all-to-all-done.seen_ref.noise_ref, f32[16,512]{1,0:T(8,128)S(1)} %copy-done, ...), custom_call_target="tpu_custom_call" | custom-call | flops 1000000000 | bytes 4000000 | tf_op jit(solution)/shard_map/spectral/pallas_call | solution.py:506
  43.7 4.0 %all-to-all-start.2 = ((bf16[32,11,2,128]{3,2,1,0:T(2,128)(2,1)}), bf16[32,11,2,128]{3,2,1,0:T(2,128)(2,1)S(1)}, u32[]{:S(2)}, u32[]{:S(2)}) async-start(bf16[32,11,2,128]{3,2,1,0:T(2,128)(2,1)} %bitcast.9), calls=%async_computation.2 | async-start | bytes 360448 | tf_op jit(solution)/shard_map/all_to_all | solution.py:514
  47.8 11.6 %all-to-all-done.2 = bf16[32,11,2,128]{3,2,1,0:T(2,128)(2,1)S(1)} async-done(((bf16[32,11,2,128]{3,2,1,0:T(2,128)(2,1)}), bf16[32,11,2,128]{3,2,1,0:T(2,128)(2,1)S(1)}, u32[]{:S(2)}, u32[]{:S(2)}) %all-to-all-start.2) | async-done | bytes 180256 | tf_op jit(solution)/shard_map/all_to_all | solution.py:514
  59.3 2.7 %relax.1 = (f32[64,2048]{1,0:T(8,128)S(1)}, f32[32,1,128]{2,1,0:T(1,128)}) custom-call(s32[64,128]{1,0:T(8,128)S(1)} %get-tuple-element.21.col_scr, f32[64,128]{1,0:T(8,128)S(1)} %get-tuple-element.22.wgt_scr, f32[72,128]{1,0:T(8,128)S(1)} %get-tuple-element.28.miss_ref, f32[64,2048]{1,0:T(8,128)} %depth_hbm.3, bf16[704,128]{1,0:T(8,128)(2,1)S(1)} %bitcast.14, ...), custom_call_target="tpu_custom_call" | custom-call | flops 1000000000 | bytes 4000000 | tf_op jit(solution)/shard_map/relax/pallas_call | solution.py:517
  62.0 3.7 %all-to-all-start.3 = ((f32[32,1,128]{2,1,0:T(1,128)}), f32[32,1,128]{2,1,0:T(1,128)S(1)}, u32[]{:S(2)}, u32[]{:S(2)}) async-start(f32[32,1,128]{2,1,0:T(1,128)} %get-tuple-element.34), calls=%async_computation.3 | async-start | bytes 32768 | tf_op jit(solution)/shard_map/all_to_all | solution.py:524
  65.7 0.0 collective-permute-done.1
  65.7 2.0 %select_add_fusion = f32[64,2048]{1,0:T(8,128)} fusion(f32[64,2048]{1,0:T(8,128)S(1)} %get-tuple-element.35, f32[64,2048]{1,0:T(8,128)S(1)} %broadcast_select_fusion, f32[64,2048]{1,0:T(8,128)} %collective-permute-done.1, pred[2048]{0:T(1024)(128)(4,1)S(1)} %compare_reduce_fusion), kind=kLoop, calls=%fused_computation | loop fusion | flops 262144 | bytes 2099200 | tf_op jit(solution)/shard_map/add | solution.py:525
  67.7 7.5 %all-to-all-done.3 = f32[32,1,128]{2,1,0:T(1,128)S(1)} async-done(((f32[32,1,128]{2,1,0:T(1,128)}), f32[32,1,128]{2,1,0:T(1,128)S(1)}, u32[]{:S(2)}, u32[]{:S(2)}) %all-to-all-start.3) | async-done | bytes 16416 | tf_op jit(solution)/shard_map/all_to_all | solution.py:524
  75.2 0.6 slice_reduce_fusion
  (2 shorter events, 0.1 us)
Async XLA Ops:
  1.3 15.1 %copy-start.1 = (s32[2,16]{1,0:T(2,128)S(1)}, s32[2,16]{1,0:T(2,128)}, u32[]{:S(2)}) copy-start(s32[2,16]{1,0:T(2,128)} %sel_ref.3) | copy-start | bytes 388
  3.9 12.5 %all-to-all-start = ((bf16[4,96,128]{2,1,0:T(8,128)(2,1)}), bf16[4,96,128]{2,1,0:T(8,128)(2,1)S(1)}, u32[]{:S(2)}, u32[]{:S(2)}) async-start(bf16[4,96,128]{2,1,0:T(8,128)(2,1)} %get-tuple-element.24), calls=%async_computation | async-start | bytes 196608 | tf_op jit(solution)/shard_map/all_to_all | solution.py:483
  11.7 19.4 %collective-permute-start = (f32[64,2048]{1,0:T(8,128)}, f32[64,2048]{1,0:T(8,128)}, u32[]{:S(2)}, u32[]{:S(2)}) collective-permute-start(f32[64,2048]{1,0:T(8,128)} %bitcast.4.stream_hbm), channel_id=1, source_target_pairs={{0,32},{32,0},{64,96},{96,64},{128,160},{160,128},{192,224},{224,1... | collective-permute-start | bytes 1572872 | tf_op jit(solution)/shard_map/ppermute | solution.py:438
  16.4 24.8 %copy-start = (f32[16,512]{1,0:T(8,128)S(1)}, f32[16,512]{1,0:T(8,128)}, u32[]{:S(2)}) copy-start(f32[16,512]{1,0:T(8,128)} %spec_ref.1) | copy-start | bytes 98308
  16.4 24.8 %copy-start.2 = (bf16[128,512]{1,0:T(8,128)(2,1)S(1)}, bf16[128,512]{1,0:T(8,128)(2,1)}, u32[]{:S(2)}) copy-start(bf16[128,512]{1,0:T(8,128)(2,1)} %constant.17.clone.ht_ref) | copy-start | bytes 393220
  19.2 22.0 %all-to-all-start.1 = ((bf16[32,6,2,128]{3,2,1,0:T(2,128)(2,1)}), bf16[32,6,2,128]{3,2,1,0:T(2,128)(2,1)S(1)}, u32[]{:S(2)}, u32[]{:S(2)}) async-start(bf16[32,6,2,128]{3,2,1,0:T(2,128)(2,1)} %bitcast.7), calls=%async_computation.1 | async-start | bytes 196608 | tf_op jit(solution)/shard_map/all_to_all | solution.py:500
  32.3 33.4 %collective-permute-start.1 = (f32[64,2048]{1,0:T(8,128)S(1)}, f32[64,2048]{1,0:T(8,128)}, u32[]{:S(2)}, u32[]{:S(2)}) collective-permute-start(f32[64,2048]{1,0:T(8,128)S(1)} %broadcast_select_fusion), channel_id=1, source_target_pairs={{0,64},{32,96},{64,0},{96,32},{128,192},{160,224},{192,128},{224,1... | collective-permute-start | bytes 1572872 | tf_op jit(solution)/shard_map/ppermute | solution.py:438
  43.7 15.6 %all-to-all-start.2 = ((bf16[32,11,2,128]{3,2,1,0:T(2,128)(2,1)}), bf16[32,11,2,128]{3,2,1,0:T(2,128)(2,1)S(1)}, u32[]{:S(2)}, u32[]{:S(2)}) async-start(bf16[32,11,2,128]{3,2,1,0:T(2,128)(2,1)} %bitcast.9), calls=%async_computation.2 | async-start | bytes 360448 | tf_op jit(solution)/shard_map/all_to_all | solution.py:514
  62.0 13.2 %all-to-all-start.3 = ((f32[32,1,128]{2,1,0:T(1,128)}), f32[32,1,128]{2,1,0:T(1,128)S(1)}, u32[]{:S(2)}, u32[]{:S(2)}) async-start(f32[32,1,128]{2,1,0:T(1,128)} %get-tuple-element.34), calls=%async_computation.3 | async-start | bytes 32768 | tf_op jit(solution)/shard_map/all_to_all | solution.py:524

commit v7 on v6

--- a/solution.py
+++ b/solution.py
@@ -44,6 +44,11 @@
 
 def summed(values):
     return jnp.sum(jnp.sum(values, axis=0, keepdims=True), axis=1, keepdims=True)
+
+
+def split2(value):
+    high = value.astype(jnp.bfloat16).astype(jnp.float32)
+    return high, value - high
 
 
 def split3(value):
@@ -214,15 +219,14 @@
     )
     half = LANES // 2
     low = lax.broadcasted_iota(jnp.int32, (pairs, LANES), 1) < half
-    even = split3(jnp.where(low, top, pltpu.roll(bottom, half, axis=1)))
-    odd = split3(jnp.where(low, pltpu.roll(top, half, axis=1), bottom))
+    even = split2(jnp.where(low, top, pltpu.roll(bottom, half, axis=1)))
+    odd = split2(jnp.where(low, pltpu.roll(top, half, axis=1), bottom))
     for band in range(bands):
         at = band * block
         pack_scr[at : at + 8, :] = values[band]
-        for piece in range(3):
+        for piece in range(2):
             row = (odd if band % 2 else even)[piece][band // 2 : band // 2 + 1]
             pack_scr[at + 8 + piece : at + 9 + piece, :] = row
-        pack_scr[at + 11 : at + 12, :] = jnp.zeros((1, LANES), jnp.float32)
     send_ref[...] = pack_scr[...].astype(jnp.bfloat16)
 
 
@@ -241,8 +245,8 @@
     low = lane < half
     tops, bottoms = [], []
     for pair in range(bands // 2):
-        even = unpack_scr[24 * pair : 24 * pair + 8, :]
-        odd = unpack_scr[24 * pair + 12 : 24 * pair + 20, :]
+        even = unpack_scr[20 * pair : 20 * pair + 8, :]
+        odd = unpack_scr[20 * pair + 10 : 20 * pair + 18, :]
         tops.append(jnp.where(low, even, pltpu.roll(odd, half, axis=1)))
         bottoms.append(jnp.where(low, pltpu.roll(even, half, axis=1), odd))
     columns = jnp.concatenate(
@@ -262,13 +266,13 @@
     weighted = weighted.astype(jnp.bfloat16)
     stacked = jnp.concatenate([weighted, shaped], axis=0)
     inverted = jnp.dot(stacked, tt_ref[...], preferred_element_type=jnp.float32)
-    depth = sum(unpack_scr[pl.ds(8 + piece, bands, stride=12), :] for piece in range(3))
+    depth = sum(unpack_scr[pl.ds(8 + piece, bands, stride=10), :] for piece in range(2))
     band_row = lax.broadcasted_iota(jnp.int32, (bands, LANES), 0)
     band_low = lax.broadcasted_iota(jnp.int32, (bands, LANES), 1) < half
     above = jnp.where(band_row > 0, pltpu.roll(depth, 1, axis=0), 0.0)
     below = jnp.where(band_row < bands - 1, pltpu.roll(depth, bands - 1, axis=0), 0.0)
-    beside = split3(pltpu.roll(jnp.where(band_low, below, above), half, axis=1))
-    block = modes_here + 6
+    beside = split2(pltpu.roll(jnp.where(band_low, below, above), half, axis=1))
+    block = modes_here + 4
     low16 = lax.broadcasted_iota(jnp.int32, (modes_here, LANES), 1) < half
     for pair in range(bands // 2):
         first = inverted[0:modes_here, pair * LANES : (pair + 1) * LANES]
@@ -302,9 +306,8 @@
         at = band * block + modes_here
         pack_scr[at : at + 1, :] = edges[band : band + 1]
         pack_scr[at + 1 : at + 2, :] = pieces
-        for piece in range(3):
+        for piece in range(2):
             pack_scr[at + 2 + piece : at + 3 + piece, :] = beside[piece][band : band + 1]
-        pack_scr[at + 5 : at + 6, :] = jnp.zeros((1, LANES), jnp.float32)
     send_ref[...] = pack_scr[...].astype(jnp.bfloat16)
 
 
@@ -324,7 +327,7 @@
     bands = part_ref.shape[0]
     modes_here = n_modes // bands
     lane = lane_iota()
-    block = modes_here + 6
+    block = modes_here + 4
     unpack_scr[...] = modes_ref[...].astype(jnp.float32)
     edges = unpack_scr[pl.ds(modes_here, bands, stride=block), :]
     scalars = unpack_scr[pl.ds(modes_here + 1, bands, stride=block), :]
@@ -363,7 +366,7 @@
 
     even, odd = (
         sum(
-            unpack_scr[pl.ds(start + piece, bands // 2, stride=2 * block), :] for piece in range(3)
+            unpack_scr[pl.ds(start + piece, bands // 2, stride=2 * block), :] for piece in range(2)
         )
         for start in (modes_here + 2, modes_here + 2 + block)
     )
@@ -487,17 +490,17 @@
         gradient_kernel,
         [SMEM, SMEM, SMEM] + [VMEM] * 6,
         (
-            shape((bands * 12, LANES), bf16),
+            shape((bands * 10, LANES), bf16),
             shape((rows + 8, LANES), f32),
             shape((8, LANES), f32),
             shape((1, columns), f32),
             shape((1, columns), f32),
         ),
-        [whole, vmem((bands * 12, LANES), f32)],
+        [whole, vmem((bands * 10, LANES), f32)],
         "gradient",
     )(meta, selection, target, col_tile, wgt_tile, sent, tt, first, last)
-    send = send.reshape(bands, 6, 2, LANES)
-    col_modes = lax.all_to_all(send, "space", 0, 0, tiled=True).reshape(bands * 12, LANES)
+    send = send.reshape(bands, 5, 2, LANES)
+    col_modes = lax.all_to_all(send, "space", 0, 0, tiled=True).reshape(bands * 10, LANES)
 
     near = jnp.where(stay_first > 0.0, own, swap)
     far = swapped(near, "particle", 1)
@@ -506,19 +509,19 @@
     send = call(
         spectral_kernel,
         [SMEM, SMEM, VMEM, VMEM, VMEM, VMEM, VMEM, VMEM],
-        shape((bands * (modes_here + 6), LANES), bf16),
-        [vmem((bands * (modes_here + 6), LANES), f32), vmem((bands * 12, LANES), f32)],
+        shape((bands * (modes_here + 4), LANES), bf16),
+        [vmem((bands * (modes_here + 4), LANES), f32), vmem((bands * 10, LANES), f32)],
         "spectral",
     )(meta, selection, col_modes, sent, spectrum, part, tt, ht_all)
-    send = send.reshape(bands, modes_here // 2 + 3, 2, LANES)
+    send = send.reshape(bands, modes_here // 2 + 2, 2, LANES)
     band_modes = lax.all_to_all(send, "space", 0, 0, tiled=True)
-    band_modes = band_modes.reshape(bands * (modes_here + 6), LANES)
+    band_modes = band_modes.reshape(bands * (modes_here + 4), LANES)
 
     field, part = call(
         relax_kernel,
         [VMEM, VMEM, VMEM, HBM, VMEM, VMEM],
         (shape((rows, columns), f32), shape((bands, 1, LANES), f32)),
-        [vmem((bands * (modes_here + 6), LANES), f32), tile, padded, padded, padded, whole, dma(())],
+        [vmem((bands * (modes_here + 4), LANES), f32), tile, padded, padded, padded, whole, dma(())],
         "relax",
     )(col_tile, wgt_tile, miss, in_hbm(depth_field), band_modes, tt)
     parts = lax.all_to_all(part, "space", 0, 0, tiled=True)

time: 76.4 us -> 76.1 us (level)
  transfers between devices with their start and end apart: 6 -> 6, of which waited for: 4 -> 4; matrix products, arithmetic and copies ran while one was open for 4% -> 4% of each run, Pallas kernels for 10% -> 11%
where the time goes in v7:
time: 76.1 us; the launch traced here: 75.5 us
  starting transfers between devices  33.8 us (44%)
  waiting for transfers between devices  25.1 us (33%)
  Pallas kernels  10.5 us (14%)
  other arithmetic  4.01 us (5%)
  between operations  2.02 us (3%)
    all_to_all x1, starting transfers between devices, per_device(): lax.all_to_all(send, 'space', 0, 0, tiled=True).reshape(bands * 10, LANES)  11.8 us
    all_to_all x1, waiting for transfers between devices, per_device(): band_modes = lax.all_to_all(send, 'space', 0, 0, tiled=True)  11.2 us
    all_to_all x1, starting transfers between devices, per_device(): lax.all_to_all(sent, 'particle', 0, 0, axis_index_groups=groups, tiled=True)  7.82 us
    all_to_all x1, waiting for transfers between devices, per_device(): parts = lax.all_to_all(part, 'space', 0, 0, tiled=True)  7.51 us
    ppermute x2, starting transfers between devices, swapped(): return lax.ppermute(value, axis, pairs)  6.17 us
    all_to_all x1, waiting for transfers between devices, per_device(): lax.all_to_all(send, 'space', 0, 0, tiled=True).reshape(bands * 10, LANES)  5.81 us
    all_to_all x1, starting transfers between devices, per_device(): band_modes = lax.all_to_all(send, 'space', 0, 0, tiled=True)  4.28 us
    all_to_all x1, starting transfers between devices, per_device(): parts = lax.all_to_all(part, 'space', 0, 0, tiled=True)  3.68 us
  transfers between devices with their start and end apart: 6, of which 4 were waited for; matrix products, arithmetic and copies ran while one was open for 4% of the time, Pallas kernels for 11%

profile of v7, /device:TPU:1, one launch (start us, length us, event | category | flops | bytes accessed | tf_op | source)
XLA Modules:
  0.0 75.5 jit_solution(5025103950221923204)
XLA Ops:
  1.3 0.0 copy-start.1
  1.3 2.6 %observe.1 = (bf16[4,96,128]{2,1,0:T(8,128)(2,1)}, s32[64,128]{1,0:T(8,128)S(1)}, f32[64,128]{1,0:T(8,128)S(1)}, bf16[512,2048]{1,0:T(8,128)(2,1)S(1)}, f32[1,2048]{1,0:T(1,128)S(1)}, /*index=5*/f32[1,2048]{1,0:T(1,128)S(1)}) custom-call(f32[1]{0:T(128)S(6)} %copy.14.lw_ref, s32[16,64]{1,0:T(8,128)} %bitcast.18, f32[16,64]{1,0:T(8,128)} %bitcast.19, ...), custom_call_target="tpu_custom_call" | custom-call | flops 40000000000 | bytes 4000000 | tf_op jit(solution)/shard_map/observe/pallas_call | solution.py:470
  3.9 7.8 %all-to-all-start = ((bf16[4,96,128]{2,1,0:T(8,128)(2,1)}), bf16[4,96,128]{2,1,0:T(8,128)(2,1)S(1)}, u32[]{:S(2)}, u32[]{:S(2)}) async-start(bf16[4,96,128]{2,1,0:T(8,128)(2,1)} %get-tuple-element.24), calls=%async_computation | async-start | bytes 196608 | tf_op jit(solution)/shard_map/all_to_all | solution.py:486
  11.7 3.4 %collective-permute-start = (f32[64,2048]{1,0:T(8,128)}, f32[64,2048]{1,0:T(8,128)}, u32[]{:S(2)}, u32[]{:S(2)}) collective-permute-start(f32[64,2048]{1,0:T(8,128)} %bitcast.4.stream_hbm), channel_id=1, source_target_pairs={{0,32},{32,0},{64,96},{96,64},{128,160},{160,128},{192,224},{224,1... | collective-permute-start | bytes 1572872 | tf_op jit(solution)/shard_map/ppermute | solution.py:441
  15.7 0.1 pad_add_fusion.meta_ref
  15.8 0.6 all-to-all-done.seen_ref.noise_ref
  16.4 0.0 copy-done.1
  16.4 0.0 copy-start
  16.4 0.0 copy-start.2
  16.4 2.8 %gradient.1 = (bf16[320,128]{1,0:T(8,128)(2,1)}, f32[72,128]{1,0:T(8,128)S(1)}, f32[8,128]{1,0:T(8,128)S(1)}, f32[1,2048]{1,0:T(1,128)S(1)}, f32[1,2048]{1,0:T(1,128)S(1)}) custom-call(s32[2]{0:T(128)S(1)} %pad_add_fusion.meta_ref, s32[2,16]{1,0:T(2,128)S(1)} %copy-done.1, f32[1]{0:T(128)S(6)} %copy.15.target_ref, s32[64,128]{1,0:T(8,128)S(1)} %get-tuple-element.21.col_scr, ...), custom_call_target="tpu_custom_call" | custom-call | flops 40000000000 | bytes 4000000 | tf_op jit(solution)/shard_map/gradient/pallas_call | solution.py:489
  19.2 11.8 %all-to-all-start.1 = ((bf16[32,5,2,128]{3,2,1,0:T(2,128)(2,1)}), bf16[32,5,2,128]{3,2,1,0:T(2,128)(2,1)S(1)}, u32[]{:S(2)}, u32[]{:S(2)}) async-start(bf16[32,5,2,128]{3,2,1,0:T(2,128)(2,1)} %bitcast.7), calls=%async_computation.1 | async-start | bytes 163840 | tf_op jit(solution)/shard_map/all_to_all | solution.py:503
  31.1 0.0 collective-permute-done
  31.1 1.3 %broadcast_select_fusion = f32[64,2048]{1,0:T(8,128)S(1)} fusion(f32[64,2048]{1,0:T(8,128)} %collective-permute-done, pred[2048]{0:T(1024)(128)(4,1)S(1)} %compare_reduce_fusion.1, f32[1,64,2048]{2,1,0:T(8,128)} %param.12), kind=kLoop, calls=%fused_computation.1 | loop fusion | flops 131072 | bytes 1574912 | tf_op jit(solution)/shard_map/jit(_where)/select_n | solution.py:505
  32.3 2.8 %collective-permute-start.1 = (f32[64,2048]{1,0:T(8,128)S(1)}, f32[64,2048]{1,0:T(8,128)}, u32[]{:S(2)}, u32[]{:S(2)}) collective-permute-start(f32[64,2048]{1,0:T(8,128)S(1)} %broadcast_select_fusion), channel_id=1, source_target_pairs={{0,64},{32,96},{64,0},{96,32},{128,192},{160,224},{192,128},{224,1... | collective-permute-start | bytes 1572872 | tf_op jit(solution)/shard_map/ppermute | solution.py:441
  35.2 5.8 %all-to-all-done.1 = bf16[32,5,2,128]{3,2,1,0:T(2,128)(2,1)S(1)} async-done(((bf16[32,5,2,128]{3,2,1,0:T(2,128)(2,1)}), bf16[32,5,2,128]{3,2,1,0:T(2,128)(2,1)S(1)}, u32[]{:S(2)}, u32[]{:S(2)}) %all-to-all-start.1) | async-done | bytes 81952 | tf_op jit(solution)/shard_map/all_to_all | solution.py:503
  41.0 0.0 copy-done
  41.0 0.0 copy-done.2
  41.0 2.5 %spectral.1 = bf16[640,128]{1,0:T(8,128)(2,1)} custom-call(s32[2]{0:T(128)S(1)} %pad_add_fusion.meta_ref, s32[2,16]{1,0:T(2,128)S(1)} %copy-done.1, bf16[320,128]{1,0:T(8,128)(2,1)S(1)} %bitcast.15, bf16[4,96,128]{2,1,0:T(8,128)(2,1)S(1)} %all-to-all-done.seen_ref.noise_ref, f32[16,512]{1,0:T(8,128)S(1)} %copy-done, ...), custom_call_target="tpu_custom_call" | custom-call | flops 1000000000 | bytes 4000000 | tf_op jit(solution)/shard_map/spectral/pallas_call | solution.py:509
  43.4 4.3 %all-to-all-start.2 = ((bf16[32,10,2,128]{3,2,1,0:T(2,128)(2,1)}), bf16[32,10,2,128]{3,2,1,0:T(2,128)(2,1)S(1)}, u32[]{:S(2)}, u32[]{:S(2)}) async-start(bf16[32,10,2,128]{3,2,1,0:T(2,128)(2,1)} %bitcast.9), calls=%async_computation.2 | async-start | bytes 327680 | tf_op jit(solution)/shard_map/all_to_all | solution.py:517
  47.8 11.2 %all-to-all-done.2 = bf16[32,10,2,128]{3,2,1,0:T(2,128)(2,1)S(1)} async-done(((bf16[32,10,2,128]{3,2,1,0:T(2,128)(2,1)}), bf16[32,10,2,128]{3,2,1,0:T(2,128)(2,1)S(1)}, u32[]{:S(2)}, u32[]{:S(2)}) %all-to-all-start.2) | async-done | bytes 163872 | tf_op jit(solution)/shard_map/all_to_all | solution.py:517
  59.0 2.7 %relax.1 = (f32[64,2048]{1,0:T(8,128)S(1)}, f32[32,1,128]{2,1,0:T(1,128)}) custom-call(s32[64,128]{1,0:T(8,128)S(1)} %get-tuple-element.21.col_scr, f32[64,128]{1,0:T(8,128)S(1)} %get-tuple-element.22.wgt_scr, f32[72,128]{1,0:T(8,128)S(1)} %get-tuple-element.28.miss_ref, f32[64,2048]{1,0:T(8,128)} %depth_hbm.3, bf16[640,128]{1,0:T(8,128)(2,1)S(1)} %bitcast.14, ...), custom_call_target="tpu_custom_call" | custom-call | flops 1000000000 | bytes 4000000 | tf_op jit(solution)/shard_map/relax/pallas_call | solution.py:520
  61.7 3.7 %all-to-all-start.3 = ((f32[32,1,128]{2,1,0:T(1,128)}), f32[32,1,128]{2,1,0:T(1,128)S(1)}, u32[]{:S(2)}, u32[]{:S(2)}) async-start(f32[32,1,128]{2,1,0:T(1,128)} %get-tuple-element.34), calls=%async_computation.3 | async-start | bytes 32768 | tf_op jit(solution)/shard_map/all_to_all | solution.py:527
  65.4 0.0 collective-permute-done.1
  65.4 2.0 %select_add_fusion = f32[64,2048]{1,0:T(8,128)} fusion(f32[64,2048]{1,0:T(8,128)S(1)} %get-tuple-element.35, f32[64,2048]{1,0:T(8,128)S(1)} %broadcast_select_fusion, f32[64,2048]{1,0:T(8,128)} %collective-permute-done.1, pred[2048]{0:T(1024)(128)(4,1)S(1)} %compare_reduce_fusion), kind=kLoop, calls=%fused_computation | loop fusion | flops 262144 | bytes 2099200 | tf_op jit(solution)/shard_map/add | solution.py:528
  67.3 7.5 %all-to-all-done.3 = f32[32,1,128]{2,1,0:T(1,128)S(1)} async-done(((f32[32,1,128]{2,1,0:T(1,128)}), f32[32,1,128]{2,1,0:T(1,128)S(1)}, u32[]{:S(2)}, u32[]{:S(2)}) %all-to-all-start.3) | async-done | bytes 16416 | tf_op jit(solution)/shard_map/all_to_all | solution.py:527
  74.9 0.6 slice_reduce_fusion
  (2 shorter events, 0.1 us)
Async XLA Ops:
  1.3 15.1 %copy-start.1 = (s32[2,16]{1,0:T(2,128)S(1)}, s32[2,16]{1,0:T(2,128)}, u32[]{:S(2)}) copy-start(s32[2,16]{1,0:T(2,128)} %sel_ref.3) | copy-start | bytes 388
  3.9 12.5 %all-to-all-start = ((bf16[4,96,128]{2,1,0:T(8,128)(2,1)}), bf16[4,96,128]{2,1,0:T(8,128)(2,1)S(1)}, u32[]{:S(2)}, u32[]{:S(2)}) async-start(bf16[4,96,128]{2,1,0:T(8,128)(2,1)} %get-tuple-element.24), calls=%async_computation | async-start | bytes 196608 | tf_op jit(solution)/shard_map/all_to_all | solution.py:486
  11.7 19.4 %collective-permute-start = (f32[64,2048]{1,0:T(8,128)}, f32[64,2048]{1,0:T(8,128)}, u32[]{:S(2)}, u32[]{:S(2)}) collective-permute-start(f32[64,2048]{1,0:T(8,128)} %bitcast.4.stream_hbm), channel_id=1, source_target_pairs={{0,32},{32,0},{64,96},{96,64},{128,160},{160,128},{192,224},{224,1... | collective-permute-start | bytes 1572872 | tf_op jit(solution)/shard_map/ppermute | solution.py:441
  16.4 24.6 %copy-start = (f32[16,512]{1,0:T(8,128)S(1)}, f32[16,512]{1,0:T(8,128)}, u32[]{:S(2)}) copy-start(f32[16,512]{1,0:T(8,128)} %spec_ref.1) | copy-start | bytes 98308
  16.4 24.6 %copy-start.2 = (bf16[128,512]{1,0:T(8,128)(2,1)S(1)}, bf16[128,512]{1,0:T(8,128)(2,1)}, u32[]{:S(2)}) copy-start(bf16[128,512]{1,0:T(8,128)(2,1)} %constant.17.clone.ht_ref) | copy-start | bytes 393220
  19.2 21.8 %all-to-all-start.1 = ((bf16[32,5,2,128]{3,2,1,0:T(2,128)(2,1)}), bf16[32,5,2,128]{3,2,1,0:T(2,128)(2,1)S(1)}, u32[]{:S(2)}, u32[]{:S(2)}) async-start(bf16[32,5,2,128]{3,2,1,0:T(2,128)(2,1)} %bitcast.7), calls=%async_computation.1 | async-start | bytes 163840 | tf_op jit(solution)/shard_map/all_to_all | solution.py:503
  32.3 33.0 %collective-permute-start.1 = (f32[64,2048]{1,0:T(8,128)S(1)}, f32[64,2048]{1,0:T(8,128)}, u32[]{:S(2)}, u32[]{:S(2)}) collective-permute-start(f32[64,2048]{1,0:T(8,128)S(1)} %broadcast_select_fusion), channel_id=1, source_target_pairs={{0,64},{32,96},{64,0},{96,32},{128,192},{160,224},{192,128},{224,1... | collective-permute-start | bytes 1572872 | tf_op jit(solution)/shard_map/ppermute | solution.py:441
  43.4 15.5 %all-to-all-start.2 = ((bf16[32,10,2,128]{3,2,1,0:T(2,128)(2,1)}), bf16[32,10,2,128]{3,2,1,0:T(2,128)(2,1)S(1)}, u32[]{:S(2)}, u32[]{:S(2)}) async-start(bf16[32,10,2,128]{3,2,1,0:T(2,128)(2,1)} %bitcast.9), calls=%async_computation.2 | async-start | bytes 327680 | tf_op jit(solution)/shard_map/all_to_all | solution.py:517
  61.7 13.2 %all-to-all-start.3 = ((f32[32,1,128]{2,1,0:T(1,128)}), f32[32,1,128]{2,1,0:T(1,128)S(1)}, u32[]{:S(2)}, u32[]{:S(2)}) async-start(f32[32,1,128]{2,1,0:T(1,128)} %get-tuple-element.34), calls=%async_computation.3 | async-start | bytes 32768 | tf_op jit(solution)/shard_map/all_to_all | solution.py:527

commit v8 on v7

--- a/solution.py
+++ b/solution.py
@@ -40,6 +40,11 @@
 
 def lane_iota():
     return lax.broadcasted_iota(jnp.int32, (8, LANES), 1)
+
+
+def parity_sign(shape, axis):
+    place = lax.broadcasted_iota(jnp.int32, shape, axis)
+    return (1 - 2 * (place & 1)).astype(jnp.float32)
 
 
 def summed(values):
@@ -149,7 +154,7 @@
 ):
     rows = grad_scr.shape[0]
     per_row = LANES * 8 // rows
-    columns = tt_ref.shape[1]
+    columns = 2 * tt_ref.shape[1]
     position = source_slot(sel_ref, meta_ref) & (GROUP - 1)
     first = seen_ref.shape[1] - 32
     sent = seen_ref[position][first:, :].astype(jnp.float32)
@@ -203,13 +208,21 @@
                 chunk * 8 : chunk * 8 + 8, :
             ]
     gradient = grad_scr[...].astype(jnp.bfloat16)
+    gradient = jnp.concatenate([gradient[:, : columns // 2], gradient[:, columns // 2 :]], axis=0)
     modes = lax.dot_general(
         tt_ref[...], gradient, (((1,), (1,)), ((), ())), preferred_element_type=jnp.float32
     )
+    half = LANES // 2
     bands = modes.shape[0] // 16
     block = send_ref.shape[0] // bands
-    split = modes.reshape(bands, 2, 8, rows)
-    values = jnp.concatenate([split[:, 0], split[:, 1]], axis=2)
+    modes = modes + parity_sign(modes.shape, 0) * pltpu.roll(modes, half, axis=1)
+    split = modes.reshape(bands, 2, 8, LANES)
+    small = (bands, 8, LANES)
+    values = jnp.where(
+        lax.broadcasted_iota(jnp.int32, small, 2) < half,
+        split[:, 0],
+        parity_sign(small, 1) * split[:, 1],
+    )
     pairs = columns // LANES
     top, bottom = (
         jnp.concatenate(
@@ -217,7 +230,6 @@
         )
         for ref in (top_ref, bottom_ref)
     )
-    half = LANES // 2
     low = lax.broadcasted_iota(jnp.int32, (pairs, LANES), 1) < half
     even = split2(jnp.where(low, top, pltpu.roll(bottom, half, axis=1)))
     odd = split2(jnp.where(low, pltpu.roll(top, half, axis=1), bottom))
@@ -238,7 +250,7 @@
     modes_here, n_modes = spec_ref.shape
     bands = n_modes // modes_here
     unpack_scr[...] = modes_ref[...].astype(jnp.float32)
-    rows = tt_ref.shape[1]
+    rows = 2 * tt_ref.shape[1]
     norm_factor = 4.0 / (rows * rows)
     position = source_slot(sel_ref, meta_ref) & (GROUP - 1)
     lane = lane_iota()
@@ -249,12 +261,18 @@
         odd = unpack_scr[20 * pair + 10 : 20 * pair + 18, :]
         tops.append(jnp.where(low, even, pltpu.roll(odd, half, axis=1)))
         bottoms.append(jnp.where(low, pltpu.roll(even, half, axis=1), odd))
+    folded = bands // 4
     columns = jnp.concatenate(
-        [jnp.concatenate(tops, axis=1), jnp.concatenate(bottoms, axis=1)], axis=0
+        [
+            jnp.concatenate(part, axis=1)
+            for part in (tops[:folded], bottoms[:folded], tops[folded:], bottoms[folded:])
+        ],
+        axis=0,
     ).astype(jnp.bfloat16)
-    coefficients = lax.dot_general(
+    sums = lax.dot_general(
         columns, tt_ref[...], (((1,), (1,)), ((), ())), preferred_element_type=jnp.float32
     )
+    coefficients = sums[:modes_here] + parity_sign(spec_ref.shape, 1) * sums[modes_here:]
     scaled = norm_factor * spec_ref[...]
     weighted = coefficients * scaled
     energy = summed(coefficients * weighted)
@@ -265,7 +283,12 @@
     shaped = (jnp.sqrt(scaled) * noise.astype(jnp.float32)).astype(jnp.bfloat16)
     weighted = weighted.astype(jnp.bfloat16)
     stacked = jnp.concatenate([weighted, shaped], axis=0)
-    inverted = jnp.dot(stacked, tt_ref[...], preferred_element_type=jnp.float32)
+    flipped = stacked.astype(jnp.float32) * parity_sign(stacked.shape, 1)
+    both = jnp.concatenate([stacked, flipped.astype(jnp.bfloat16)], axis=0)
+    inverted = jnp.dot(both, tt_ref[...], preferred_element_type=jnp.float32)
+    inverted = jnp.concatenate(
+        [inverted[: 2 * modes_here], inverted[2 * modes_here :]], axis=1
+    )
     depth = sum(unpack_scr[pl.ds(8 + piece, bands, stride=10), :] for piece in range(2))
     band_row = lax.broadcasted_iota(jnp.int32, (bands, LANES), 0)
     band_low = lax.broadcasted_iota(jnp.int32, (bands, LANES), 1) < half
@@ -323,7 +346,7 @@
     def rate(depth):
         return RELAX_RATE * depth / (4.0 * depth + STRETCH)
 
-    n_modes, columns = tt_ref.shape
+    n_modes, columns = tt_ref.shape[0], 2 * tt_ref.shape[1]
     bands = part_ref.shape[0]
     modes_here = n_modes // bands
     lane = lane_iota()
@@ -350,9 +373,20 @@
     step = (misfit + weight) / (energy + 1.0)
     main = jnp.concatenate(
         [unpack_scr[at * block : at * block + modes_here, :] for at in range(bands)], axis=0
-    ).astype(jnp.bfloat16)
-    pulled = lax.dot_general(main, tt_ref[...], (((0,), (0,)), ((), ())), preferred_element_type=jnp.float32)
-    pulled_h = jnp.dot(halo.astype(jnp.bfloat16), tt_ref[...], preferred_element_type=jnp.float32)
+    )
+    both = jnp.concatenate([main, main * parity_sign(main.shape, 0)], axis=1)
+    pulled = lax.dot_general(
+        both.astype(jnp.bfloat16),
+        tt_ref[...],
+        (((0,), (0,)), ((), ())),
+        preferred_element_type=jnp.float32,
+    )
+    pulled = jnp.concatenate([pulled[:LANES], pulled[LANES:]], axis=1)
+    both = jnp.concatenate([halo, halo * parity_sign(halo.shape, 1)], axis=0)
+    pulled_h = jnp.dot(
+        both.astype(jnp.bfloat16), tt_ref[...], preferred_element_type=jnp.float32
+    )
+    pulled_h = jnp.concatenate([pulled_h[:8], pulled_h[8:]], axis=1)
     for at in range(0, rows, 8):
         inc_scr[at : at + 8, :] = step * pulled[at : at + 8] + NOISE_AMP * pulled[rows + at : rows + at + 8]
     edge = pulled_h
@@ -451,7 +485,7 @@
     bands = lax.axis_size("space")
     particles = lax.axis_size("particle")
     y_table = table(rows * bands, n_modes // 2)
-    tt_all = jnp.asarray(np.ascontiguousarray(y_table.T))
+    tt_all = jnp.asarray(np.ascontiguousarray(y_table[: columns // 2].T))
     ht_all = jnp.asarray(halo_table(y_table, bands))
     f32, bf16 = jnp.float32, jnp.bfloat16
     shape = jax.ShapeDtypeStruct
@@ -474,7 +508,7 @@
             shape((GROUP, modes_here * n_modes // LANES + 32, LANES), bf16),
             shape((rows, LANES), jnp.int32),
             shape((rows, LANES), f32),
-            shape((n_modes, columns), bf16),
+            shape((n_modes, columns // 2), bf16),
             shape((1, columns), f32),
             shape((1, columns), f32),
         ),

time: 76.1 us -> 75.6 us (level)
  waiting for transfers between devices: 25.1 us -> 27.8 us
  other arithmetic: 4.01 us -> 1.74 us
  Pallas kernels: 10.5 us -> 9.54 us
    select_n x1, other arithmetic: 1.26 us -> 0.06 us  [per_device(): near = jnp.where(stay_first > 0.0, own, swap)]
    all_to_all x1, waiting for transfers between devices: 5.81 us -> 6.99 us  [per_device(): lax.all_to_all(send, 'space', 0, 0, tiled=True).reshape(bands * 10, LANES)]
    all_to_all x1, waiting for transfers between devices: 7.51 us -> 8.58 us  [per_device(): parts = lax.all_to_all(part, 'space', 0, 0, tiled=True)]
    add x1, other arithmetic: 1.96 us -> 0.9 us  [per_device(): analysis = field + jnp.where(stay_second > 0.0, near, far)]
  transfers between devices with their start and end apart: 6 -> 6, of which waited for: 4 -> 4; matrix products, arithmetic and copies ran while one was open for 4% -> 1% of each run, Pallas kernels for 11% -> 10%
where the time goes in v8:
time: 75.6 us; the launch traced here: 75.1 us
  starting transfers between devices  33.3 us (44%)
  waiting for transfers between devices  27.8 us (37%)
  Pallas kernels  9.54 us (13%)
  between operations  2.04 us (3%)
  other arithmetic  1.74 us (2%)
    all_to_all x1, starting transfers between devices, per_device(): lax.all_to_all(send, 'space', 0, 0, tiled=True).reshape(bands * 10, LANES)  11.7 us
    all_to_all x1, waiting for transfers between devices, per_device(): band_modes = lax.all_to_all(send, 'space', 0, 0, tiled=True)  11.5 us
    all_to_all x1, waiting for transfers between devices, per_device(): parts = lax.all_to_all(part, 'space', 0, 0, tiled=True)  8.58 us
    all_to_all x1, starting transfers between devices, per_device(): lax.all_to_all(sent, 'particle', 0, 0, axis_index_groups=groups, tiled=True)  7.82 us
    all_to_all x1, waiting for transfers between devices, per_device(): lax.all_to_all(send, 'space', 0, 0, tiled=True).reshape(bands * 10, LANES)  6.99 us
    ppermute x2, starting transfers between devices, swapped(): return lax.ppermute(value, axis, pairs)  6.16 us
    all_to_all x1, starting transfers between devices, per_device(): band_modes = lax.all_to_all(send, 'space', 0, 0, tiled=True)  3.85 us
    all_to_all x1, starting transfers between devices, per_device(): parts = lax.all_to_all(part, 'space', 0, 0, tiled=True)  3.74 us
  transfers between devices with their start and end apart: 6, of which 4 were waited for; matrix products, arithmetic and copies ran while one was open for 1% of the time, Pallas kernels for 10%

profile of v8, /device:TPU:1, one launch (start us, length us, event | category | flops | bytes accessed | tf_op | source)
XLA Modules:
  0.0 75.1 jit_solution(17017366895356677995)
XLA Ops:
  1.3 0.0 copy-start.3
  1.3 2.3 %observe.1 = (bf16[4,96,128]{2,1,0:T(8,128)(2,1)}, s32[64,128]{1,0:T(8,128)S(1)}, f32[64,128]{1,0:T(8,128)S(1)}, bf16[512,1024]{1,0:T(8,128)(2,1)S(1)}, f32[1,2048]{1,0:T(1,128)S(1)}, /*index=5*/f32[1,2048]{1,0:T(1,128)S(1)}) custom-call(f32[1]{0:T(128)S(6)} %copy.14.lw_ref, s32[16,64]{1,0:T(8,128)} %bitcast.20, f32[16,64]{1,0:T(8,128)} %bitcast.21, ...), custom_call_target="tpu_custom_call" | custom-call | flops 40000000000 | bytes 4000000 | tf_op jit(solution)/shard_map/observe/pallas_call | solution.py:504
  3.6 7.8 %all-to-all-start = ((bf16[4,96,128]{2,1,0:T(8,128)(2,1)}), bf16[4,96,128]{2,1,0:T(8,128)(2,1)S(1)}, u32[]{:S(2)}, u32[]{:S(2)}) async-start(bf16[4,96,128]{2,1,0:T(8,128)(2,1)} %get-tuple-element.24), calls=%async_computation | async-start | bytes 196608 | tf_op jit(solution)/shard_map/all_to_all | solution.py:520
  11.4 0.0 copy-done.3
  11.4 3.4 %collective-permute-start = (f32[64,2048]{1,0:T(8,128)S(1)}, f32[64,2048]{1,0:T(8,128)S(1)}, u32[]{:S(2)}, u32[]{:S(2)}) collective-permute-start(f32[64,2048]{1,0:T(8,128)S(1)} %bitcast.18), channel_id=1, source_target_pairs={{0,32},{32,0},{64,96},{96,64},{128,160},{160,128},{192,224},{224,1... | collective-permute-start | bytes 1572872 | tf_op jit(solution)/shard_map/ppermute | solution.py:475
  15.4 0.1 pad_add_fusion.meta_ref
  15.5 0.7 all-to-all-done.seen_ref.noise_ref
  16.2 0.0 copy-start.1
  16.2 0.7 copy-done.1
  16.9 2.5 %gradient.1 = (bf16[320,128]{1,0:T(8,128)(2,1)}, f32[72,128]{1,0:T(8,128)S(1)}, f32[8,128]{1,0:T(8,128)S(1)}, f32[1,2048]{1,0:T(1,128)S(1)}, f32[1,2048]{1,0:T(1,128)S(1)}) custom-call(s32[2]{0:T(128)S(1)} %pad_add_fusion.meta_ref, s32[2,16]{1,0:T(2,128)S(1)} %copy-done.1, f32[1]{0:T(128)S(6)} %copy.15.target_ref, s32[64,128]{1,0:T(8,128)S(1)} %get-tuple-element.21.col_scr, ...), custom_call_target="tpu_custom_call" | custom-call | flops 40000000000 | bytes 4000000 | tf_op jit(solution)/shard_map/gradient/pallas_call | solution.py:523
  19.4 11.7 %all-to-all-start.1 = ((bf16[32,5,2,128]{3,2,1,0:T(2,128)(2,1)}), bf16[32,5,2,128]{3,2,1,0:T(2,128)(2,1)S(1)}, u32[]{:S(2)}, u32[]{:S(2)}) async-start(bf16[32,5,2,128]{3,2,1,0:T(2,128)(2,1)} %bitcast.7), calls=%async_computation.1 | async-start | bytes 163840 | tf_op jit(solution)/shard_map/all_to_all | solution.py:537
  31.2 0.0 copy-start
  31.2 0.0 copy-start.2
  31.2 0.0 collective-permute-done
  31.2 0.1 broadcast_select_fusion
  31.3 2.8 %collective-permute-start.1 = (f32[64,2048]{1,0:T(8,128)S(1)}, f32[64,2048]{1,0:T(8,128)S(1)}, u32[]{:S(2)}, u32[]{:S(2)}) collective-permute-start(f32[64,2048]{1,0:T(8,128)S(1)} %broadcast_select_fusion), channel_id=1, source_target_pairs={{0,64},{32,96},{64,0},{96,32},{128,192},{160,224},{192,128},{224,1... | collective-permute-start | bytes 1572872 | tf_op jit(solution)/shard_map/ppermute | solution.py:475
  34.1 7.0 %all-to-all-done.1 = bf16[32,5,2,128]{3,2,1,0:T(2,128)(2,1)S(1)} async-done(((bf16[32,5,2,128]{3,2,1,0:T(2,128)(2,1)}), bf16[32,5,2,128]{3,2,1,0:T(2,128)(2,1)S(1)}, u32[]{:S(2)}, u32[]{:S(2)}) %all-to-all-start.1) | async-done | bytes 81952 | tf_op jit(solution)/shard_map/all_to_all | solution.py:537
  41.1 0.0 copy-done
  41.1 0.0 copy-done.2
  41.1 2.1 %spectral.1 = bf16[640,128]{1,0:T(8,128)(2,1)} custom-call(s32[2]{0:T(128)S(1)} %pad_add_fusion.meta_ref, s32[2,16]{1,0:T(2,128)S(1)} %copy-done.1, bf16[320,128]{1,0:T(8,128)(2,1)S(1)} %bitcast.15, bf16[4,96,128]{2,1,0:T(8,128)(2,1)S(1)} %all-to-all-done.seen_ref.noise_ref, f32[16,512]{1,0:T(8,128)S(1)} %copy-done, ...), custom_call_target="tpu_custom_call" | custom-call | flops 1000000000 | bytes 4000000 | tf_op jit(solution)/shard_map/spectral/pallas_call | solution.py:543
  43.2 3.9 %all-to-all-start.2 = ((bf16[32,10,2,128]{3,2,1,0:T(2,128)(2,1)}), bf16[32,10,2,128]{3,2,1,0:T(2,128)(2,1)S(1)}, u32[]{:S(2)}, u32[]{:S(2)}) async-start(bf16[32,10,2,128]{3,2,1,0:T(2,128)(2,1)} %bitcast.9), calls=%async_computation.2 | async-start | bytes 327680 | tf_op jit(solution)/shard_map/all_to_all | solution.py:551
  47.1 11.5 %all-to-all-done.2 = bf16[32,10,2,128]{3,2,1,0:T(2,128)(2,1)S(1)} async-done(((bf16[32,10,2,128]{3,2,1,0:T(2,128)(2,1)}), bf16[32,10,2,128]{3,2,1,0:T(2,128)(2,1)S(1)}, u32[]{:S(2)}, u32[]{:S(2)}) %all-to-all-start.2) | async-done | bytes 163872 | tf_op jit(solution)/shard_map/all_to_all | solution.py:551
  58.6 2.7 %relax.1 = (f32[64,2048]{1,0:T(8,128)S(1)}, f32[32,1,128]{2,1,0:T(1,128)}) custom-call(s32[64,128]{1,0:T(8,128)S(1)} %get-tuple-element.21.col_scr, f32[64,128]{1,0:T(8,128)S(1)} %get-tuple-element.22.wgt_scr, f32[72,128]{1,0:T(8,128)S(1)} %get-tuple-element.28.miss_ref, f32[64,2048]{1,0:T(8,128)} %depth_hbm.3, bf16[640,128]{1,0:T(8,128)(2,1)S(1)} %bitcast.14, ...), custom_call_target="tpu_custom_call" | custom-call | flops 1000000000 | bytes 4000000 | tf_op jit(solution)/shard_map/relax/pallas_call | solution.py:554
  61.2 3.7 %all-to-all-start.3 = ((f32[32,1,128]{2,1,0:T(1,128)}), f32[32,1,128]{2,1,0:T(1,128)S(1)}, u32[]{:S(2)}, u32[]{:S(2)}) async-start(f32[32,1,128]{2,1,0:T(1,128)} %get-tuple-element.34), calls=%async_computation.3 | async-start | bytes 32768 | tf_op jit(solution)/shard_map/all_to_all | solution.py:561
  65.0 0.0 collective-permute-done.1
  65.0 0.9 %select_add_fusion = f32[64,2048]{1,0:T(8,128)} fusion(f32[64,2048]{1,0:T(8,128)S(1)} %get-tuple-element.35, f32[64,2048]{1,0:T(8,128)S(1)} %broadcast_select_fusion, f32[64,2048]{1,0:T(8,128)S(1)} %collective-permute-done.1, pred[2048]{0:T(1024)(128)(4,1)S(1)} %compare_reduce_fusion), kind=kLoop, calls=%fused_computation | loop fusion | flops 262144 | bytes 2099200 | tf_op jit(solution)/shard_map/add | solution.py:562
  65.9 8.6 %all-to-all-done.3 = f32[32,1,128]{2,1,0:T(1,128)S(1)} async-done(((f32[32,1,128]{2,1,0:T(1,128)}), f32[32,1,128]{2,1,0:T(1,128)S(1)}, u32[]{:S(2)}, u32[]{:S(2)}) %all-to-all-start.3) | async-done | bytes 16416 | tf_op jit(solution)/shard_map/all_to_all | solution.py:561
  74.5 0.6 slice_reduce_fusion
  (2 shorter events, 0.1 us)
Async XLA Ops:
  1.3 10.1 %copy-start.3 = (f32[1,64,2048]{2,1,0:T(8,128)S(1)}, f32[1,64,2048]{2,1,0:T(8,128)}, u32[]{:S(2)}) copy-start(f32[1,64,2048]{2,1,0:T(8,128)} %param.12) | copy-start | bytes 1572868
  3.6 12.6 %all-to-all-start = ((bf16[4,96,128]{2,1,0:T(8,128)(2,1)}), bf16[4,96,128]{2,1,0:T(8,128)(2,1)S(1)}, u32[]{:S(2)}, u32[]{:S(2)}) async-start(bf16[4,96,128]{2,1,0:T(8,128)(2,1)} %get-tuple-element.24), calls=%async_computation | async-start | bytes 196608 | tf_op jit(solution)/shard_map/all_to_all | solution.py:520
  11.4 19.8 %collective-permute-start = (f32[64,2048]{1,0:T(8,128)S(1)}, f32[64,2048]{1,0:T(8,128)S(1)}, u32[]{:S(2)}, u32[]{:S(2)}) collective-permute-start(f32[64,2048]{1,0:T(8,128)S(1)} %bitcast.18), channel_id=1, source_target_pairs={{0,32},{32,0},{64,96},{96,64},{128,160},{160,128},{192,224},{224,1... | collective-permute-start | bytes 1572872 | tf_op jit(solution)/shard_map/ppermute | solution.py:475
  16.2 0.7 copy-start.1
  19.4 21.7 %all-to-all-start.1 = ((bf16[32,5,2,128]{3,2,1,0:T(2,128)(2,1)}), bf16[32,5,2,128]{3,2,1,0:T(2,128)(2,1)S(1)}, u32[]{:S(2)}, u32[]{:S(2)}) async-start(bf16[32,5,2,128]{3,2,1,0:T(2,128)(2,1)} %bitcast.7), calls=%async_computation.1 | async-start | bytes 163840 | tf_op jit(solution)/shard_map/all_to_all | solution.py:537
  31.2 9.9 %copy-start = (f32[16,512]{1,0:T(8,128)S(1)}, f32[16,512]{1,0:T(8,128)}, u32[]{:S(2)}) copy-start(f32[16,512]{1,0:T(8,128)} %spec_ref.1) | copy-start | bytes 98308
  31.2 9.9 %copy-start.2 = (bf16[128,512]{1,0:T(8,128)(2,1)S(1)}, bf16[128,512]{1,0:T(8,128)(2,1)}, u32[]{:S(2)}) copy-start(bf16[128,512]{1,0:T(8,128)(2,1)} %constant.17.clone.ht_ref) | copy-start | bytes 393220
  31.3 33.7 %collective-permute-start.1 = (f32[64,2048]{1,0:T(8,128)S(1)}, f32[64,2048]{1,0:T(8,128)S(1)}, u32[]{:S(2)}, u32[]{:S(2)}) collective-permute-start(f32[64,2048]{1,0:T(8,128)S(1)} %broadcast_select_fusion), channel_id=1, source_target_pairs={{0,64},{32,96},{64,0},{96,32},{128,192},{160,224},{192,128},{224,1... | collective-permute-start | bytes 1572872 | tf_op jit(solution)/shard_map/ppermute | solution.py:475
  43.2 15.4 %all-to-all-start.2 = ((bf16[32,10,2,128]{3,2,1,0:T(2,128)(2,1)}), bf16[32,10,2,128]{3,2,1,0:T(2,128)(2,1)S(1)}, u32[]{:S(2)}, u32[]{:S(2)}) async-start(bf16[32,10,2,128]{3,2,1,0:T(2,128)(2,1)} %bitcast.9), calls=%async_computation.2 | async-start | bytes 327680 | tf_op jit(solution)/shard_map/all_to_all | solution.py:551
  61.2 13.2 %all-to-all-start.3 = ((f32[32,1,128]{2,1,0:T(1,128)}), f32[32,1,128]{2,1,0:T(1,128)S(1)}, u32[]{:S(2)}, u32[]{:S(2)}) async-start(f32[32,1,128]{2,1,0:T(1,128)} %get-tuple-element.34), calls=%async_computation.3 | async-start | bytes 32768 | tf_op jit(solution)/shard_map/all_to_all | solution.py:561

commit v9 on v8

--- a/solution.py
+++ b/solution.py
@@ -63,10 +63,15 @@
     return high, mid, rest - mid
 
 
-def source_slot(sel_ref, meta_ref):
-    slot = meta_ref[0]
-    one = jnp.where(sel_ref[1, slot] < 1, slot, slot ^ 2)
-    return jnp.where(sel_ref[0, one] < 1, one, one ^ 1)
+def chosen(info_ref, section, slot):
+    per_section = (info_ref.shape[0] - 2) // 2
+    return info_ref[2 + section * per_section + slot]
+
+
+def source_slot(info_ref):
+    slot = info_ref[0]
+    one = jnp.where(chosen(info_ref, 1, slot) < 1, slot, slot ^ 2)
+    return jnp.where(chosen(info_ref, 0, one) < 1, one, one ^ 1)
 
 
 def fill_tile(source_ref, scr):
@@ -149,20 +154,20 @@
 
 
 def gradient_kernel(
-    meta_ref, sel_ref, target_ref, col_scr, wgt_scr, seen_ref, tt_ref, top_ref, bottom_ref,
+    info_ref, target_ref, col_scr, wgt_scr, seen_ref, tt_ref, top_ref, bottom_ref,
     send_ref, miss_ref, part_ref, first_ref, second_ref, grad_scr, pack_scr,
 ):
     rows = grad_scr.shape[0]
     per_row = LANES * 8 // rows
     columns = 2 * tt_ref.shape[1]
-    position = source_slot(sel_ref, meta_ref) & (GROUP - 1)
+    position = source_slot(info_ref) & (GROUP - 1)
     first = seen_ref.shape[1] - 32
     sent = seen_ref[position][first:, :].astype(jnp.float32)
     mismatch = sent[0:8] + sent[8:16] + sent[16:24]
     weight = sent[24:25] + sent[25:26] + sent[26:27] - target_ref[0]
-    slot = meta_ref[0]
+    slot = info_ref[0]
     for section, stay_ref in enumerate((first_ref, second_ref)):
-        stay = jnp.where(sel_ref[section, slot] < 1, 1.0, 0.0)
+        stay = jnp.where(chosen(info_ref, section, slot) < 1, 1.0, 0.0)
         stay_ref[...] = jnp.full(stay_ref.shape, stay, jnp.float32)
     miss_ref[rows:, :] = jnp.broadcast_to(weight, (8, LANES))
     tiles = [mismatch] + [
@@ -243,7 +248,7 @@
 
 
 def spectral_kernel(
-    meta_ref, sel_ref, modes_ref, noise_ref, spec_ref, part_ref, tt_ref, ht_ref, send_ref, pack_scr,
+    info_ref, modes_ref, noise_ref, spec_ref, part_ref, tt_ref, ht_ref, send_ref, pack_scr,
     unpack_scr,
 ):
     half = LANES // 2
@@ -252,7 +257,7 @@
     unpack_scr[...] = modes_ref[...].astype(jnp.float32)
     rows = 2 * tt_ref.shape[1]
     norm_factor = 4.0 / (rows * rows)
-    position = source_slot(sel_ref, meta_ref) & (GROUP - 1)
+    position = source_slot(info_ref) & (GROUP - 1)
     lane = lane_iota()
     low = lane < half
     tops, bottoms = [], []
@@ -491,7 +496,8 @@
     shape = jax.ShapeDtypeStruct
     groups = [[g * GROUP + i for i in range(GROUP)] for g in range(particles // GROUP)]
     slot = lax.axis_index("particle")
-    meta = jnp.stack([slot, lax.axis_index("space")]).astype(jnp.int32)
+    place = jnp.stack([slot, lax.axis_index("space")]).astype(jnp.int32)
+    info = jnp.concatenate([place, selection.reshape(-1)])
     own = stream[0]
     col_t, val_t, wgt_t = obs_col.T, obs_val.T, obs_weight.T
     vmem = pltpu.VMEM
@@ -522,7 +528,7 @@
 
     send, miss, part, stay_first, stay_second = call(
         gradient_kernel,
-        [SMEM, SMEM, SMEM] + [VMEM] * 6,
+        [SMEM, SMEM] + [VMEM] * 6,
         (
             shape((bands * 10, LANES), bf16),
             shape((rows + 8, LANES), f32),
@@ -532,7 +538,7 @@
         ),
         [whole, vmem((bands * 10, LANES), f32)],
         "gradient",
-    )(meta, selection, target, col_tile, wgt_tile, sent, tt, first, last)
+    )(info, target, col_tile, wgt_tile, sent, tt, first, last)
     send = send.reshape(bands, 5, 2, LANES)
     col_modes = lax.all_to_all(send, "space", 0, 0, tiled=True).reshape(bands * 10, LANES)
 
@@ -542,11 +548,11 @@
 
     send = call(
         spectral_kernel,
-        [SMEM, SMEM, VMEM, VMEM, VMEM, VMEM, VMEM, VMEM],
+        [SMEM] + [VMEM] * 6,
         shape((bands * (modes_here + 4), LANES), bf16),
         [vmem((bands * (modes_here + 4), LANES), f32), vmem((bands * 10, LANES), f32)],
         "spectral",
-    )(meta, selection, col_modes, sent, spectrum, part, tt, ht_all)
+    )(info, col_modes, sent, spectrum, part, tt, ht_all)
     send = send.reshape(bands, modes_here // 2 + 2, 2, LANES)
     band_modes = lax.all_to_all(send, "space", 0, 0, tiled=True)
     band_modes = band_modes.reshape(bands * (modes_here + 4), LANES)

time: 75.6 us -> 74.9 us (level)
  transfers between devices with their start and end apart: 6 -> 6, of which waited for: 4 -> 4; matrix products, arithmetic and copies ran while one was open for 1% -> 2% of each run, Pallas kernels for 10% -> 10%
where the time goes in v9:
time: 74.9 us; the launch traced here: 74.4 us
  starting transfers between devices  33.4 us (45%)
  waiting for transfers between devices  27.5 us (37%)
  Pallas kernels  9.52 us (13%)
  between operations  2.06 us (3%)
  other arithmetic  1.74 us (2%)
    all_to_all x1, starting transfers between devices, per_device(): lax.all_to_all(send, 'space', 0, 0, tiled=True).reshape(bands * 10, LANES)  11.7 us
    all_to_all x1, waiting for transfers between devices, per_device(): band_modes = lax.all_to_all(send, 'space', 0, 0, tiled=True)  11.5 us
    all_to_all x1, waiting for transfers between devices, per_device(): parts = lax.all_to_all(part, 'space', 0, 0, tiled=True)  8.58 us
    all_to_all x1, starting transfers between devices, per_device(): lax.all_to_all(sent, 'particle', 0, 0, axis_index_groups=groups, tiled=True)  7.82 us
    all_to_all x1, waiting for transfers between devices, per_device(): lax.all_to_all(send, 'space', 0, 0, tiled=True).reshape(bands * 10, LANES)  6.88 us
    ppermute x2, starting transfers between devices, swapped(): return lax.ppermute(value, axis, pairs)  6.27 us
    all_to_all x1, starting transfers between devices, per_device(): band_modes = lax.all_to_all(send, 'space', 0, 0, tiled=True)  3.86 us
    all_to_all x1, starting transfers between devices, per_device(): parts = lax.all_to_all(part, 'space', 0, 0, tiled=True)  3.74 us
  transfers between devices with their start and end apart: 6, of which 4 were waited for; matrix products, arithmetic and copies ran while one was open for 2% of the time, Pallas kernels for 10%

profile of v9, /device:TPU:1, one launch (start us, length us, event | category | flops | bytes accessed | tf_op | source)
XLA Modules:
  0.0 74.4 jit_solution(2163017063611663274)
XLA Ops:
  1.3 0.0 copy-start.2
  1.3 2.3 %observe.1 = (bf16[4,96,128]{2,1,0:T(8,128)(2,1)}, s32[64,128]{1,0:T(8,128)S(1)}, f32[64,128]{1,0:T(8,128)S(1)}, bf16[512,1024]{1,0:T(8,128)(2,1)S(1)}, f32[1,2048]{1,0:T(1,128)S(1)}, /*index=5*/f32[1,2048]{1,0:T(1,128)S(1)}) custom-call(f32[1]{0:T(128)S(6)} %copy.14.lw_ref, s32[16,64]{1,0:T(8,128)} %bitcast.20, f32[16,64]{1,0:T(8,128)} %bitcast.21, ...), custom_call_target="tpu_custom_call" | custom-call | flops 40000000000 | bytes 4000000 | tf_op jit(solution)/shard_map/observe/pallas_call | solution.py:510
  3.6 7.8 %all-to-all-start = ((bf16[4,96,128]{2,1,0:T(8,128)(2,1)}), bf16[4,96,128]{2,1,0:T(8,128)(2,1)S(1)}, u32[]{:S(2)}, u32[]{:S(2)}) async-start(bf16[4,96,128]{2,1,0:T(8,128)(2,1)} %get-tuple-element.24), calls=%async_computation | async-start | bytes 196608 | tf_op jit(solution)/shard_map/all_to_all | solution.py:526
  11.4 0.0 copy-done.2
  11.4 3.4 %collective-permute-start = (f32[64,2048]{1,0:T(8,128)S(1)}, f32[64,2048]{1,0:T(8,128)S(1)}, u32[]{:S(2)}, u32[]{:S(2)}) collective-permute-start(f32[64,2048]{1,0:T(8,128)S(1)} %bitcast.18), channel_id=1, source_target_pairs={{0,32},{32,0},{64,96},{96,64},{128,160},{160,128},{192,224},{224,1... | collective-permute-start | bytes 1572872 | tf_op jit(solution)/shard_map/ppermute | solution.py:480
  14.8 0.0 copy-start.3
  15.5 0.0 copy-done.3
  15.5 0.1 reshape.20
  15.5 0.1 pad_add_fusion.info_ref
  15.6 0.6 all-to-all-done.seen_ref.noise_ref
  16.2 2.5 %gradient.1 = (bf16[320,128]{1,0:T(8,128)(2,1)}, f32[72,128]{1,0:T(8,128)S(1)}, f32[8,128]{1,0:T(8,128)S(1)}, f32[1,2048]{1,0:T(1,128)S(1)}, f32[1,2048]{1,0:T(1,128)S(1)}) custom-call(s32[34]{0:T(128)S(1)} %pad_add_fusion.info_ref, f32[1]{0:T(128)S(6)} %copy.15.target_ref, s32[64,128]{1,0:T(8,128)S(1)} %get-tuple-element.21.col_scr, ...), custom_call_target="tpu_custom_call" | custom-call | flops 40000000000 | bytes 4000000 | tf_op jit(solution)/shard_map/gradient/pallas_call | solution.py:529
  18.7 11.7 %all-to-all-start.1 = ((bf16[32,5,2,128]{3,2,1,0:T(2,128)(2,1)}), bf16[32,5,2,128]{3,2,1,0:T(2,128)(2,1)S(1)}, u32[]{:S(2)}, u32[]{:S(2)}) async-start(bf16[32,5,2,128]{3,2,1,0:T(2,128)(2,1)} %bitcast.7), calls=%async_computation.1 | async-start | bytes 163840 | tf_op jit(solution)/shard_map/all_to_all | solution.py:543
  30.5 0.0 copy-start
  30.5 0.0 copy-start.1
  30.5 0.0 collective-permute-done
  30.5 0.1 broadcast_select_fusion
  30.6 2.9 %collective-permute-start.1 = (f32[64,2048]{1,0:T(8,128)S(1)}, f32[64,2048]{1,0:T(8,128)S(1)}, u32[]{:S(2)}, u32[]{:S(2)}) collective-permute-start(f32[64,2048]{1,0:T(8,128)S(1)} %broadcast_select_fusion), channel_id=1, source_target_pairs={{0,64},{32,96},{64,0},{96,32},{128,192},{160,224},{192,128},{224,1... | collective-permute-start | bytes 1572872 | tf_op jit(solution)/shard_map/ppermute | solution.py:480
  33.5 6.9 %all-to-all-done.1 = bf16[32,5,2,128]{3,2,1,0:T(2,128)(2,1)S(1)} async-done(((bf16[32,5,2,128]{3,2,1,0:T(2,128)(2,1)}), bf16[32,5,2,128]{3,2,1,0:T(2,128)(2,1)S(1)}, u32[]{:S(2)}, u32[]{:S(2)}) %all-to-all-start.1) | async-done | bytes 81952 | tf_op jit(solution)/shard_map/all_to_all | solution.py:543
  40.4 0.0 copy-done
  40.4 0.0 copy-done.1
  40.4 2.1 %spectral.1 = bf16[640,128]{1,0:T(8,128)(2,1)} custom-call(s32[34]{0:T(128)S(1)} %pad_add_fusion.info_ref, bf16[320,128]{1,0:T(8,128)(2,1)S(1)} %bitcast.15, bf16[4,96,128]{2,1,0:T(8,128)(2,1)S(1)} %all-to-all-done.seen_ref.noise_ref, f32[16,512]{1,0:T(8,128)S(1)} %copy-done, f32[8,128]{1,0:T(8,128)S(1)} %get-tuple-element.33.part_ref, ...), custom_call_target="tpu_custom_call" | custom-call | flops 1000000000 | bytes 4000000 | tf_op jit(solution)/shard_map/spectral/pallas_call | solution.py:549
  42.5 3.9 %all-to-all-start.2 = ((bf16[32,10,2,128]{3,2,1,0:T(2,128)(2,1)}), bf16[32,10,2,128]{3,2,1,0:T(2,128)(2,1)S(1)}, u32[]{:S(2)}, u32[]{:S(2)}) async-start(bf16[32,10,2,128]{3,2,1,0:T(2,128)(2,1)} %bitcast.9), calls=%async_computation.2 | async-start | bytes 327680 | tf_op jit(solution)/shard_map/all_to_all | solution.py:557
  46.4 11.5 %all-to-all-done.2 = bf16[32,10,2,128]{3,2,1,0:T(2,128)(2,1)S(1)} async-done(((bf16[32,10,2,128]{3,2,1,0:T(2,128)(2,1)}), bf16[32,10,2,128]{3,2,1,0:T(2,128)(2,1)S(1)}, u32[]{:S(2)}, u32[]{:S(2)}) %all-to-all-start.2) | async-done | bytes 163872 | tf_op jit(solution)/shard_map/all_to_all | solution.py:557
  57.9 2.7 %relax.1 = (f32[64,2048]{1,0:T(8,128)S(1)}, f32[32,1,128]{2,1,0:T(1,128)}) custom-call(s32[64,128]{1,0:T(8,128)S(1)} %get-tuple-element.21.col_scr, f32[64,128]{1,0:T(8,128)S(1)} %get-tuple-element.22.wgt_scr, f32[72,128]{1,0:T(8,128)S(1)} %get-tuple-element.28.miss_ref, f32[64,2048]{1,0:T(8,128)} %depth_hbm.3, bf16[640,128]{1,0:T(8,128)(2,1)S(1)} %bitcast.14, ...), custom_call_target="tpu_custom_call" | custom-call | flops 1000000000 | bytes 4000000 | tf_op jit(solution)/shard_map/relax/pallas_call | solution.py:560
  60.5 3.7 %all-to-all-start.3 = ((f32[32,1,128]{2,1,0:T(1,128)}), f32[32,1,128]{2,1,0:T(1,128)S(1)}, u32[]{:S(2)}, u32[]{:S(2)}) async-start(f32[32,1,128]{2,1,0:T(1,128)} %get-tuple-element.34), calls=%async_computation.3 | async-start | bytes 32768 | tf_op jit(solution)/shard_map/all_to_all | solution.py:567
  64.3 0.0 collective-permute-done.1
  64.3 0.9 %select_add_fusion = f32[64,2048]{1,0:T(8,128)} fusion(f32[64,2048]{1,0:T(8,128)S(1)} %get-tuple-element.35, f32[64,2048]{1,0:T(8,128)S(1)} %broadcast_select_fusion, f32[64,2048]{1,0:T(8,128)S(1)} %collective-permute-done.1, pred[2048]{0:T(1024)(128)(4,1)S(1)} %compare_reduce_fusion), kind=kLoop, calls=%fused_computation | loop fusion | flops 262144 | bytes 2099200 | tf_op jit(solution)/shard_map/add | solution.py:568
  65.2 8.6 %all-to-all-done.3 = f32[32,1,128]{2,1,0:T(1,128)S(1)} async-done(((f32[32,1,128]{2,1,0:T(1,128)}), f32[32,1,128]{2,1,0:T(1,128)S(1)}, u32[]{:S(2)}, u32[]{:S(2)}) %all-to-all-start.3) | async-done | bytes 16416 | tf_op jit(solution)/shard_map/all_to_all | solution.py:567
  73.8 0.6 slice_reduce_fusion
  (2 shorter events, 0.1 us)
Async XLA Ops:
  1.3 10.1 %copy-start.2 = (f32[1,64,2048]{2,1,0:T(8,128)S(1)}, f32[1,64,2048]{2,1,0:T(8,128)}, u32[]{:S(2)}) copy-start(f32[1,64,2048]{2,1,0:T(8,128)} %param.12) | copy-start | bytes 1572868
  3.6 12.6 %all-to-all-start = ((bf16[4,96,128]{2,1,0:T(8,128)(2,1)}), bf16[4,96,128]{2,1,0:T(8,128)(2,1)S(1)}, u32[]{:S(2)}, u32[]{:S(2)}) async-start(bf16[4,96,128]{2,1,0:T(8,128)(2,1)} %get-tuple-element.24), calls=%async_computation | async-start | bytes 196608 | tf_op jit(solution)/shard_map/all_to_all | solution.py:526
  11.4 19.1 %collective-permute-start = (f32[64,2048]{1,0:T(8,128)S(1)}, f32[64,2048]{1,0:T(8,128)S(1)}, u32[]{:S(2)}, u32[]{:S(2)}) collective-permute-start(f32[64,2048]{1,0:T(8,128)S(1)} %bitcast.18), channel_id=1, source_target_pairs={{0,32},{32,0},{64,96},{96,64},{128,160},{160,128},{192,224},{224,1... | collective-permute-start | bytes 1572872 | tf_op jit(solution)/shard_map/ppermute | solution.py:480
  14.8 0.7 copy-start.3
  18.7 21.7 %all-to-all-start.1 = ((bf16[32,5,2,128]{3,2,1,0:T(2,128)(2,1)}), bf16[32,5,2,128]{3,2,1,0:T(2,128)(2,1)S(1)}, u32[]{:S(2)}, u32[]{:S(2)}) async-start(bf16[32,5,2,128]{3,2,1,0:T(2,128)(2,1)} %bitcast.7), calls=%async_computation.1 | async-start | bytes 163840 | tf_op jit(solution)/shard_map/all_to_all | solution.py:543
  30.5 9.9 %copy-start = (f32[16,512]{1,0:T(8,128)S(1)}, f32[16,512]{1,0:T(8,128)}, u32[]{:S(2)}) copy-start(f32[16,512]{1,0:T(8,128)} %spec_ref.1) | copy-start | bytes 98308
  30.5 9.9 %copy-start.1 = (bf16[128,512]{1,0:T(8,128)(2,1)S(1)}, bf16[128,512]{1,0:T(8,128)(2,1)}, u32[]{:S(2)}) copy-start(bf16[128,512]{1,0:T(8,128)(2,1)} %constant.17.clone.ht_ref) | copy-start | bytes 393220
  30.6 33.7 %collective-permute-start.1 = (f32[64,2048]{1,0:T(8,128)S(1)}, f32[64,2048]{1,0:T(8,128)S(1)}, u32[]{:S(2)}, u32[]{:S(2)}) collective-permute-start(f32[64,2048]{1,0:T(8,128)S(1)} %broadcast_select_fusion), channel_id=1, source_target_pairs={{0,64},{32,96},{64,0},{96,32},{128,192},{160,224},{192,128},{224,1... | collective-permute-start | bytes 1572872 | tf_op jit(solution)/shard_map/ppermute | solution.py:480
  42.5 15.4 %all-to-all-start.2 = ((bf16[32,10,2,128]{3,2,1,0:T(2,128)(2,1)}), bf16[32,10,2,128]{3,2,1,0:T(2,128)(2,1)S(1)}, u32[]{:S(2)}, u32[]{:S(2)}) async-start(bf16[32,10,2,128]{3,2,1,0:T(2,128)(2,1)} %bitcast.9), calls=%async_computation.2 | async-start | bytes 327680 | tf_op jit(solution)/shard_map/all_to_all | solution.py:557
  60.5 13.2 %all-to-all-start.3 = ((f32[32,1,128]{2,1,0:T(1,128)}), f32[32,1,128]{2,1,0:T(1,128)S(1)}, u32[]{:S(2)}, u32[]{:S(2)}) async-start(f32[32,1,128]{2,1,0:T(1,128)} %get-tuple-element.34), calls=%async_computation.3 | async-start | bytes 32768 | tf_op jit(solution)/shard_map/all_to_all | solution.py:567

commit v10 on v9

--- a/solution.py
+++ b/solution.py
@@ -111,11 +111,11 @@
     pairs = (
         (col_hbm, col_ref),
         (val_hbm, val_ref),
-        (stream_hbm, stream_ref),
+        (wgt_hbm, wgt_ref),
         (noise_hbm, noise_ref),
-        (wgt_hbm, wgt_ref),
         (depth_hbm.at[0:8, :], depth_ref.at[0:8, :]),
         (depth_hbm.at[rows - 8 : rows, :], depth_ref.at[8:16, :]),
+        (stream_hbm, stream_ref),
         (tt_hbm, tt_ref),
     )
     loads = [pltpu.make_async_copy(a, b, sems.at[at]) for at, (a, b) in enumerate(pairs)]
@@ -123,20 +123,9 @@
         load.start()
     per_row = col_ref.shape[0]
     modes_here, n_modes = noise_ref.shape
-    loads[0].wait()
-    loads[1].wait()
-    fill_tile(col_ref, col_scr)
-    fill_tile(val_ref, val_scr)
-    loads[2].wait()
-    gather_rows(stream_ref, col_scr, seen_scr)
-    mismatch = packed(val_scr[...] - seen_scr[...], per_row)
-    weight = jnp.full((8, LANES), lw_ref[0], jnp.float32)
-    row = lax.broadcasted_iota(jnp.int32, (8, LANES), 0)
-    high, mid, low = split3(weight)
-    weight = jnp.where(row == 0, high, jnp.where(row == 1, mid, jnp.where(row == 2, low, 0.0)))
-    values = jnp.concatenate(list(split3(mismatch)) + [weight], axis=0).astype(jnp.bfloat16)
-    loads[4].wait()
-    fill_tile(wgt_ref, wgt_scr)
+    for at, (source, tile) in enumerate(((col_ref, col_scr), (val_ref, val_scr), (wgt_ref, wgt_scr))):
+        loads[at].wait()
+        fill_tile(source, tile)
     loads[3].wait()
     noise = noise_ref[...]
     chunks = n_modes // LANES
@@ -145,11 +134,20 @@
             out_ref[peer, chunk * modes_here : (chunk + 1) * modes_here, :] = noise[
                 :, chunk * LANES : (chunk + 1) * LANES
             ]
-        out_ref[peer, chunks * modes_here :, :] = values
+    loads[4].wait()
     loads[5].wait()
-    loads[6].wait()
     first_ref[...] = depth_ref[0:1, :]
     last_ref[...] = depth_ref[15:16, :]
+    weight = jnp.full((8, LANES), lw_ref[0], jnp.float32)
+    row = lax.broadcasted_iota(jnp.int32, (8, LANES), 0)
+    high, mid, low = split3(weight)
+    weight = jnp.where(row == 0, high, jnp.where(row == 1, mid, jnp.where(row == 2, low, 0.0)))
+    loads[6].wait()
+    gather_rows(stream_ref, col_scr, seen_scr)
+    mismatch = packed(val_scr[...] - seen_scr[...], per_row)
+    values = jnp.concatenate(list(split3(mismatch)) + [weight], axis=0).astype(jnp.bfloat16)
+    for peer in range(GROUP):
+        out_ref[peer, chunks * modes_here :, :] = values
     loads[7].wait()
 
 

time: 74.9 us -> 74.9 us (level)
  no operation moved by 1% of the time
where the time goes in v10:
time: 74.9 us; the launch traced here: 74.4 us
  starting transfers between devices  33.4 us (45%)
  waiting for transfers between devices  27.5 us (37%)
  Pallas kernels  9.51 us (13%)
  between operations  2.06 us (3%)
  other arithmetic  1.74 us (2%)
    all_to_all x1, starting transfers between devices, per_device(): lax.all_to_all(send, 'space', 0, 0, tiled=True).reshape(bands * 10, LANES)  11.7 us
    all_to_all x1, waiting for transfers between devices, per_device(): band_modes = lax.all_to_all(send, 'space', 0, 0, tiled=True)  11.5 us
    all_to_all x1, waiting for transfers between devices, per_device(): parts = lax.all_to_all(part, 'space', 0, 0, tiled=True)  8.58 us
    all_to_all x1, starting transfers between devices, per_device(): lax.all_to_all(sent, 'particle', 0, 0, axis_index_groups=groups, tiled=True)  7.82 us
    all_to_all x1, waiting for transfers between devices, per_device(): lax.all_to_all(send, 'space', 0, 0, tiled=True).reshape(bands * 10, LANES)  6.88 us
    ppermute x2, starting transfers between devices, swapped(): return lax.ppermute(value, axis, pairs)  6.27 us
    all_to_all x1, starting transfers between devices, per_device(): band_modes = lax.all_to_all(send, 'space', 0, 0, tiled=True)  3.86 us
    all_to_all x1, starting transfers between devices, per_device(): parts = lax.all_to_all(part, 'space', 0, 0, tiled=True)  3.74 us
  transfers between devices with their start and end apart: 6, of which 4 were waited for; matrix products, arithmetic and copies ran while one was open for 2% of the time, Pallas kernels for 10%

profile of v10, /device:TPU:1, one launch (start us, length us, event | category | flops | bytes accessed | tf_op | source)
XLA Modules:
  0.0 74.4 jit_solution(1937326972515320834)
XLA Ops:
  1.3 0.0 copy-start.2
  1.3 2.3 %observe.1 = (bf16[4,96,128]{2,1,0:T(8,128)(2,1)}, s32[64,128]{1,0:T(8,128)S(1)}, f32[64,128]{1,0:T(8,128)S(1)}, bf16[512,1024]{1,0:T(8,128)(2,1)S(1)}, f32[1,2048]{1,0:T(1,128)S(1)}, /*index=5*/f32[1,2048]{1,0:T(1,128)S(1)}) custom-call(f32[1]{0:T(128)S(6)} %copy.14.lw_ref, s32[16,64]{1,0:T(8,128)} %bitcast.20, f32[16,64]{1,0:T(8,128)} %bitcast.21, ...), custom_call_target="tpu_custom_call" | custom-call | flops 40000000000 | bytes 4000000 | tf_op jit(solution)/shard_map/observe/pallas_call | solution.py:508
  3.6 7.8 %all-to-all-start = ((bf16[4,96,128]{2,1,0:T(8,128)(2,1)}), bf16[4,96,128]{2,1,0:T(8,128)(2,1)S(1)}, u32[]{:S(2)}, u32[]{:S(2)}) async-start(bf16[4,96,128]{2,1,0:T(8,128)(2,1)} %get-tuple-element.24), calls=%async_computation | async-start | bytes 196608 | tf_op jit(solution)/shard_map/all_to_all | solution.py:524
  11.4 0.0 copy-done.2
  11.4 3.4 %collective-permute-start = (f32[64,2048]{1,0:T(8,128)S(1)}, f32[64,2048]{1,0:T(8,128)S(1)}, u32[]{:S(2)}, u32[]{:S(2)}) collective-permute-start(f32[64,2048]{1,0:T(8,128)S(1)} %bitcast.18), channel_id=1, source_target_pairs={{0,32},{32,0},{64,96},{96,64},{128,160},{160,128},{192,224},{224,1... | collective-permute-start | bytes 1572872 | tf_op jit(solution)/shard_map/ppermute | solution.py:478
  14.8 0.0 copy-start.3
  15.4 0.0 copy-done.3
  15.5 0.1 reshape.20
  15.5 0.1 pad_add_fusion.info_ref
  15.6 0.6 all-to-all-done.seen_ref.noise_ref
  16.2 2.5 %gradient.1 = (bf16[320,128]{1,0:T(8,128)(2,1)}, f32[72,128]{1,0:T(8,128)S(1)}, f32[8,128]{1,0:T(8,128)S(1)}, f32[1,2048]{1,0:T(1,128)S(1)}, f32[1,2048]{1,0:T(1,128)S(1)}) custom-call(s32[34]{0:T(128)S(1)} %pad_add_fusion.info_ref, f32[1]{0:T(128)S(6)} %copy.15.target_ref, s32[64,128]{1,0:T(8,128)S(1)} %get-tuple-element.21.col_scr, ...), custom_call_target="tpu_custom_call" | custom-call | flops 40000000000 | bytes 4000000 | tf_op jit(solution)/shard_map/gradient/pallas_call | solution.py:527
  18.7 11.7 %all-to-all-start.1 = ((bf16[32,5,2,128]{3,2,1,0:T(2,128)(2,1)}), bf16[32,5,2,128]{3,2,1,0:T(2,128)(2,1)S(1)}, u32[]{:S(2)}, u32[]{:S(2)}) async-start(bf16[32,5,2,128]{3,2,1,0:T(2,128)(2,1)} %bitcast.7), calls=%async_computation.1 | async-start | bytes 163840 | tf_op jit(solution)/shard_map/all_to_all | solution.py:541
  30.5 0.0 copy-start
  30.5 0.0 copy-start.1
  30.5 0.0 collective-permute-done
  30.5 0.1 broadcast_select_fusion
  30.6 2.9 %collective-permute-start.1 = (f32[64,2048]{1,0:T(8,128)S(1)}, f32[64,2048]{1,0:T(8,128)S(1)}, u32[]{:S(2)}, u32[]{:S(2)}) collective-permute-start(f32[64,2048]{1,0:T(8,128)S(1)} %broadcast_select_fusion), channel_id=1, source_target_pairs={{0,64},{32,96},{64,0},{96,32},{128,192},{160,224},{192,128},{224,1... | collective-permute-start | bytes 1572872 | tf_op jit(solution)/shard_map/ppermute | solution.py:478
  33.5 6.9 %all-to-all-done.1 = bf16[32,5,2,128]{3,2,1,0:T(2,128)(2,1)S(1)} async-done(((bf16[32,5,2,128]{3,2,1,0:T(2,128)(2,1)}), bf16[32,5,2,128]{3,2,1,0:T(2,128)(2,1)S(1)}, u32[]{:S(2)}, u32[]{:S(2)}) %all-to-all-start.1) | async-done | bytes 81952 | tf_op jit(solution)/shard_map/all_to_all | solution.py:541
  40.4 0.0 copy-done
  40.4 0.0 copy-done.1
  40.4 2.1 %spectral.1 = bf16[640,128]{1,0:T(8,128)(2,1)} custom-call(s32[34]{0:T(128)S(1)} %pad_add_fusion.info_ref, bf16[320,128]{1,0:T(8,128)(2,1)S(1)} %bitcast.15, bf16[4,96,128]{2,1,0:T(8,128)(2,1)S(1)} %all-to-all-done.seen_ref.noise_ref, f32[16,512]{1,0:T(8,128)S(1)} %copy-done, f32[8,128]{1,0:T(8,128)S(1)} %get-tuple-element.33.part_ref, ...), custom_call_target="tpu_custom_call" | custom-call | flops 1000000000 | bytes 4000000 | tf_op jit(solution)/shard_map/spectral/pallas_call | solution.py:547
  42.4 3.9 %all-to-all-start.2 = ((bf16[32,10,2,128]{3,2,1,0:T(2,128)(2,1)}), bf16[32,10,2,128]{3,2,1,0:T(2,128)(2,1)S(1)}, u32[]{:S(2)}, u32[]{:S(2)}) async-start(bf16[32,10,2,128]{3,2,1,0:T(2,128)(2,1)} %bitcast.9), calls=%async_computation.2 | async-start | bytes 327680 | tf_op jit(solution)/shard_map/all_to_all | solution.py:555
  46.4 11.5 %all-to-all-done.2 = bf16[32,10,2,128]{3,2,1,0:T(2,128)(2,1)S(1)} async-done(((bf16[32,10,2,128]{3,2,1,0:T(2,128)(2,1)}), bf16[32,10,2,128]{3,2,1,0:T(2,128)(2,1)S(1)}, u32[]{:S(2)}, u32[]{:S(2)}) %all-to-all-start.2) | async-done | bytes 163872 | tf_op jit(solution)/shard_map/all_to_all | solution.py:555
  57.9 2.7 %relax.1 = (f32[64,2048]{1,0:T(8,128)S(1)}, f32[32,1,128]{2,1,0:T(1,128)}) custom-call(s32[64,128]{1,0:T(8,128)S(1)} %get-tuple-element.21.col_scr, f32[64,128]{1,0:T(8,128)S(1)} %get-tuple-element.22.wgt_scr, f32[72,128]{1,0:T(8,128)S(1)} %get-tuple-element.28.miss_ref, f32[64,2048]{1,0:T(8,128)} %depth_hbm.3, bf16[640,128]{1,0:T(8,128)(2,1)S(1)} %bitcast.14, ...), custom_call_target="tpu_custom_call" | custom-call | flops 1000000000 | bytes 4000000 | tf_op jit(solution)/shard_map/relax/pallas_call | solution.py:558
  60.5 3.7 %all-to-all-start.3 = ((f32[32,1,128]{2,1,0:T(1,128)}), f32[32,1,128]{2,1,0:T(1,128)S(1)}, u32[]{:S(2)}, u32[]{:S(2)}) async-start(f32[32,1,128]{2,1,0:T(1,128)} %get-tuple-element.34), calls=%async_computation.3 | async-start | bytes 32768 | tf_op jit(solution)/shard_map/all_to_all | solution.py:565
  64.3 0.0 collective-permute-done.1
  64.3 0.9 %select_add_fusion = f32[64,2048]{1,0:T(8,128)} fusion(f32[64,2048]{1,0:T(8,128)S(1)} %get-tuple-element.35, f32[64,2048]{1,0:T(8,128)S(1)} %broadcast_select_fusion, f32[64,2048]{1,0:T(8,128)S(1)} %collective-permute-done.1, pred[2048]{0:T(1024)(128)(4,1)S(1)} %compare_reduce_fusion), kind=kLoop, calls=%fused_computation | loop fusion | flops 262144 | bytes 2099200 | tf_op jit(solution)/shard_map/add | solution.py:566
  65.2 8.6 %all-to-all-done.3 = f32[32,1,128]{2,1,0:T(1,128)S(1)} async-done(((f32[32,1,128]{2,1,0:T(1,128)}), f32[32,1,128]{2,1,0:T(1,128)S(1)}, u32[]{:S(2)}, u32[]{:S(2)}) %all-to-all-start.3) | async-done | bytes 16416 | tf_op jit(solution)/shard_map/all_to_all | solution.py:565
  73.8 0.6 slice_reduce_fusion
  (2 shorter events, 0.1 us)
Async XLA Ops:
  1.3 10.1 %copy-start.2 = (f32[1,64,2048]{2,1,0:T(8,128)S(1)}, f32[1,64,2048]{2,1,0:T(8,128)}, u32[]{:S(2)}) copy-start(f32[1,64,2048]{2,1,0:T(8,128)} %param.12) | copy-start | bytes 1572868
  3.6 12.6 %all-to-all-start = ((bf16[4,96,128]{2,1,0:T(8,128)(2,1)}), bf16[4,96,128]{2,1,0:T(8,128)(2,1)S(1)}, u32[]{:S(2)}, u32[]{:S(2)}) async-start(bf16[4,96,128]{2,1,0:T(8,128)(2,1)} %get-tuple-element.24), calls=%async_computation | async-start | bytes 196608 | tf_op jit(solution)/shard_map/all_to_all | solution.py:524
  11.4 19.1 %collective-permute-start = (f32[64,2048]{1,0:T(8,128)S(1)}, f32[64,2048]{1,0:T(8,128)S(1)}, u32[]{:S(2)}, u32[]{:S(2)}) collective-permute-start(f32[64,2048]{1,0:T(8,128)S(1)} %bitcast.18), channel_id=1, source_target_pairs={{0,32},{32,0},{64,96},{96,64},{128,160},{160,128},{192,224},{224,1... | collective-permute-start | bytes 1572872 | tf_op jit(solution)/shard_map/ppermute | solution.py:478
  14.8 0.7 copy-start.3
  18.7 21.7 %all-to-all-start.1 = ((bf16[32,5,2,128]{3,2,1,0:T(2,128)(2,1)}), bf16[32,5,2,128]{3,2,1,0:T(2,128)(2,1)S(1)}, u32[]{:S(2)}, u32[]{:S(2)}) async-start(bf16[32,5,2,128]{3,2,1,0:T(2,128)(2,1)} %bitcast.7), calls=%async_computation.1 | async-start | bytes 163840 | tf_op jit(solution)/shard_map/all_to_all | solution.py:541
  30.5 9.9 %copy-start = (f32[16,512]{1,0:T(8,128)S(1)}, f32[16,512]{1,0:T(8,128)}, u32[]{:S(2)}) copy-start(f32[16,512]{1,0:T(8,128)} %spec_ref.1) | copy-start | bytes 98308
  30.5 9.9 %copy-start.1 = (bf16[128,512]{1,0:T(8,128)(2,1)S(1)}, bf16[128,512]{1,0:T(8,128)(2,1)}, u32[]{:S(2)}) copy-start(bf16[128,512]{1,0:T(8,128)(2,1)} %constant.17.clone.ht_ref) | copy-start | bytes 393220
  30.6 33.7 %collective-permute-start.1 = (f32[64,2048]{1,0:T(8,128)S(1)}, f32[64,2048]{1,0:T(8,128)S(1)}, u32[]{:S(2)}, u32[]{:S(2)}) collective-permute-start(f32[64,2048]{1,0:T(8,128)S(1)} %broadcast_select_fusion), channel_id=1, source_target_pairs={{0,64},{32,96},{64,0},{96,32},{128,192},{160,224},{192,128},{224,1... | collective-permute-start | bytes 1572872 | tf_op jit(solution)/shard_map/ppermute | solution.py:478
  42.4 15.4 %all-to-all-start.2 = ((bf16[32,10,2,128]{3,2,1,0:T(2,128)(2,1)}), bf16[32,10,2,128]{3,2,1,0:T(2,128)(2,1)S(1)}, u32[]{:S(2)}, u32[]{:S(2)}) async-start(bf16[32,10,2,128]{3,2,1,0:T(2,128)(2,1)} %bitcast.9), calls=%async_computation.2 | async-start | bytes 327680 | tf_op jit(solution)/shard_map/all_to_all | solution.py:555
  60.5 13.2 %all-to-all-start.3 = ((f32[32,1,128]{2,1,0:T(1,128)}), f32[32,1,128]{2,1,0:T(1,128)S(1)}, u32[]{:S(2)}, u32[]{:S(2)}) async-start(f32[32,1,128]{2,1,0:T(1,128)} %get-tuple-element.34), calls=%async_computation.3 | async-start | bytes 32768 | tf_op jit(solution)/shard_map/all_to_all | solution.py:565
